TPU v7x, 32 devices: a whole 2x2x4 slice. The times are simulated.
32 devices in a mesh: runs: 2 (over y), mem: 4 (over x, core), lat: 4 (over z).
Axes of the slice: x: 2, y: 2, z: 4, core: 2. Of those that a mesh axis runs over, the one named last changes fastest.
Arguments:
- states: bfloat16 [8, 12, 160, 768], P(('runs', 'mem'), 'lat'), parts along dimension 0, may hold values from -6 to 6
- land_mask: int32 [12, 768], P('lat'), may hold values 0 or 1
- cutoff: int32 [12], replicated, may hold values from 48 to 383
- kernel: float32 [7, 7, 160], replicated, may hold values from -0.875 to 0.875
- norm_gain: float32 [160], replicated, may hold values from 0.5 to 2
- norm_bias: float32 [160], replicated, may hold values from -3 to 3
- weight_in: bfloat16 [160, 640], replicated, may hold values from -0.5 to 0.5
- bias_in: float32 [640], replicated, may hold values from -4 to 4
- weight_out: bfloat16 [640, 160], replicated, may hold values from -0.25 to 0.25
Outputs:
- advanced: bfloat16 [8, 12, 160, 768], P(('runs', 'mem'), 'lat'), parts along dimension 0
There are 2 independent parts, one for each index of `runs`. A program takes and returns all parts, laid end to end along the dimension named above; an argument that names none is the same for every part. Nothing has to cross between parts.
All inputs are finite; a program needn't handle non-finite values. No bound on the sum of `land_mask` on one device may be relied on, other than what follows from the above.
Results may differ from a plain program's by a relative error of at most 0.012.
Values may be sent and summed in bfloat16 or wider, within the bound.
No kernel may reach another device: no remote copies, remote signals or barrier semaphores. Data moves between devices by JAX's collectives and lax.ppermute only.
A program may use at most 64 MiB of HBM per device.

v0:
```python
import math

import jax
import jax.numpy as jnp
from jax import lax
from jax.sharding import PartitionSpec as P

STEPS = 2
POLAR = 6


gelu_scale = 0.7978845608028654
gelu_cubic = 0.044715
epsilon = 1e-05


def spread(block, axis, holder):
    block = jnp.where(lax.axis_index(axis) == holder, block, jnp.zeros_like(block))
    return lax.psum(block, axis)


def extended(block, sides, width):
    for axis, dim in sides:
        count = lax.axis_size(axis)
        forward = [(i, i + 1) for i in range(count - 1)]
        backward = [(target, source) for source, target in forward]
        low = lax.ppermute(
            lax.slice_in_dim(block, block.shape[dim] - width, None, axis=dim), axis, forward
        )
        high = lax.ppermute(lax.slice_in_dim(block, 0, width, axis=dim), axis, backward)
        block = jnp.concatenate([low, block, high], axis=dim)
    return block


def fourier(width):
    index = jnp.arange(width, dtype=jnp.int32)
    wavenumber = jnp.where(index <= width // 2, index, index - width // 2)
    phase = index[:, None] * wavenumber[None, :] % width
    angle = phase.astype(jnp.float32) * (2.0 * math.pi / width)
    factor = jnp.where(
        (index == 0) | (index == width // 2), 1.0 / math.sqrt(width), math.sqrt(2.0 / width)
    ).astype(jnp.float32)
    table = (
        jnp.where(index[None, :] <= width // 2, jnp.cos(angle), jnp.sin(angle)) * factor[None, :]
    )
    return (table.astype(jnp.bfloat16), wavenumber)


def gelu_pair(hidden):
    inner = jnp.tanh(gelu_scale * (hidden + gelu_cubic * hidden * hidden * hidden))
    value = 0.5 * hidden * (1.0 + inner)
    slope = 0.5 * (1.0 + inner) + 0.5 * hidden * (1.0 - inner * inner) * gelu_scale * (
        1.0 + 3.0 * gelu_cubic * hidden * hidden
    )
    return (value, slope)


def depthwise(padded, kernel):
    wrapped = jnp.concatenate([padded[:, :, -3:], padded, padded[:, :, :3]], axis=2).astype(
        jnp.float32
    )
    filters = kernel[:, :, None, :]
    result = lax.conv_general_dilated(
        wrapped[None],
        filters,
        (1, 1),
        "VALID",
        dimension_numbers=("NHCW", "HWIO", "NHCW"),
        feature_group_count=kernel.shape[2],
        precision=lax.Precision.HIGHEST,
    )
    return result[0]


def polar_filter(block, limits, table, wavenumber):
    keep = (wavenumber[None, :] <= limits[:, None]).astype(jnp.float32)
    spectrum = (
        jnp.einsum("rcw,wk->rck", block, table, preferred_element_type=jnp.float32)
        * keep[:, None, :]
    )
    spectrum = spectrum.astype(jnp.bfloat16)
    return jnp.einsum("rck,wk->rcw", spectrum, table, preferred_element_type=jnp.float32).astype(
        jnp.bfloat16
    )


def per_device(
    states, land_mask, cutoff, kernel, norm_gain, norm_bias, weight_in, bias_in, weight_out
):
    member = states[0]
    is_control = lax.axis_index("mem") == 0
    table, wavenumber = fourier(member.shape[2])
    land = land_mask.astype(jnp.float32)[:, None, :]
    gain = norm_gain[:, None]
    offset = norm_bias[:, None]
    shift_in = bias_in[:, None]

    def mix_row(pair):
        control_row, tangent_row = pair
        centered = control_row - jnp.mean(control_row, axis=0, keepdims=True)
        scale = lax.rsqrt(jnp.mean(centered * centered, axis=0, keepdims=True) + epsilon)
        unit = centered * scale
        normed = (unit * gain + offset).astype(jnp.bfloat16)
        hidden = (
            jnp.einsum("ch,cw->hw", weight_in, normed, preferred_element_type=jnp.float32)
            + shift_in
        )
        value, slope = gelu_pair(hidden)
        average = jnp.mean(tangent_row, axis=0, keepdims=True)
        along = jnp.mean(tangent_row * unit, axis=0, keepdims=True)
        tangent_normed = (gain * scale * (tangent_row - average - unit * along)).astype(
            jnp.bfloat16
        )
        tangent_hidden = jnp.einsum(
            "ch,cw->hw", weight_in, tangent_normed, preferred_element_type=jnp.float32
        )
        tangent_mix = (slope * tangent_hidden).astype(jnp.bfloat16)
        mixed = jnp.where(is_control, value.astype(jnp.bfloat16), tangent_mix)
        return jnp.einsum("hc,hw->cw", weight_out, mixed, preferred_element_type=jnp.float32)

    for step in range(STEPS):
        control = spread(member, "mem", 0)
        padded = extended(jnp.stack([control, member]), (("lat", 1),), 3)
        control_padded = padded[0]
        member_padded = padded[1]
        control_conv = depthwise(control_padded, kernel)
        tangent_conv = depthwise(member_padded, kernel)
        update = lax.map(mix_row, (control_conv, tangent_conv))
        unfiltered = (land * (member.astype(jnp.float32) + update)).astype(jnp.bfloat16)
        columns = lax.all_to_all(unfiltered, "lat", split_axis=1, concat_axis=0, tiled=True)
        total_rows = columns.shape[0]
        polar = jnp.concatenate([columns[:POLAR], columns[total_rows - POLAR :]], axis=0)
        back = polar_filter(polar, cutoff, table, wavenumber)
        columns = jnp.concatenate(
            [back[:POLAR], columns[POLAR : total_rows - POLAR], back[POLAR:]], axis=0
        )
        member = lax.all_to_all(columns, "lat", split_axis=0, concat_axis=1, tiled=True)
    return member[None]


def solution(mesh):
    in_specs = (
        P(("runs", "mem"), "lat", None, None),
        P("lat", None),
        P(),
        P(),
        P(),
        P(),
        P(),
        P(),
        P(),
    )
    out_specs = P(("runs", "mem"), "lat", None, None)
    return jax.shard_map(
        per_device, mesh=mesh, in_specs=in_specs, out_specs=out_specs, check_vma=False
    )
```

profile of v0, /device:TPU:0, one launch (start us, length us, event | category | flops | bytes accessed | tf_op | source)
XLA Modules:
  0.0 515.5 jit_solution(4254657273692025866)
XLA Ops:
  6.6 2.1 broadcast_select_fusion
  8.7 38.0 %all-reduce.3.cloned.1.call-done = bf16[1,3,160,768]{3,2,1,0:T(8,128)(2,1)} async-done(((bf16[1,3,160,768]{3,2,1,0:T(8,128)(2,1)}), bf16[1,3,160,768]{3,2,1,0:T(8,128)(2,1)}) %all-reduce.3.cloned.1.call-update) | async-done | bytes 737296 | tf_op jit(solution)/shard_map/psum | solution.py:19
  47.9 4.5 collective-permute-start
  53.7 28.4 %collective-permute-done = bf16[2,3,160,768]{3,2,1,0:T(8,128)(2,1)} collective-permute-done((bf16[2,3,160,768]{3,2,1,0:T(8,128)(2,1)S(1)}, bf16[2,3,160,768]{3,2,1,0:T(8,128)(2,1)}, u32[]{:S(2)}, u32[]{:S(2)}) %collective-permute-start) | collective-permute-done | bytes 1474592 | tf_op jit(solution)/shard_map/ppermute | solution.py:27
  82.1 5.3 %collective-permute-done.1 = bf16[2,3,160,768]{3,2,1,0:T(8,128)(2,1)} collective-permute-done((bf16[2,3,160,768]{3,2,1,0:T(8,128)(2,1)S(1)}, bf16[2,3,160,768]{3,2,1,0:T(8,128)(2,1)}, u32[]{:S(2)}, u32[]{:S(2)}) %collective-permute-start.1) | collective-permute-done | bytes 1474592 | tf_op jit(solution)/shard_map/ppermute | solution.py:30
  87.5 2.0 pad_maximum_fusion
  90.2 4.6 maximum_bitcast_fusion
  94.8 1.7 pad.2
  96.5 5.5 %reshape.112 = bf16[9,160,1,8,97]{4,3,1,0,2:T(8,128)(2,1)S(1)} reshape(bf16[9,160,1,776]{3,1,0,2:T(8,128)(2,1)} %pad.2) | data formatting | bytes 4469760 | tf_op jit(solution)/shard_map/conv_general_dilated | solution.py:63
  102.0 5.5 %copy.89 = bf16[9,160,1,8,97]{1,3,4,0,2:T(8,128)(2,1)} copy(bf16[9,160,1,8,97]{4,3,1,0,2:T(8,128)(2,1)S(1)} %reshape.112) | data formatting | bytes 4469760 | tf_op jit(solution)/shard_map/conv_general_dilated | solution.py:63
  108.5 14.1 %fusion.147 = f32[3,8,97,160]{3,1,2,0:T(8,128)} fusion(bf16[9,160,1,7,6]{1,3,4,0,2:T(8,128)(2,1)S(1)} %slice.102, bf16[9,160,1,8,97]{1,3,4,0,2:T(8,128)(2,1)} %copy.89, pred[8,97]{0,1:T(8,128)(4,1)S(1)} %copy-done.12, f32[7,7,1,160]{3,1,0,2:T(8,128)S(1)} %bitcast.337), kind=kOutput, calls=%fused_computation.176 | convolution fusion | flops 226510080 | bytes 3877896 | tf_op jit(solution)/shard_map/conv_general_dilated | solution.py:63
  122.7 2.9 copy.91
  125.6 1.8 reshape.116
  127.4 2.7 slice_bitcast_fusion.6
  130.1 1.7 pad
  131.9 5.5 %reshape.105 = bf16[9,160,1,8,97]{4,3,1,0,2:T(8,128)(2,1)S(1)} reshape(bf16[9,160,1,776]{3,1,0,2:T(8,128)(2,1)} %pad) | data formatting | bytes 4469760 | tf_op jit(solution)/shard_map/conv_general_dilated | solution.py:63
  137.4 5.5 %copy.85 = bf16[9,160,1,8,97]{1,3,4,0,2:T(8,128)(2,1)} copy(bf16[9,160,1,8,97]{4,3,1,0,2:T(8,128)(2,1)S(1)} %reshape.105) | data formatting | bytes 4469760 | tf_op jit(solution)/shard_map/conv_general_dilated | solution.py:63
  143.8 14.2 %fusion.150 = f32[3,8,97,160]{3,1,2,0:T(8,128)} fusion(bf16[9,160,1,7,6]{1,3,4,0,2:T(8,128)(2,1)S(1)} %slice.97, bf16[9,160,1,8,97]{1,3,4,0,2:T(8,128)(2,1)} %copy.85, pred[8,97]{0,1:T(8,128)(4,1)S(1)} %copy-done.12, f32[7,7,1,160]{3,1,0,2:T(8,128)S(1)} %bitcast.334), kind=kOutput, calls=%fused_computation.177 | convolution fusion | flops 226510080 | bytes 3877896 | tf_op jit(solution)/shard_map/conv_general_dilated | solution.py:63
  158.0 2.6 copy.87
  160.5 1.8 reshape.109
  162.4 1.5 slice_bitcast_fusion.7
  165.1 23.7 %while.20 = (s32[]{:T(128)}, f32[3,160,768]{2,1,0:T(8,128)}, pred[]{:T(512)}, f32[3,160,768]{2,1,0:T(8,128)S(1)}, f32[160,1]{0,1:T(1,128)S(1)}, /*index=5*/f32[1...) while((s32[]{:T(128)}, f32[3,160,768]{2,1,0:T(8,128)}, ...), condition=%wide.region_6.7_spmd, body=%wide.region_1.6_spmd.sunk | while | flops 485868288 | bytes 9054857 | solution.py:128
  166.3 1.5 fusion.259
  169.1 3.9 fusion.261
  174.2 1.5 fusion.259
  176.9 4.0 fusion.261
  182.1 1.5 fusion.259
  184.8 4.0 fusion.261
  188.8 1.7 fusion.140
  190.6 1.6 copy.92
  192.2 3.5 all-to-all-start
  196.0 22.4 %all-to-all-done = bf16[3,160,768]{2,0,1:T(4,128)(2,1)S(1)} async-done(((bf16[3,160,768]{2,0,1:T(4,128)(2,1)}), bf16[3,160,768]{2,0,1:T(4,128)(2,1)S(1)}, u32[]{:S(2)}, u32[]{:S(2)}) %all-to-all-start) | async-done | bytes 737312 | tf_op jit(solution)/shard_map/all_to_all | solution.py:130
  218.6 10.1 %multiply_convert_fusion.6.clone.2 = bf16[12,40,768]{2,1,0:T(8,128)(2,1)S(1)} fusion(f32[768]{0:T(1024)S(1)} %fusion.181, s32[768]{0:T(1024)S(1)} %add_select_fusion.1, pred[768]{0:T(1024)(128)(4,1)S(1)} %iota_compare_fusion.3, bf16[6,40,768]{2,1,0:T(8,128)(2,1)S(1)} %bitcast.349, bf16[6,40,768]{2,1,0:T(8,128)(2,1)S(1)} %bitcast.347, ...), kind=kOutput, calls=%fused_computation.173.clone.clone.clone | convolution fusion | flops 574414848 | bytes 1518336 | tf_op jit(solution)/shard_map/rcw,wk->rck/dot_general | solution.py:78
  228.7 10.9 %convolution_convert_fusion.1 = bf16[12,40,768]{2,1,0:T(8,128)(2,1)S(1)} fusion(f32[768]{0:T(1024)S(1)} %fusion.181, s32[768]{0:T(1024)S(1)} %add_select_fusion.1, pred[768]{0:T(1024)(128)(4,1)S(1)} %iota_compare_fusion.3, bf16[12,40,768]{2,1,0:T(8,128)(2,1)S(1)} %multiply_convert_fusion.6.clone.2), kind=kOutput, calls=%fused_computation.179 | convolution fusion | flops 573677568 | bytes 1481472 | tf_op jit(solution)/shard_map/rck,wk->rcw/dot_general | solution.py:82
  239.6 21.0 %all_to_all.60 = bf16[12,40,768]{2,1,0:T(8,128)(2,1)S(1)} all-to-all(bf16[12,40,768]{2,1,0:T(8,128)(2,1)S(1)} %convolution_convert_fusion.1), channel_id=1, replica_groups=mesh['runs'=2,'mem'=4,'lat'=4] {'lat'}, dimensions={0} | all-to-all | bytes 1474560 | tf_op jit(solution)/shard_map/all_to_all | solution.py:137
  261.6 33.1 %all-reduce.5.cloned.1.call-done = bf16[1,3,160,768]{3,2,1,0:T(8,128)(2,1)} async-done(((bf16[1,3,160,768]{3,2,1,0:T(8,128)(2,1)}), bf16[1,3,160,768]{3,2,1,0:T(8,128)(2,1)}) %all-reduce.5.cloned.1.call-update) | async-done | bytes 737296 | tf_op jit(solution)/shard_map/psum | solution.py:19
  296.0 3.5 collective-permute-start.2
  300.8 29.5 %collective-permute-done.2 = bf16[2,3,160,768]{3,2,1,0:T(8,128)(2,1)S(1)} collective-permute-done((bf16[2,3,160,768]{3,2,1,0:T(8,128)(2,1)S(1)}, bf16[2,3,160,768]{3,2,1,0:T(8,128)(2,1)S(1)}, u32[]{:S(2)}, u32[]{:S(2)}) %collective-permute-start.2) | collective-permute-done | bytes 1474592 | tf_op jit(solution)/shard_map/ppermute | solution.py:27
  330.3 4.2 collective-permute-done.3
  337.0 1.7 pad.6
  338.7 6.6 %reshape.126 = bf16[9,160,1,8,97]{4,3,1,0,2:T(8,128)(2,1)} reshape(bf16[9,160,1,776]{3,1,0,2:T(8,128)(2,1)} %pad.6) | data formatting | bytes 4469760 | tf_op jit(solution)/shard_map/conv_general_dilated | solution.py:63
  345.3 7.2 %copy.102 = bf16[9,160,1,8,97]{1,3,4,0,2:T(8,128)(2,1)} copy(bf16[9,160,1,8,97]{4,3,1,0,2:T(8,128)(2,1)} %reshape.126) | data formatting | bytes 4469760 | tf_op jit(solution)/shard_map/conv_general_dilated | solution.py:63
  353.5 14.2 %fusion.141 = f32[3,8,97,160]{3,1,2,0:T(8,128)} fusion(bf16[9,160,1,7,6]{1,3,4,0,2:T(8,128)(2,1)S(1)} %slice.114, bf16[9,160,1,8,97]{1,3,4,0,2:T(8,128)(2,1)} %copy.102, pred[8,97]{0,1:T(8,128)(4,1)S(1)} %copy-done.13, f32[7,7,1,160]{3,1,0,2:T(8,128)S(1)} %bitcast.335), kind=kOutput, calls=%fused_computation.174 | convolution fusion | flops 226510080 | bytes 3877896 | tf_op jit(solution)/shard_map/conv_general_dilated | solution.py:63
  367.6 3.0 copy.104
  370.7 2.9 reshape.130
  373.6 2.6 slice_bitcast_fusion.4
  377.9 1.7 pad.4
  379.6 5.5 %reshape.119 = bf16[9,160,1,8,97]{4,3,1,0,2:T(8,128)(2,1)S(1)} reshape(bf16[9,160,1,776]{3,1,0,2:T(8,128)(2,1)} %pad.4) | data formatting | bytes 4469760 | tf_op jit(solution)/shard_map/conv_general_dilated | solution.py:63
  385.1 5.5 %copy.98 = bf16[9,160,1,8,97]{1,3,4,0,2:T(8,128)(2,1)} copy(bf16[9,160,1,8,97]{4,3,1,0,2:T(8,128)(2,1)S(1)} %reshape.119) | data formatting | bytes 4469760 | tf_op jit(solution)/shard_map/conv_general_dilated | solution.py:63
  391.6 14.2 %fusion.144 = f32[3,8,97,160]{3,1,2,0:T(8,128)} fusion(bf16[9,160,1,7,6]{1,3,4,0,2:T(8,128)(2,1)S(1)} %slice.109, bf16[9,160,1,8,97]{1,3,4,0,2:T(8,128)(2,1)} %copy.98, pred[8,97]{0,1:T(8,128)(4,1)S(1)} %copy-done.13, f32[7,7,1,160]{3,1,0,2:T(8,128)S(1)} %bitcast.336), kind=kOutput, calls=%fused_computation.175 | convolution fusion | flops 226510080 | bytes 3877896 | tf_op jit(solution)/shard_map/conv_general_dilated | solution.py:63
  405.8 2.6 copy.100
  408.3 1.8 reshape.123
  412.9 23.9 %while.21 = (s32[]{:T(128)}, f32[3,160,768]{2,1,0:T(8,128)}, pred[]{:T(512)}, f32[3,160,768]{2,1,0:T(8,128)S(1)}, f32[160,1]{0,1:T(1,128)S(1)}, /*index=5*/f32[1...) while((s32[]{:T(128)}, f32[3,160,768]{2,1,0:T(8,128)}, ...), condition=%wide.region_13.14_spmd, body=%wide.region_8.13_spmd.sunk | while | flops 485868288 | bytes 9054857 | solution.py:128
  414.3 1.5 fusion.266
  417.0 3.9 fusion.268
  422.2 1.5 fusion.266
  424.9 4.0 fusion.268
  430.1 1.5 fusion.266
  432.8 4.0 fusion.268
  436.8 1.7 fusion.138
  439.1 25.8 %all_to_all.61 = bf16[3,160,768]{2,0,1:T(4,128)(2,1)S(1)} all-to-all(bf16[3,160,768]{2,0,1:T(4,128)(2,1)S(1)} %copy.105), channel_id=1, replica_groups=mesh['runs'=2,'mem'=4,'lat'=4] {'lat'}, dimensions={1} | all-to-all | bytes 1474560 | tf_op jit(solution)/shard_map/all_to_all | solution.py:130
  465.8 10.1 %multiply_convert_fusion.5.clone.5 = bf16[12,40,768]{2,1,0:T(8,128)(2,1)S(1)} fusion(f32[768]{0:T(1024)S(1)} %fusion.181, s32[768]{0:T(1024)S(1)} %add_select_fusion.1, pred[768]{0:T(1024)(128)(4,1)S(1)} %iota_compare_fusion.3, bf16[6,40,768]{2,1,0:T(8,128)(2,1)S(1)} %bitcast.348, bf16[6,40,768]{2,1,0:T(8,128)(2,1)S(1)} %bitcast.346, ...), kind=kOutput, calls=%fused_computation.172.clone.clone.clone.2 | convolution fusion | flops 574414848 | bytes 1518336 | tf_op jit(solution)/shard_map/rcw,wk->rck/dot_general | solution.py:78
  475.9 10.7 %convolution_convert_fusion = bf16[12,40,768]{2,1,0:T(8,128)(2,1)S(1)} fusion(f32[768]{0:T(1024)S(1)} %fusion.181, s32[768]{0:T(1024)S(1)} %add_select_fusion.1, pred[768]{0:T(1024)(128)(4,1)S(1)} %iota_compare_fusion.3, bf16[12,40,768]{2,1,0:T(8,128)(2,1)S(1)} %multiply_convert_fusion.5.clone.5), kind=kOutput, calls=%fused_computation.178 | convolution fusion | flops 573677568 | bytes 1481472 | tf_op jit(solution)/shard_map/rck,wk->rcw/dot_general | solution.py:82
  486.6 20.6 %all_to_all.62 = bf16[12,40,768]{2,1,0:T(8,128)(2,1)S(1)} all-to-all(bf16[12,40,768]{2,1,0:T(8,128)(2,1)S(1)} %convolution_convert_fusion), channel_id=1, replica_groups=mesh['runs'=2,'mem'=4,'lat'=4] {'lat'}, dimensions={0} | all-to-all | bytes 1474560 | tf_op jit(solution)/shard_map/all_to_all | solution.py:137
  (119 shorter events, 35.8 us)
Async XLA Ops:
  6.5 102.0 %copy-start = (f32[7,7,160]{2,1,0:T(8,128)S(1)}, f32[7,7,160]{2,1,0:T(8,128)}, u32[]{:S(2)}) copy-start(f32[7,7,160]{2,1,0:T(8,128)} %param.16) | copy-start | bytes 94084
  6.5 41.3 %copy-start.3 = (bf16[1,3,160,768]{3,2,1,0:T(8,128)(2,1)S(1)}, bf16[1,3,160,768]{3,2,1,0:T(8,128)(2,1)}, u32[]{:S(2)}) copy-start(bf16[1,3,160,768]{3,2,1,0:T(8,128)(2,1)} %param.13) | copy-start | bytes 2211844
  6.5 40.1 %all-reduce.3.cloned.1.call-start = ((), (), s32[]{:S(2)}) async-start(), calls=%async_computation.4 | async-start | bytes 1474560 | tf_op jit(solution)/shard_map/psum | solution.py:19
  6.5 47.1 %copy-start.10 = (f32[640]{0:T(1024)S(1)}, f32[640]{0:T(1024)}, u32[]{:S(2)}) copy-start(f32[640]{0:T(1024)} %param.20) | copy-start | bytes 7684
  6.5 47.1 %copy-start.9 = (s32[3,768]{1,0:T(4,128)S(1)}, s32[3,768]{1,0:T(4,128)}, u32[]{:S(2)}) copy-start(s32[3,768]{1,0:T(4,128)} %param.14) | copy-start | bytes 27652
  47.9 34.3 %collective-permute-start = (bf16[2,3,160,768]{3,2,1,0:T(8,128)(2,1)S(1)}, bf16[2,3,160,768]{3,2,1,0:T(8,128)(2,1)}, u32[]{:S(2)}, u32[]{:S(2)}) collective-permute-start(bf16[2,3,160,768]{3,2,1,0:T(8,128)(2,1)S(1)} %constant_dynamic-update-slice_fusion), channel_id=1, source_target_pairs={{0,1},{1,2},{2,3},{4,5},{5,6},{6,7},{8,9},{9,10},{10,11},{12,13},{... | collective-permute-start | bytes 4423688 | tf_op jit(solution)/shard_map/ppermute | solution.py:27
  52.4 35.1 %collective-permute-start.1 = (bf16[2,3,160,768]{3,2,1,0:T(8,128)(2,1)S(1)}, bf16[2,3,160,768]{3,2,1,0:T(8,128)(2,1)}, u32[]{:S(2)}, u32[]{:S(2)}) collective-permute-start(bf16[2,3,160,768]{3,2,1,0:T(8,128)(2,1)S(1)} %constant_dynamic-update-slice_fusion), channel_id=1, source_target_pairs={{1,0},{2,1},{3,2},{5,4},{6,5},{7,6},{9,8},{10,9},{11,10},{13,12},{... | collective-permute-start | bytes 4423688 | tf_op jit(solution)/shard_map/ppermute | solution.py:30
  102.0 6.5 %copy-start.12 = (pred[8,97]{0,1:T(8,128)(4,1)S(1)}, pred[8,97]{0,1:T(8,128)(4,1)}, u32[]{:S(2)}) copy-start(pred[8,97]{0,1:T(8,128)(4,1)} %constant.118) | copy-start | bytes 2332
  127.4 2.8 copy-start.2
  162.4 2.8 copy-start.5
  162.4 2.8 copy-start.6
  190.5 5.4 %copy-start.11 = (s32[12]{0:T(128)S(1)}, s32[12]{0:T(128)}, u32[]{:S(2)}) copy-start(s32[12]{0:T(128)} %param.15) | copy-start | bytes 148
  192.2 26.2 %all-to-all-start = ((bf16[3,160,768]{2,0,1:T(4,128)(2,1)}), bf16[3,160,768]{2,0,1:T(4,128)(2,1)S(1)}, u32[]{:S(2)}, u32[]{:S(2)}) async-start(bf16[3,160,768]{2,0,1:T(4,128)(2,1)} %copy.92), calls=%async_computation | async-start | bytes 1966080 | tf_op jit(solution)/shard_map/all_to_all | solution.py:130
  195.7 99.0 %all-reduce.5.cloned.1.call-start = ((), (), s32[]{:S(2)}) async-start(), calls=%async_computation.5 | async-start | bytes 1474560 | tf_op jit(solution)/shard_map/psum | solution.py:19
  196.0 32.7 %copy-start.7 = (f32[12,768]{1,0:T(8,128)}, f32[12,768]{1,0:T(8,128)S(1)}, u32[]{:S(2)}) copy-start(f32[12,768]{1,0:T(8,128)S(1)} %compare_convert_fusion) | copy-start | bytes 110596
  261.6 72.9 %copy-start.1 = (bf16[4,3,40,768]{3,2,0,1:T(8,128)(2,1)}, bf16[4,3,40,768]{3,2,0,1:T(8,128)(2,1)S(1)}, u32[]{:S(2)}) copy-start(bf16[4,3,40,768]{3,2,0,1:T(8,128)(2,1)S(1)} %copy.96) | copy-start | bytes 2211844
  294.7 39.8 %copy-start.4 = (bf16[1,3,160,768]{3,2,1,0:T(8,128)(2,1)S(1)}, bf16[1,3,160,768]{3,2,1,0:T(8,128)(2,1)}, u32[]{:S(2)}) copy-start(bf16[1,3,160,768]{3,2,1,0:T(8,128)(2,1)} %all-reduce.5.cloned.1.call-done) | copy-start | bytes 2211844
  296.0 34.3 %collective-permute-start.2 = (bf16[2,3,160,768]{3,2,1,0:T(8,128)(2,1)S(1)}, bf16[2,3,160,768]{3,2,1,0:T(8,128)(2,1)S(1)}, u32[]{:S(2)}, u32[]{:S(2)}) collective-permute-start(bf16[2,3,160,768]{3,2,1,0:T(8,128)(2,1)S(1)} %pad_maximum_fusion.2), channel_id=1, source_target_pairs={{0,1},{1,2},{2,3},{4,5},{5,6},{6,7},{8,9},{9,10},{10,11},{12,13},{... | collective-permute-start | bytes 4423688 | tf_op jit(solution)/shard_map/ppermute | solution.py:27
  299.5 35.0 %collective-permute-start.3 = (bf16[2,3,160,768]{3,2,1,0:T(8,128)(2,1)S(1)}, bf16[2,3,160,768]{3,2,1,0:T(8,128)(2,1)S(1)}, u32[]{:S(2)}, u32[]{:S(2)}) collective-permute-start(bf16[2,3,160,768]{3,2,1,0:T(8,128)(2,1)S(1)} %pad_maximum_fusion.2), channel_id=1, source_target_pairs={{1,0},{2,1},{3,2},{5,4},{6,5},{7,6},{9,8},{10,9},{11,10},{13,12},{... | collective-permute-start | bytes 4423688 | tf_op jit(solution)/shard_map/ppermute | solution.py:30
  345.3 8.2 %copy-start.13 = (pred[8,97]{0,1:T(8,128)(4,1)S(1)}, pred[8,97]{0,1:T(8,128)(4,1)}, u32[]{:S(2)}) copy-start(pred[8,97]{0,1:T(8,128)(4,1)} %constant.118) | copy-start | bytes 2332
  465.0 0.8 copy-start.8
Sparse Core Ops, SparseCore 0:
  9.7 36.8 all-reduce.2
  261.6 33.0 all-reduce.4
where the time goes:
time: 526 us; the launch traced here: 515 us
  waiting for transfers between devices  161 us (31%)
  matrix products  131 us (25%)
  local copies, waits for them, and re-layouts  94.5 us (18%)
  blocking collectives  67.5 us (13%)
  other arithmetic  32.2 us (6%)
  starting transfers between devices  14.3 us (3%)
  between operations  14.3 us (3%)
    psum x2, waiting for transfers between devices, spread(): return lax.psum(block, axis)  71.1 us
    conv_general_dilated x20, local copies, waits for them, and re-layouts, depthwise(): lax.conv_general_dilated(wrapped[None], filters, (1, 1), 'VALID', dimensi...  70.1 us
    ppermute x2, waiting for transfers between devices, extended(): lax.ppermute(lax.slice_in_dim(block, block.shape[dim] - width, None, axis...  57.9 us
    conv_general_dilated x4, matrix products, depthwise(): lax.conv_general_dilated(wrapped[None], filters, (1, 1), 'VALID', dimensi...  56.6 us
    all_to_all x2, blocking collectives, per_device(): lax.all_to_all(columns, 'lat', split_axis=0, concat_axis=1, tiled=True)  41.6 us
    all_to_all x1, blocking collectives, per_device(): lax.all_to_all(unfiltered, 'lat', split_axis=1, concat_axis=0, tiled=True)  25.8 us
    dot_general x6, matrix products, mix_row(): jnp.einsum('hc,hw->cw', weight_out, mixed, preferred_element_type=jnp.flo...  23.8 us
    all_to_all x1, waiting for transfers between devices, per_device(): lax.all_to_all(unfiltered, 'lat', split_axis=1, concat_axis=0, tiled=True)  22.4 us
  transfers between devices with their start and end apart: 7, of which 7 were waited for; matrix products, arithmetic and copies ran while one was open for 0% of the time, Pallas kernels for 0%

commit v1 on v0

v1 whole, which is shorter than its diff:
```python
import math

import jax
import jax.numpy as jnp
import numpy as np
from jax import lax
from jax.experimental import pallas as pl
from jax.experimental.pallas import tpu as pltpu
from jax.sharding import PartitionSpec as P

STEPS = 2
POLAR = 6
HALO = 3
TAPS = 7
GROUP = 16

gelu_scale = 0.7978845608028654
gelu_cubic = 0.044715
epsilon = 1e-05


def fourier(width):
    index = np.arange(width, dtype=np.int32)
    wavenumber = np.where(index <= width // 2, index, index - width // 2).astype(np.int32)
    phase = index[:, None] * wavenumber[None, :] % width
    angle = phase.astype(np.float64) * (2.0 * math.pi / width)
    factor = np.where((index == 0) | (index == width // 2), 1.0 / math.sqrt(width), math.sqrt(2.0 / width))
    table = np.where(index[None, :] <= width // 2, np.cos(angle), np.sin(angle)) * factor[None, :]
    return table.astype(np.float32).astype(jnp.bfloat16), wavenumber


def tap_matrix(kernel, rows):
    channels = kernel.shape[2]
    groups = channels // GROUP
    shifted = jnp.stack([jnp.pad(kernel, ((r, rows - 1 - r), (0, 0), (0, 0))) for r in range(rows)])
    shifted = shifted.transpose(3, 2, 0, 1).reshape(groups, GROUP, TAPS, rows, rows + 2 * HALO)
    shifted = shifted.transpose(0, 2, 3, 1, 4)
    high = shifted.astype(jnp.bfloat16)
    low = (shifted - high.astype(jnp.float32)).astype(jnp.bfloat16)
    eye = jnp.eye(GROUP, dtype=jnp.bfloat16)
    both = jnp.stack([high, low], axis=4)
    full = both[..., None] * eye[:, None, None, :]
    return full.reshape(groups, TAPS * rows * GROUP, 2 * (rows + 2 * HALO) * GROUP)


def convolve(up, own, down, taps, out):
    rows, channels, width = out.shape

    def group(b, _):
        at = pl.ds(pl.multiple_of(b * GROUP, GROUP), GROUP)
        field = jnp.concatenate([up[:, at, :], own[:, at, :], down[:, at, :]], axis=0)
        field = field.reshape((rows + 2 * HALO) * GROUP, width)
        field = jnp.concatenate([field, field], axis=0)
        parts = jnp.dot(taps[b], field, preferred_element_type=jnp.float32)
        size = rows * GROUP
        total = parts[HALO * size : (HALO + 1) * size]
        for j in range(TAPS):
            if j != HALO:
                total = total + pltpu.roll(parts[j * size : (j + 1) * size], (HALO - j) % width, 1)
        out[:, at, :] = total.reshape(rows, GROUP, width)
        return 0

    lax.fori_loop(0, channels // GROUP, group, 0)


def polar_filter(raw, keep, polar, table, out, select):
    rows, channels, width = out.shape
    spectrum = jnp.dot(raw[...], table[...], preferred_element_type=jnp.float32)
    parts = [
        (spectrum[r * channels : (r + 1) * channels] * keep[r : r + 1, :]).astype(jnp.bfloat16) for r in range(rows)
    ]
    back = lax.dot_general(
        jnp.concatenate(parts, axis=0), table[...], (((1,), (1,)), ((), ())), preferred_element_type=jnp.float32
    ).astype(jnp.bfloat16)
    for r in range(rows):
        row = back[r * channels : (r + 1) * channels]
        if select:
            row = jnp.where(polar[r] > 0, row, raw[r * channels : (r + 1) * channels, :])
        out[r] = row


LANES = 256
CHUNK = 16


def control_kernel(
    select, polar, up, own, down, taps, gain, bias, w_in, b_in, w_out, land, keep, table,
    out, unit_out, scale_out, slope_out, conv, normed, hidden, act, raw,
):
    rows, channels, width = out.shape
    hid = w_in.shape[0]
    convolve(up, own, down, taps, conv)
    for r in range(rows):
        for w in range(0, width, LANES):
            at = slice(w, w + LANES)
            value = conv[r, :, at]
            centered = value - jnp.mean(value, axis=0, keepdims=True)
            scale = lax.rsqrt(jnp.mean(centered * centered, axis=0, keepdims=True) + epsilon)
            unit = centered * scale
            unit_out[r, :, at] = unit
            scale_out[r, :, at] = scale
            normed[:, at] = (unit * gain[...] + bias[...]).astype(jnp.bfloat16)
        hidden[...] = jnp.dot(w_in[...], normed[...], preferred_element_type=jnp.float32)

        def pair(c, _):
            at = pl.ds(pl.multiple_of(c * CHUNK, CHUNK), CHUNK)
            h = hidden[at, :] + b_in[at, :]
            square = h * h
            t = jnp.tanh(h * (gelu_scale + (gelu_scale * gelu_cubic) * square))
            half = 0.5 + 0.5 * t
            act[at, :] = (h * half).astype(jnp.bfloat16)
            slope = half + (0.5 * h) * (1.0 - t * t) * (gelu_scale + (3.0 * gelu_scale * gelu_cubic) * square)
            slope_out[r, at, :] = slope
            return 0

        lax.fori_loop(0, hid // CHUNK, pair, 0)
        update = jnp.dot(w_out[...], act[...], preferred_element_type=jnp.float32)
        raw[r * channels : (r + 1) * channels, :] = (
            land[r : r + 1, :] * (own[r].astype(jnp.float32) + update)
        ).astype(jnp.bfloat16)
    polar_filter(raw, keep, polar, table, out, select)


def tangent_kernel(
    select, polar, up, own, down, taps, gain, w_in, w_out, land, keep, table, unit_in, scale_in, slope_in, advanced,
    out, conv, normed, hidden, act, raw,
):
    rows, channels, width = out.shape
    hid = w_in.shape[0]
    is_control = polar[rows] > 0

    @pl.when(is_control)
    def _():
        out[...] = advanced[...]

    @pl.when(jnp.logical_not(is_control))
    def _():
        convolve(up, own, down, taps, conv)
        for r in range(rows):
            for w in range(0, width, LANES):
                at = slice(w, w + LANES)
                value = conv[r, :, at]
                unit = unit_in[r, :, at]
                average = jnp.mean(value, axis=0, keepdims=True)
                along = jnp.mean(value * unit, axis=0, keepdims=True)
                normed[:, at] = (gain[...] * scale_in[r, :, at] * (value - average - unit * along)).astype(jnp.bfloat16)
            hidden[...] = jnp.dot(w_in[...], normed[...], preferred_element_type=jnp.float32)

            def mix(c, _):
                at = pl.ds(pl.multiple_of(c * CHUNK, CHUNK), CHUNK)
                act[at, :] = (slope_in[r, at, :] * hidden[at, :]).astype(jnp.bfloat16)
                return 0

            lax.fori_loop(0, hid // CHUNK, mix, 0)
            update = jnp.dot(w_out[...], act[...], preferred_element_type=jnp.float32)
            raw[r * channels : (r + 1) * channels, :] = (
                land[r : r + 1, :] * (own[r].astype(jnp.float32) + update)
            ).astype(jnp.bfloat16)
        polar_filter(raw, keep, polar, table, out, select)


def scratch(rows, channels, width, hid):
    return [
        pltpu.VMEM((rows, channels, width), jnp.float32),
        pltpu.VMEM((channels, width), jnp.bfloat16),
        pltpu.VMEM((hid, width), jnp.float32),
        pltpu.VMEM((hid, width), jnp.bfloat16),
        pltpu.VMEM((rows * channels, width), jnp.bfloat16),
    ]


SMEM = pl.BlockSpec(memory_space=pltpu.SMEM)
VMEM = pl.BlockSpec(memory_space=pltpu.VMEM)
LIMIT = 48 << 20


def per_device(
    states, land_mask, cutoff, kernel, norm_gain, norm_bias, weight_in, bias_in, weight_out
):
    member = states[0]
    rows, channels, width = member.shape
    hid = weight_in.shape[1]
    bands = lax.axis_size("lat")
    members = lax.axis_size("mem")
    total_rows = rows * bands
    me = lax.axis_index("mem")
    select = total_rows > 2 * POLAR

    table, wavenumber = fourier(width)
    row = lax.axis_index("lat") * rows + jnp.arange(rows)
    is_polar = (row < POLAR) | (row >= total_rows - POLAR)
    place = jnp.clip(jnp.where(row < POLAR, row, row - total_rows + 2 * POLAR), 0, 2 * POLAR - 1)
    keep = (jnp.asarray(wavenumber)[None, :] <= cutoff[place][:, None]).astype(jnp.float32)
    flags = jnp.concatenate([is_polar.astype(jnp.int32), (me == 0).astype(jnp.int32)[None]])
    land = land_mask.astype(jnp.float32)
    taps = tap_matrix(kernel, rows)
    w_in = weight_in.T
    w_out = weight_out.T
    gain = norm_gain[:, None]
    offset = norm_bias[:, None]
    shift_in = bias_in[:, None]
    table = jnp.asarray(table)

    forward = [(i, i + 1) for i in range(bands - 1)]
    backward = [(i + 1, i) for i in range(bands - 1)]

    def spread(block):
        count = 2
        while count < members:
            sent = lax.ppermute(block, "mem", [(i, i + count) for i in range(0, count, 2) if i + count < members])
            block = jnp.where((me >= count) & (me < 2 * count), sent, block)
            count *= 2
        sent = lax.ppermute(block, "mem", [(i, i + 1) for i in range(0, members - 1, 2)])
        return jnp.where(me % 2 == 1, sent, block)

    params = pltpu.CompilerParams(vmem_limit_bytes=LIMIT)
    field = jax.ShapeDtypeStruct((rows, channels, width), jnp.bfloat16)

    def control_step(up, own, down):
        return pl.pallas_call(
            lambda *refs: control_kernel(select, *refs),
            out_shape=(
                field,
                jax.ShapeDtypeStruct((rows, channels, width), jnp.float32),
                jax.ShapeDtypeStruct((rows, 1, width), jnp.float32),
                jax.ShapeDtypeStruct((rows, hid, width), jnp.float32),
            ),
            in_specs=[SMEM] + [VMEM] * 12,
            out_specs=(VMEM,) * 4,
            scratch_shapes=scratch(rows, channels, width, hid),
            compiler_params=params,
            name="control",
        )(flags, up, own, down, taps, gain, offset, w_in, shift_in, w_out, land, keep, table)

    def tangent_step(up, own, down, unit, scale, slope, advanced):
        return pl.pallas_call(
            lambda *refs: tangent_kernel(select, *refs),
            out_shape=field,
            in_specs=[SMEM] + [VMEM] * 14,
            out_specs=VMEM,
            scratch_shapes=scratch(rows, channels, width, hid),
            compiler_params=params,
            name="tangent",
        )(flags, up, own, down, taps, gain, w_in, w_out, land, keep, table, unit, scale, slope, advanced)

    control = spread(member)
    for step in range(STEPS):
        up = lax.ppermute(member, "lat", forward)
        down = lax.ppermute(member, "lat", backward)
        control_up = spread(up)
        control_down = spread(down)
        control, unit, scale, slope = control_step(control_up, control, control_down)
        member = tangent_step(up, member, down, unit, scale, slope, control)
    return member[None]


def solution(mesh):
    in_specs = (
        P(("runs", "mem"), "lat", None, None),
        P("lat", None),
        P(),
        P(),
        P(),
        P(),
        P(),
        P(),
        P(),
    )
    out_specs = P(("runs", "mem"), "lat", None, None)
    return jax.shard_map(
        per_device, mesh=mesh, in_specs=in_specs, out_specs=out_specs, check_vma=False
    )
```

time: 526 us -> 212 us (0.40)
  the two profiles are of different devices: /device:TPU:0 before, /device:TPU:10 now
where the time goes in v1:
time: 212 us; the launch traced here: 210 us
  Pallas kernels  78.8 us (37%)
  local copies, waits for them, and re-layouts  51.3 us (24%)
  waiting for transfers between devices  47 us (22%)
  starting transfers between devices  25.1 us (12%)
  other arithmetic  7.24 us (3%)
    pallas_call x2, Pallas kernels, control_step(): pl.pallas_call(lambda *refs: control_kernel(select, *refs), out_shape=(fi...  48.6 us
    mul x6, local copies, waits for them, and re-layouts, tap_matrix(): full = both[..., None] * eye[:, None, None, :]  47.2 us
    pallas_call x2, Pallas kernels, tangent_step(): pl.pallas_call(lambda *refs: tangent_kernel(select, *refs), out_shape=fie...  30.2 us
    ppermute x5, waiting for transfers between devices, spread(): lax.ppermute(block, 'mem', [(i, i + count) for i in range(0, count, 2) if...  27.3 us
    ppermute x2, waiting for transfers between devices, per_device(): up = lax.ppermute(member, 'lat', forward)  14.7 us
    ppermute x2, starting transfers between devices, per_device(): up = lax.ppermute(member, 'lat', forward)  7.06 us
    ppermute x5, starting transfers between devices, spread(): lax.ppermute(block, 'mem', [(i, i + 1) for i in range(0, members - 1, 2)])  6.68 us
    ppermute x5, starting transfers between devices, spread(): lax.ppermute(block, 'mem', [(i, i + count) for i in range(0, count, 2) if...  6.55 us
  transfers between devices with their start and end apart: 14, of which 8 were waited for; matrix products, arithmetic and copies ran while one was open for 27% of the time, Pallas kernels for 0%

profile of v1, /device:TPU:10, one launch (start us, length us, event | category | flops | bytes accessed | tf_op | source)
XLA Modules:
  0.0 210.0 jit_solution(9591523941159236474)
XLA Ops:
  0.0 3.6 %collective-permute-start = (bf16[3,160,768]{2,1,0:T(8,128)(2,1)}, bf16[3,160,768]{2,1,0:T(8,128)(2,1)S(1)}, u32[]{:S(2)}, u32[]{:S(2)}) collective-permute-start(bf16[3,160,768]{2,1,0:T(8,128)(2,1)} %bitcast.47), channel_id=1, source_target_pairs={{0,1},{1,2},{2,3},{4,5},{5,6},{6,7},{8,9},{9,10},{10,11},{12,13},{... | collective-permute-start | bytes 2211848 | tf_op jit(solution)/shard_map/ppermute | solution.py:248
  3.6 2.4 %collective-permute-start.1 = (bf16[3,160,768]{2,1,0:T(8,128)(2,1)}, bf16[3,160,768]{2,1,0:T(8,128)(2,1)S(1)}, u32[]{:S(2)}, u32[]{:S(2)}) collective-permute-start(bf16[3,160,768]{2,1,0:T(8,128)(2,1)} %bitcast.48), channel_id=1, source_target_pairs={{1,0},{2,1},{3,2},{5,4},{6,5},{7,6},{9,8},{10,9},{11,10},{13,12},{... | collective-permute-start | bytes 2211848 | tf_op jit(solution)/shard_map/ppermute | solution.py:249
  6.0 1.3 collective-permute-start.4
  7.3 0.9 pad_bitcast_fusion.2
  8.3 0.5 reshape.39
  8.8 1.0 fusion.1
  9.8 0.1 fusion.2
  9.9 1.0 copy-done.5
  10.9 0.4 pad_maximum_fusion
  11.4 0.5 copy.14
  11.9 7.3 %mul.24 = bf16[10,7,3,16,2,9,16]{3,2,1,6,5,4,0:T(4,128)(2,1)} broadcast(bf16[10,7,3,16,2,9]{3,2,1,5,4,0:T(4,128)(2,1)S(1)} %copy.14), dimensions={0,1,2,3,4,5} | broadcast | bytes 2056320 | tf_op jit(solution)/shard_map/mul | solution.py:42
  19.1 30.0 %mul.25 = bf16[10,336,288]{1,2,0:T(8,128)(2,1)} reshape(bf16[10,7,3,16,2,9,16]{3,2,1,6,5,4,0:T(4,128)(2,1)} %mul.24) | data formatting | bytes 3870720 | tf_op jit(solution)/shard_map/mul | solution.py:42
  49.1 4.3 %copy.16 = bf16[10,336,288]{2,1,0:T(8,128)(2,1)} copy(bf16[10,336,288]{1,2,0:T(8,128)(2,1)} %mul.25) | data formatting | bytes 3870720 | tf_op jit(solution)/shard_map/mul | solution.py:42
  53.5 2.2 %mul.26 = bf16[7,3,16,2,9,16]{2,1,0,5,4,3:T(4,128)(2,1)} broadcast(bf16[16,16]{0,1:T(8,128)(2,1)S(1)} %fusion.3), dimensions={2,5} | broadcast | bytes 194048 | tf_op jit(solution)/shard_map/mul | solution.py:42
  55.7 0.0 copy-start.9
  55.7 3.2 %mul.27 = bf16[336,288]{0,1:T(8,128)(2,1)S(1)} reshape(bf16[7,3,16,2,9,16]{2,1,0,5,4,3:T(4,128)(2,1)} %mul.26) | data formatting | bytes 387072 | tf_op jit(solution)/shard_map/mul | solution.py:42
  58.9 0.2 copy.15
  59.1 0.1 copy.21.refs_5_
  59.2 0.2 copy.17
  59.5 0.1 copy.19.refs_6_
  59.6 0.1 broadcast_in_dim.25.refs_8_
  59.8 0.6 gather_fusion
  60.4 0.0 collective-permute-done.refs_1_
  60.4 1.4 collective-permute-start.2
  61.8 3.5 %broadcast_multiply_fusion.refs_4_ = bf16[10,336,288]{2,1,0:T(8,128)(2,1)} fusion(bf16[10,336,288]{2,1,0:T(8,128)(2,1)} %copy.16, bf16[336,288]{1,0:T(8,128)(2,1)S(1)} %copy.15), kind=kLoop, calls=%fused_computation.5 | loop fusion | flops 967680 | bytes 4064256 | tf_op jit(solution)/shard_map/mul | solution.py:42
  65.4 1.3 collective-permute-start.6
  66.7 0.1 add_convert_fusion.refs_0_
  66.7 0.0 collective-permute-done.4
  66.8 1.2 broadcast_select_fusion.3
  68.0 1.3 collective-permute-start.5
  69.3 5.5 %collective-permute-done.2 = bf16[3,160,768]{2,1,0:T(8,128)(2,1)S(1)} collective-permute-done((bf16[3,160,768]{2,1,0:T(8,128)(2,1)S(1)}, bf16[3,160,768]{2,1,0:T(8,128)(2,1)S(1)}, u32[]{:S(2)}, u32[]{:S(2)}) %collective-permute-start.2) | collective-permute-done | bytes 737312 | tf_op jit(solution)/shard_map/ppermute | solution.py:210
  74.8 0.1 broadcast_select_fusion.4
  74.9 0.0 copy-start.8
  74.9 1.3 collective-permute-start.3
  76.2 6.4 %collective-permute-done.6 = bf16[3,160,768]{2,1,0:T(8,128)(2,1)S(1)} collective-permute-done((bf16[3,160,768]{2,1,0:T(8,128)(2,1)S(1)}, bf16[3,160,768]{2,1,0:T(8,128)(2,1)S(1)}, u32[]{:S(2)}, u32[]{:S(2)}) %collective-permute-start.6) | collective-permute-done | bytes 737312 | tf_op jit(solution)/shard_map/ppermute | solution.py:210
  82.7 0.1 broadcast_select_fusion.2
  82.7 1.3 collective-permute-start.7
  84.1 0.1 compare_convert_fusion.refs_11_.refs_9_
  84.2 0.0 collective-permute-done.5
  84.2 0.1 broadcast_select_fusion.8.refs_2_
  84.3 0.1 broadcast_select_fusion.9.refs_1_
  84.4 0.0 copy-start.2
  84.4 0.0 copy-start.3
  84.4 1.5 collective-permute-done.7
  85.9 0.1 broadcast_select_fusion.7.refs_3_
  86.0 24.3 %control.2 = (bf16[3,160,768]{2,1,0:T(8,128)(2,1)S(1)}, f32[3,160,768]{2,1,0:T(8,128)}, f32[3,1,768]{2,1,0:T(1,128)S(1)}, f32[3,640,768]{2,1,0:T(8,128)}) custom-call(s32[4]{0:T(128)S(1)} %add_convert_fusion.refs_0_, bf16[3,160,768]{2,1,0:T(8,128)(2,1)S(1)} %broadcast_select_fusion.9.refs_1_, bf16[3,160,768]{2,1,0:T(8,128)(2,1)S(1)} %broadcast_select_fusion.8.refs_2_, ...), custom_call_target="tpu_custom_call" | custom-call | tf_op jit(solution)/shard_map/control/pallas_call | solution.py:220
  110.3 14.6 %tangent.2.refs_2_ = bf16[3,160,768]{2,1,0:T(8,128)(2,1)S(1)} custom-call(s32[4]{0:T(128)S(1)} %add_convert_fusion.refs_0_, bf16[3,160,768]{2,1,0:T(8,128)(2,1)S(1)} %collective-permute-done.refs_1_, bf16[3,160,768]{2,1,0:T(8,128)(2,1)S(1)} %bitcast.50, bf16[3,160,768]{2,1,0:T(8,128)(2,1)S(1)} %collective-permute-done.1.refs_3_, ...), custom_call_target="tpu_custom_call" | custom-call | tf_op jit(solution)/shard_map/tangent/pallas_call | solution.py:236
  124.9 3.5 %collective-permute-start.8 = (bf16[3,160,768]{2,1,0:T(8,128)(2,1)S(1)}, bf16[3,160,768]{2,1,0:T(8,128)(2,1)S(1)}, u32[]{:S(2)}, u32[]{:S(2)}) collective-permute-start(bf16[3,160,768]{2,1,0:T(8,128)(2,1)S(1)} %tangent.2.refs_2_), channel_id=1, source_target_pairs={{0,1},{1,2},{2,3},{4,5},{5,6},{6,7},{8,9},{9,10},{10,11},{12,13},{... | collective-permute-start | bytes 2211848 | tf_op jit(solution)/shard_map/ppermute | solution.py:248
  128.4 2.4 %collective-permute-start.9 = (bf16[3,160,768]{2,1,0:T(8,128)(2,1)S(1)}, bf16[3,160,768]{2,1,0:T(8,128)(2,1)S(1)}, u32[]{:S(2)}, u32[]{:S(2)}) collective-permute-start(bf16[3,160,768]{2,1,0:T(8,128)(2,1)S(1)} %tangent.2.refs_2_), channel_id=1, source_target_pairs={{1,0},{2,1},{3,2},{5,4},{6,5},{7,6},{9,8},{10,9},{11,10},{13,12},{... | collective-permute-start | bytes 2211848 | tf_op jit(solution)/shard_map/ppermute | solution.py:249
  130.8 14.7 %collective-permute-done.8.refs_1_ = bf16[3,160,768]{2,1,0:T(8,128)(2,1)S(1)} collective-permute-done((bf16[3,160,768]{2,1,0:T(8,128)(2,1)S(1)}, bf16[3,160,768]{2,1,0:T(8,128)(2,1)S(1)}, u32[]{:S(2)}, u32[]{:S(2)}) %collective-permute-start.8) | collective-permute-done | bytes 737312 | tf_op jit(solution)/shard_map/ppermute | solution.py:248
  145.6 1.3 collective-permute-start.10
  146.9 1.9 collective-permute-done.9.refs_3_
  148.7 1.3 collective-permute-start.12
  150.0 8.9 %collective-permute-done.10 = bf16[3,160,768]{2,1,0:T(8,128)(2,1)S(1)} collective-permute-done((bf16[3,160,768]{2,1,0:T(8,128)(2,1)S(1)}, bf16[3,160,768]{2,1,0:T(8,128)(2,1)S(1)}, u32[]{:S(2)}, u32[]{:S(2)}) %collective-permute-start.10) | collective-permute-done | bytes 737312 | tf_op jit(solution)/shard_map/ppermute | solution.py:210
  158.9 0.1 broadcast_select_fusion.1
  159.0 1.3 collective-permute-start.11
  160.4 6.5 %collective-permute-done.12 = bf16[3,160,768]{2,1,0:T(8,128)(2,1)S(1)} collective-permute-done((bf16[3,160,768]{2,1,0:T(8,128)(2,1)S(1)}, bf16[3,160,768]{2,1,0:T(8,128)(2,1)S(1)}, u32[]{:S(2)}, u32[]{:S(2)}) %collective-permute-start.12) | collective-permute-done | bytes 737312 | tf_op jit(solution)/shard_map/ppermute | solution.py:210
  166.8 0.1 broadcast_select_fusion
  166.9 1.3 collective-permute-start.13
  168.3 0.1 broadcast_select_fusion.6.refs_1_
  168.3 1.7 collective-permute-done.13
  170.0 0.1 broadcast_select_fusion.5.refs_3_
  170.1 24.3 %control.3 = (bf16[3,160,768]{2,1,0:T(8,128)(2,1)S(1)}, f32[3,160,768]{2,1,0:T(8,128)}, f32[3,1,768]{2,1,0:T(1,128)S(1)}, f32[3,640,768]{2,1,0:T(8,128)}) custom-call(s32[4]{0:T(128)S(1)} %add_convert_fusion.refs_0_, bf16[3,160,768]{2,1,0:T(8,128)(2,1)S(1)} %broadcast_select_fusion.6.refs_1_, bf16[3,160,768]{2,1,0:T(8,128)(2,1)S(1)} %get-tuple-element.16.refs_14_.refs_2_, ...), custom_call_target="tpu_custom_call" | custom-call | tf_op jit(solution)/shard_map/control/pallas_call | solution.py:220
  194.4 15.5 %tangent.3 = bf16[3,160,768]{2,1,0:T(8,128)(2,1)} custom-call(s32[4]{0:T(128)S(1)} %add_convert_fusion.refs_0_, bf16[3,160,768]{2,1,0:T(8,128)(2,1)S(1)} %collective-permute-done.8.refs_1_, bf16[3,160,768]{2,1,0:T(8,128)(2,1)S(1)} %tangent.2.refs_2_, bf16[3,160,768]{2,1,0:T(8,128)(2,1)S(1)} %collective-permute-done.9.refs_3_, ...), custom_call_target="tpu_custom_call" | custom-call | tf_op jit(solution)/shard_map/tangent/pallas_call | solution.py:236
  (28 shorter events, 0.1 us)
Async XLA Ops:
  0.0 59.7 %copy-start = (s32[12]{0:T(128)S(1)}, s32[12]{0:T(128)}, u32[]{:S(2)}) copy-start(s32[12]{0:T(128)} %param.13) | copy-start | bytes 148
  0.0 60.4 %collective-permute-start = (bf16[3,160,768]{2,1,0:T(8,128)(2,1)}, bf16[3,160,768]{2,1,0:T(8,128)(2,1)S(1)}, u32[]{:S(2)}, u32[]{:S(2)}) collective-permute-start(bf16[3,160,768]{2,1,0:T(8,128)(2,1)} %bitcast.47), channel_id=1, source_target_pairs={{0,1},{1,2},{2,3},{4,5},{5,6},{6,7},{8,9},{9,10},{10,11},{12,13},{... | collective-permute-start | bytes 2211848 | tf_op jit(solution)/shard_map/ppermute | solution.py:248
  3.6 61.8 %collective-permute-start.1 = (bf16[3,160,768]{2,1,0:T(8,128)(2,1)}, bf16[3,160,768]{2,1,0:T(8,128)(2,1)S(1)}, u32[]{:S(2)}, u32[]{:S(2)}) collective-permute-start(bf16[3,160,768]{2,1,0:T(8,128)(2,1)} %bitcast.48), channel_id=1, source_target_pairs={{1,0},{2,1},{3,2},{5,4},{6,5},{7,6},{9,8},{10,9},{11,10},{13,12},{... | collective-permute-start | bytes 2211848 | tf_op jit(solution)/shard_map/ppermute | solution.py:249
  6.0 60.7 %collective-permute-start.4 = (bf16[3,160,768]{2,1,0:T(8,128)(2,1)}, bf16[3,160,768]{2,1,0:T(8,128)(2,1)}, u32[]{:S(2)}, u32[]{:S(2)}) collective-permute-start(bf16[3,160,768]{2,1,0:T(8,128)(2,1)} %bitcast.49), channel_id=1, source_target_pairs={{0,8},{1,9},{2,10},{3,11},{16,24},{17,25},{18,26},{19,27}} | collective-permute-start | bytes 2211848 | tf_op jit(solution)/shard_map/ppermute | solution.py:210
  9.8 1.1 copy-start.5
  55.6 3.5 %copy-start.10 = (f32[160]{0:T(256)S(1)}, f32[160]{0:T(256)}, u32[]{:S(2)}) copy-start(f32[160]{0:T(256)} %param.15) | copy-start | bytes 1924
  55.6 3.6 %copy-start.6 = (bf16[160,640]{1,0:T(8,128)(2,1)S(1)}, bf16[160,640]{1,0:T(8,128)(2,1)}, u32[]{:S(2)}) copy-start(bf16[160,640]{1,0:T(8,128)(2,1)} %param.17) | copy-start | bytes 614404
  55.6 3.8 %copy-start.7 = (s32[3,768]{1,0:T(4,128)S(1)}, s32[3,768]{1,0:T(4,128)}, u32[]{:S(2)}) copy-start(s32[3,768]{1,0:T(4,128)} %param.12) | copy-start | bytes 27652
  55.6 3.8 %copy-start.11 = (f32[160]{0:T(256)S(1)}, f32[160]{0:T(256)}, u32[]{:S(2)}) copy-start(f32[160]{0:T(256)} %param.16) | copy-start | bytes 1924
  55.7 3.9 %copy-start.9 = (f32[640]{0:T(1024)S(1)}, f32[640]{0:T(1024)}, u32[]{:S(2)}) copy-start(f32[640]{0:T(1024)} %param.18) | copy-start | bytes 7684
  60.4 6.4 %copy-start.4 = (bf16[1,3,160,768]{3,2,1,0:T(8,128)(2,1)S(1)}, bf16[1,3,160,768]{3,2,1,0:T(8,128)(2,1)}, u32[]{:S(2)}) copy-start(bf16[1,3,160,768]{3,2,1,0:T(8,128)(2,1)} %param.11) | copy-start | bytes 2211844
  60.4 14.4 %collective-permute-start.2 = (bf16[3,160,768]{2,1,0:T(8,128)(2,1)S(1)}, bf16[3,160,768]{2,1,0:T(8,128)(2,1)S(1)}, u32[]{:S(2)}, u32[]{:S(2)}) collective-permute-start(bf16[3,160,768]{2,1,0:T(8,128)(2,1)S(1)} %collective-permute-done.refs_1_), channel_id=1, source_target_pairs={{0,8},{1,9},{2,10},{3,11},{16,24},{17,25},{18,26},{19,27}} | collective-permute-start | bytes 2211848 | tf_op jit(solution)/shard_map/ppermute | solution.py:210
  65.4 17.3 %collective-permute-start.6 = (bf16[3,160,768]{2,1,0:T(8,128)(2,1)S(1)}, bf16[3,160,768]{2,1,0:T(8,128)(2,1)S(1)}, u32[]{:S(2)}, u32[]{:S(2)}) collective-permute-start(bf16[3,160,768]{2,1,0:T(8,128)(2,1)S(1)} %collective-permute-done.1.refs_3_), channel_id=1, source_target_pairs={{0,8},{1,9},{2,10},{3,11},{16,24},{17,25},{18,26},{19,27}} | collective-permute-start | bytes 2211848 | tf_op jit(solution)/shard_map/ppermute | solution.py:210
  68.0 16.2 %collective-permute-start.5 = (bf16[3,160,768]{2,1,0:T(8,128)(2,1)S(1)}, bf16[3,160,768]{2,1,0:T(8,128)(2,1)S(1)}, u32[]{:S(2)}, u32[]{:S(2)}) collective-permute-start(bf16[3,160,768]{2,1,0:T(8,128)(2,1)S(1)} %broadcast_select_fusion.3), channel_id=1, source_target_pairs={{0,4},{8,12},{1,5},{9,13},{2,6},{10,14},{3,7},{11,15},{16,20},{24,... | collective-permute-start | bytes 2211848 | tf_op jit(solution)/shard_map/ppermute | solution.py:213
  74.9 9.2 %copy-start.8 = (s32[768]{0:T(1024)S(1)}, s32[768]{0:T(1024)}, u32[]{:S(2)}) copy-start(s32[768]{0:T(1024)} %constant.49.clone) | copy-start | bytes 9220
  74.9 9.4 %collective-permute-start.3 = (bf16[3,160,768]{2,1,0:T(8,128)(2,1)S(1)}, bf16[3,160,768]{2,1,0:T(8,128)(2,1)S(1)}, u32[]{:S(2)}, u32[]{:S(2)}) collective-permute-start(bf16[3,160,768]{2,1,0:T(8,128)(2,1)S(1)} %broadcast_select_fusion.4), channel_id=1, source_target_pairs={{0,4},{8,12},{1,5},{9,13},{2,6},{10,14},{3,7},{11,15},{16,20},{24,... | collective-permute-start | bytes 2211848 | tf_op jit(solution)/shard_map/ppermute | solution.py:213
  82.7 3.1 %collective-permute-start.7 = (bf16[3,160,768]{2,1,0:T(8,128)(2,1)S(1)}, bf16[3,160,768]{2,1,0:T(8,128)(2,1)S(1)}, u32[]{:S(2)}, u32[]{:S(2)}) collective-permute-start(bf16[3,160,768]{2,1,0:T(8,128)(2,1)S(1)} %broadcast_select_fusion.2), channel_id=1, source_target_pairs={{0,4},{8,12},{1,5},{9,13},{2,6},{10,14},{3,7},{11,15},{16,20},{24,... | collective-permute-start | bytes 2211848 | tf_op jit(solution)/shard_map/ppermute | solution.py:213
  84.4 1.6 copy-start.2
  84.4 1.6 copy-start.3
  124.9 20.7 %collective-permute-start.8 = (bf16[3,160,768]{2,1,0:T(8,128)(2,1)S(1)}, bf16[3,160,768]{2,1,0:T(8,128)(2,1)S(1)}, u32[]{:S(2)}, u32[]{:S(2)}) collective-permute-start(bf16[3,160,768]{2,1,0:T(8,128)(2,1)S(1)} %tangent.2.refs_2_), channel_id=1, source_target_pairs={{0,1},{1,2},{2,3},{4,5},{5,6},{6,7},{8,9},{9,10},{10,11},{12,13},{... | collective-permute-start | bytes 2211848 | tf_op jit(solution)/shard_map/ppermute | solution.py:248
  128.4 20.4 %collective-permute-start.9 = (bf16[3,160,768]{2,1,0:T(8,128)(2,1)S(1)}, bf16[3,160,768]{2,1,0:T(8,128)(2,1)S(1)}, u32[]{:S(2)}, u32[]{:S(2)}) collective-permute-start(bf16[3,160,768]{2,1,0:T(8,128)(2,1)S(1)} %tangent.2.refs_2_), channel_id=1, source_target_pairs={{1,0},{2,1},{3,2},{5,4},{6,5},{7,6},{9,8},{10,9},{11,10},{13,12},{... | collective-permute-start | bytes 2211848 | tf_op jit(solution)/shard_map/ppermute | solution.py:249
  145.6 13.3 %collective-permute-start.10 = (bf16[3,160,768]{2,1,0:T(8,128)(2,1)S(1)}, bf16[3,160,768]{2,1,0:T(8,128)(2,1)S(1)}, u32[]{:S(2)}, u32[]{:S(2)}) collective-permute-start(bf16[3,160,768]{2,1,0:T(8,128)(2,1)S(1)} %collective-permute-done.8.refs_1_), channel_id=1, source_target_pairs={{0,8},{1,9},{2,10},{3,11},{16,24},{17,25},{18,26},{19,27}} | collective-permute-start | bytes 2211848 | tf_op jit(solution)/shard_map/ppermute | solution.py:210
  148.7 18.1 %collective-permute-start.12 = (bf16[3,160,768]{2,1,0:T(8,128)(2,1)S(1)}, bf16[3,160,768]{2,1,0:T(8,128)(2,1)S(1)}, u32[]{:S(2)}, u32[]{:S(2)}) collective-permute-start(bf16[3,160,768]{2,1,0:T(8,128)(2,1)S(1)} %collective-permute-done.9.refs_3_), channel_id=1, source_target_pairs={{0,8},{1,9},{2,10},{3,11},{16,24},{17,25},{18,26},{19,27}} | collective-permute-start | bytes 2211848 | tf_op jit(solution)/shard_map/ppermute | solution.py:210
  159.0 9.2 %collective-permute-start.11 = (bf16[3,160,768]{2,1,0:T(8,128)(2,1)S(1)}, bf16[3,160,768]{2,1,0:T(8,128)(2,1)S(1)}, u32[]{:S(2)}, u32[]{:S(2)}) collective-permute-start(bf16[3,160,768]{2,1,0:T(8,128)(2,1)S(1)} %broadcast_select_fusion.1), channel_id=1, source_target_pairs={{0,4},{8,12},{1,5},{9,13},{2,6},{10,14},{3,7},{11,15},{16,20},{24,... | collective-permute-start | bytes 2211848 | tf_op jit(solution)/shard_map/ppermute | solution.py:213
  166.9 3.1 %collective-permute-start.13 = (bf16[3,160,768]{2,1,0:T(8,128)(2,1)S(1)}, bf16[3,160,768]{2,1,0:T(8,128)(2,1)S(1)}, u32[]{:S(2)}, u32[]{:S(2)}) collective-permute-start(bf16[3,160,768]{2,1,0:T(8,128)(2,1)S(1)} %broadcast_select_fusion), channel_id=1, source_target_pairs={{0,4},{8,12},{1,5},{9,13},{2,6},{10,14},{3,7},{11,15},{16,20},{24,... | collective-permute-start | bytes 2211848 | tf_op jit(solution)/shard_map/ppermute | solution.py:213
  194.4 15.5 %copy-start.1 = (s32[12]{0:T(128)S(1)}, s32[12]{0:T(128)}, u32[]{:S(2)}) copy-start(s32[12]{0:T(128)} %param.13) | copy-start | bytes 148

commit v2 on v1

v2 whole, which is shorter than its diff:
```python
import math

import jax
import jax.numpy as jnp
import numpy as np
from jax import lax
from jax.experimental import pallas as pl
from jax.experimental.pallas import tpu as pltpu
from jax.sharding import PartitionSpec as P

STEPS = 2
POLAR = 6
HALO = 3
TAPS = 7
GROUP = 16
LANES = 128
CHUNK = 16
BIAS_ROWS = 16

gelu_scale = 0.7978845608028654
gelu_cubic = 0.044715
epsilon = 1e-05

f32 = jnp.float32
bf16 = jnp.bfloat16


def fourier(width):
    index = np.arange(width, dtype=np.int32)
    wavenumber = np.where(index <= width // 2, index, index - width // 2).astype(np.int32)
    phase = index[:, None] * wavenumber[None, :] % width
    angle = phase.astype(np.float64) * (2.0 * math.pi / width)
    factor = np.where((index == 0) | (index == width // 2), 1.0 / math.sqrt(width), math.sqrt(2.0 / width))
    table = np.where(index[None, :] <= width // 2, np.cos(angle), np.sin(angle)) * factor[None, :]
    return table.astype(np.float32).astype(bf16), wavenumber


def unroll(count, most):
    return max(u for u in range(1, most + 1) if count % u == 0)


def prepare_kernel(kernel, gain, offset, taps, gain_out, offset_out):
    rows, _, channels, depth = taps.shape
    lane = lax.broadcasted_iota(jnp.int32, (channels, depth), 1)
    here = lax.broadcasted_iota(jnp.int32, (channels, depth), 0)
    own = lane % GROUP == here % GROUP
    for j in range(TAPS):
        columns = [jnp.broadcast_to(kernel[j, :, i : i + 1], (channels, depth)) for i in range(TAPS)]
        for r in range(rows):
            total = jnp.zeros((channels, depth), f32)
            for i in range(TAPS):
                total = jnp.where(own & (lane // GROUP == r + i), columns[i], total)
            taps[r, j] = total.astype(bf16)
    gain_out[...] = jnp.broadcast_to(gain[...], gain_out.shape)
    offset_out[...] = jnp.broadcast_to(offset[...], offset_out.shape)


def convolve(up, own, down, taps, out):
    rows, channels, width = out.shape

    def group(b, _):
        at = pl.ds(pl.multiple_of(b * GROUP, GROUP), GROUP)
        field = jnp.concatenate([up[:, at, :], own[:, at, :], down[:, at, :]], axis=0)
        field = field.reshape((rows + 2 * HALO) * GROUP, width)
        parts = jnp.dot(taps[:, :, at, :].reshape(rows * TAPS * GROUP, field.shape[0]), field, preferred_element_type=f32)
        for r in range(rows):
            part = [parts[(r * TAPS + j) * GROUP : (r * TAPS + j + 1) * GROUP] for j in range(TAPS)]
            total = part[HALO]
            for j in range(TAPS):
                if j != HALO:
                    total = total + pltpu.roll(part[j], (HALO - j) % width, 1)
            out[r, at, :] = total
        return 0

    groups = channels // GROUP
    lax.fori_loop(0, groups, group, 0, unroll=unroll(groups, 5))


def add_bias_rows(normed, channels):
    width = normed.shape[1]
    row = lax.broadcasted_iota(jnp.int32, (BIAS_ROWS, width), 0)
    normed[channels:, :] = jnp.where(row < 3, 1.0, 0.0).astype(bf16)


def polar_filter(raw, keep, polar, table, out, select):
    rows, channels, width = out.shape
    spectrum = jnp.dot(raw[...], table[...], preferred_element_type=f32)
    parts = [(spectrum[r * channels : (r + 1) * channels] * keep[r : r + 1, :]).astype(bf16) for r in range(rows)]
    back = lax.dot_general(
        jnp.concatenate(parts, axis=0), table[...], (((1,), (1,)), ((), ())), preferred_element_type=f32
    ).astype(bf16)
    for r in range(rows):
        row = back[r * channels : (r + 1) * channels]
        if select:
            row = jnp.where(polar[r] > 0, row, raw[r * channels : (r + 1) * channels, :])
        out[r] = row


def control_kernel(
    select, advance_all, polar, up, own, down, taps, gain, bias, w_in, w_out, land, keep, table,
    out, unit_out, scale_out, slope_out, conv, normed, hidden, act, raw,
):
    rows, channels, width = out.shape
    hid = w_in.shape[0]
    add_bias_rows(normed, channels)
    convolve(up, own, down, taps, conv)
    for r in range(rows):
        for w in range(0, width, LANES):
            at = slice(w, w + LANES)
            value = conv[r, :, at]
            centered = value - jnp.mean(value, axis=0, keepdims=True)
            scale = lax.rsqrt(jnp.mean(centered * centered, axis=0, keepdims=True) + epsilon)
            unit = centered * scale
            unit_out[r, :, at] = unit
            scale_out[r, :, at] = scale
            normed[:channels, at] = (unit * gain[...] + bias[...]).astype(bf16)
        hidden[...] = jnp.dot(w_in[...], normed[...], preferred_element_type=f32)

        def pair(c, _):
            at = pl.ds(pl.multiple_of(c * CHUNK, CHUNK), CHUNK)
            h = hidden[at, :]
            square = h * h
            t = jnp.tanh(h * (gelu_scale + (gelu_scale * gelu_cubic) * square))
            half = 0.5 + 0.5 * t
            act[at, :] = (h * half).astype(bf16)
            lean = h * (2.0 * gelu_scale + (6.0 * gelu_scale * gelu_cubic) * square)
            slope_out[r, at, :] = half * (1.0 + (1.0 - half) * lean)
            return 0

        lax.fori_loop(0, hid // CHUNK, pair, 0, unroll=unroll(hid // CHUNK, 5))
        update = jnp.dot(w_out[...], act[...], preferred_element_type=f32)
        raw[r * channels : (r + 1) * channels, :] = (land[r : r + 1, :] * (own[r].astype(f32) + update)).astype(bf16)
    polar_filter(raw, keep, polar, table, out, select)


def tangent_kernel(
    select, polar, up, own, down, taps, gain, w_in, w_out, land, keep, table, unit_in, scale_in, slope_in, advanced,
    out, conv, normed, hidden, act, raw,
):
    rows, channels, width = out.shape
    hid = w_in.shape[0]
    is_control = polar[rows] > 0

    @pl.when(is_control)
    def _():
        out[...] = advanced[...]

    @pl.when(jnp.logical_not(is_control))
    def _():
        convolve(up, own, down, taps, conv)
        for r in range(rows):
            for w in range(0, width, LANES):
                at = slice(w, w + LANES)
                value = conv[r, :, at]
                unit = unit_in[r, :, at]
                average = jnp.mean(value, axis=0, keepdims=True)
                along = jnp.mean(value * unit, axis=0, keepdims=True)
                normed[:channels, at] = (gain[...] * scale_in[r, :, at] * (value - average - unit * along)).astype(bf16)
            hidden[...] = jnp.dot(w_in[:, :channels], normed[:channels, :], preferred_element_type=f32)

            def mix(c, _):
                at = pl.ds(pl.multiple_of(c * CHUNK, CHUNK), CHUNK)
                act[at, :] = (slope_in[r, at, :] * hidden[at, :]).astype(bf16)
                return 0

            lax.fori_loop(0, hid // CHUNK, mix, 0, unroll=unroll(hid // CHUNK, 5))
            update = jnp.dot(w_out[...], act[...], preferred_element_type=f32)
            raw[r * channels : (r + 1) * channels, :] = (
                land[r : r + 1, :] * (own[r].astype(f32) + update)
            ).astype(bf16)
        polar_filter(raw, keep, polar, table, out, select)


def scratch(rows, channels, width, hid):
    return [
        pltpu.VMEM((rows, channels, width), f32),
        pltpu.VMEM((channels + BIAS_ROWS, width), bf16),
        pltpu.VMEM((hid, width), f32),
        pltpu.VMEM((hid, width), bf16),
        pltpu.VMEM((rows * channels, width), bf16),
    ]


SMEM = pl.BlockSpec(memory_space=pltpu.SMEM)
VMEM = pl.BlockSpec(memory_space=pltpu.VMEM)
LIMIT = 24 << 20


def per_device(
    states, land_mask, cutoff, kernel, norm_gain, norm_bias, weight_in, bias_in, weight_out
):
    member = states[0]
    rows, channels, width = member.shape
    hid = weight_in.shape[1]
    bands = lax.axis_size("lat")
    members = lax.axis_size("mem")
    total_rows = rows * bands
    me = lax.axis_index("mem")
    select = total_rows > 2 * POLAR
    field = jax.ShapeDtypeStruct((rows, channels, width), bf16)
    params = pltpu.CompilerParams(vmem_limit_bytes=LIMIT)

    def send(block, pairs):
        return lax.ppermute(block, ("mem", "lat"), [(a * bands + i, b * bands + j) for (a, i), (b, j) in pairs])

    def exchange(block, which):
        forward = [((m, z), (m, z + 1)) for m in which for z in range(bands - 1)]
        return send(block, forward), send(block, [(b, a) for a, b in forward])

    def across(block, pairs):
        return send(block, [((a, z), (b, z)) for a, b in pairs for z in range(bands)])

    evens = list(range(0, members, 2))
    partners = [(m, m + 1) for m in evens if m + 1 < members]
    odd = me % 2 == 1

    up, down = exchange(member, range(members))
    control = member
    count = 2
    while count < members:
        sent = across(control, [(m, m + count) for m in range(0, count, 2) if m + count < members])
        control = jnp.where((me >= count) & (me < 2 * count), sent, control)
        count *= 2
    control_up, control_down = exchange(control, evens[1:])
    control_up = jnp.where(me == 0, up, control_up)
    control_down = jnp.where(me == 0, down, control_down)
    control = jnp.where(odd, across(control, partners), control)

    table, wavenumber = fourier(width)
    table = jnp.asarray(table)
    row = lax.axis_index("lat") * rows + jnp.arange(rows)
    is_polar = (row < POLAR) | (row >= total_rows - POLAR)
    place = jnp.clip(jnp.where(row < POLAR, row, row - total_rows + 2 * POLAR), 0, 2 * POLAR - 1)
    keep = (jnp.asarray(wavenumber)[None, :] <= cutoff[place][:, None]).astype(f32)
    flags = jnp.concatenate([is_polar.astype(jnp.int32), (me == 0).astype(jnp.int32)[None]])
    land = land_mask.astype(f32)
    high = lax.reduce_precision(bias_in, 8, 7)
    middle = lax.reduce_precision(bias_in - high, 8, 7)
    low = bias_in - high - middle
    bias_rows = jnp.pad(jnp.stack([high, middle, low]), ((0, BIAS_ROWS - 3), (0, 0))).astype(bf16)
    w_in = jnp.concatenate([weight_in, bias_rows], axis=0).T
    w_out = weight_out.T
    taps, gain, offset = pl.pallas_call(
        prepare_kernel,
        out_shape=(
            jax.ShapeDtypeStruct((rows, TAPS, channels, (rows + 2 * HALO) * GROUP), bf16),
            jax.ShapeDtypeStruct((channels, LANES), f32),
            jax.ShapeDtypeStruct((channels, LANES), f32),
        ),
        in_specs=[VMEM] * 3,
        out_specs=(VMEM,) * 3,
        compiler_params=params,
        name="prepare",
    )(kernel.transpose(1, 2, 0), norm_gain[:, None], norm_bias[:, None])

    def control_step(up, own, down):
        return pl.pallas_call(
            lambda *refs: control_kernel(select, True, *refs),
            out_shape=(
                field,
                jax.ShapeDtypeStruct((rows, channels, width), f32),
                jax.ShapeDtypeStruct((rows, 1, width), f32),
                jax.ShapeDtypeStruct((rows, hid, width), f32),
            ),
            in_specs=[SMEM] + [VMEM] * 11,
            out_specs=(VMEM,) * 4,
            scratch_shapes=scratch(rows, channels, width, hid),
            compiler_params=params,
            name="control",
        )(flags, up, own, down, taps, gain, offset, w_in, w_out, land, keep, table)

    def tangent_step(up, own, down, unit, scale, slope, advanced):
        return pl.pallas_call(
            lambda *refs: tangent_kernel(select, *refs),
            out_shape=field,
            in_specs=[SMEM] + [VMEM] * 14,
            out_specs=VMEM,
            scratch_shapes=scratch(rows, channels, width, hid),
            compiler_params=params,
            name="tangent",
        )(flags, up, own, down, taps, gain, w_in, w_out, land, keep, table, unit, scale, slope, advanced)

    for step in range(STEPS):
        if step > 0:
            up, down = exchange(member, range(1, members))
            control_up, control_down, _ = lax.optimization_barrier((control_up, control_down, member))
        control_up = jnp.where(odd, across(control_up, partners), control_up)
        control_down = jnp.where(odd, across(control_down, partners), control_down)
        control, unit, scale, slope = control_step(control_up, control, control_down)
        if step + 1 < STEPS:
            control_up, control_down = exchange(control, evens)
        member = tangent_step(up, member, down, unit, scale, slope, control)
    return member[None]


def solution(mesh):
    in_specs = (
        P(("runs", "mem"), "lat", None, None),
        P("lat", None),
        P(),
        P(),
        P(),
        P(),
        P(),
        P(),
        P(),
    )
    out_specs = P(("runs", "mem"), "lat", None, None)
    return jax.shard_map(
        per_device, mesh=mesh, in_specs=in_specs, out_specs=out_specs, check_vma=False
    )
```

time: 212 us -> 93.9 us (0.44)
  local copies, waits for them, and re-layouts: 51.3 us -> 1.54 us
  Pallas kernels: 78.8 us -> 40.3 us
  waiting for transfers between devices: 47 us -> 15 us
  starting transfers between devices: 25.1 us -> 31.6 us
  other arithmetic: 7.24 us -> 4.42 us
    mul x6 -> x0, local copies, waits for them, and re-layouts: 47.2 us -> none  [tap_matrix(): full = both[..., None] * eye[:, None, None, :]]
    ppermute x14, waiting for transfers between devices: 47 us -> 15 us  [send(): lax.ppermute(block, ('mem', 'lat'), [(a * bands + i, b * bands + j) for (...]
    pallas_call x2 -> x3, Pallas kernels: 48.6 us -> 22.7 us  [the longest x2 21.5 us: control_step(): pl.pallas_call(lambda *refs: control_kernel(select, True, *refs), out_sha...]
    pallas_call x2, Pallas kernels: 30.2 us -> 17.6 us  [tangent_step(): pl.pallas_call(lambda *refs: tangent_kernel(select, *refs), out_shape=fie...]
    ppermute x14, starting transfers between devices: 25.1 us -> 31.6 us  [send(): lax.ppermute(block, ('mem', 'lat'), [(a * bands + i, b * bands + j) for (...]
    mul x1 -> x0, other arithmetic: 3.54 us -> none  [tap_matrix(): full = both[..., None] * eye[:, None, None, :]]
    select_n x10 -> x8, other arithmetic: 1.98 us -> 4.1 us  [the longest x1 1.24 us: per_device(): control = jnp.where((me >= count) & (me < 2 * count), sent, control)]
  transfers between devices with their start and end apart: 14 -> 14, of which waited for: 8 -> 5; matrix products, arithmetic and copies ran while one was open for 27% -> 6% of each run, Pallas kernels for 0% -> 22%
where the time goes in v2:
time: 93.9 us; the launch traced here: 93.3 us
  Pallas kernels  40.3 us (43%)
  starting transfers between devices  31.6 us (34%)
  waiting for transfers between devices  15 us (16%)
  other arithmetic  4.42 us (5%)
  local copies, waits for them, and re-layouts  1.54 us (2%)
    ppermute x14, starting transfers between devices, send(): lax.ppermute(block, ('mem', 'lat'), [(a * bands + i, b * bands + j) for (...  31.6 us
    pallas_call x2, Pallas kernels, control_step(): pl.pallas_call(lambda *refs: control_kernel(select, True, *refs), out_sha...  21.5 us
    pallas_call x2, Pallas kernels, tangent_step(): pl.pallas_call(lambda *refs: tangent_kernel(select, *refs), out_shape=fie...  17.6 us
    ppermute x14, waiting for transfers between devices, send(): lax.ppermute(block, ('mem', 'lat'), [(a * bands + i, b * bands + j) for (...  15 us
  transfers between devices with their start and end apart: 14, of which 5 were waited for; matrix products, arithmetic and copies ran while one was open for 6% of the time, Pallas kernels for 22%

profile of v2, /device:TPU:10, one launch (start us, length us, event | category | flops | bytes accessed | tf_op | source)
XLA Modules:
  0.0 93.3 jit_solution(580953280452230294)
XLA Ops:
  0.0 0.0 copy-start
  0.0 0.0 copy-start.5
  0.0 1.4 %collective-permute-start.2 = (bf16[3,160,768]{2,1,0:T(8,128)(2,1)}, bf16[3,160,768]{2,1,0:T(8,128)(2,1)S(1)}, u32[]{:S(2)}, u32[]{:S(2)}) collective-permute-start(bf16[3,160,768]{2,1,0:T(8,128)(2,1)} %bitcast.16), channel_id=1, source_target_pairs={{0,8},{1,9},{2,10},{3,11},{16,24},{17,25},{18,26},{19,27}} | collective-permute-start | bytes 2211848 | tf_op jit(solution)/shard_map/ppermute | solution.py:204
  1.5 2.4 %collective-permute-start.1 = (bf16[3,160,768]{2,1,0:T(8,128)(2,1)}, bf16[3,160,768]{2,1,0:T(8,128)(2,1)S(1)}, u32[]{:S(2)}, u32[]{:S(2)}) collective-permute-start(bf16[3,160,768]{2,1,0:T(8,128)(2,1)} %bitcast.17), channel_id=1, source_target_pairs={{1,0},{2,1},{3,2},{5,4},{6,5},{7,6},{9,8},{10,9},{11,10},{13,12},{... | collective-permute-start | bytes 2211848 | tf_op jit(solution)/shard_map/ppermute | solution.py:204
  3.8 3.5 %collective-permute-start = (bf16[3,160,768]{2,1,0:T(8,128)(2,1)}, bf16[3,160,768]{2,1,0:T(8,128)(2,1)S(1)}, u32[]{:S(2)}, u32[]{:S(2)}) collective-permute-start(bf16[3,160,768]{2,1,0:T(8,128)(2,1)} %bitcast.18), channel_id=1, source_target_pairs={{0,1},{1,2},{2,3},{4,5},{5,6},{6,7},{8,9},{9,10},{10,11},{12,13},{... | collective-permute-start | bytes 2211848 | tf_op jit(solution)/shard_map/ppermute | solution.py:204
  7.3 0.0 copy-start.9
  7.3 0.0 copy-start.10
  7.3 0.0 copy-start.6
  7.4 6.4 %collective-permute-done.2 = bf16[3,160,768]{2,1,0:T(8,128)(2,1)S(1)} collective-permute-done((bf16[3,160,768]{2,1,0:T(8,128)(2,1)}, bf16[3,160,768]{2,1,0:T(8,128)(2,1)S(1)}, u32[]{:S(2)}, u32[]{:S(2)}) %collective-permute-start.2) | collective-permute-done | bytes 737312 | tf_op jit(solution)/shard_map/ppermute | solution.py:204
  13.7 1.2 %broadcast_select_fusion = bf16[3,160,768]{2,1,0:T(8,128)(2,1)S(1)} fusion(bf16[3,160,768]{2,1,0:T(8,128)(2,1)S(1)} %collective-permute-done.2, pred[]{:T(512)S(6)} %and.11, bf16[1,3,160,768]{3,2,1,0:T(8,128)(2,1)} %param.11), kind=kLoop, calls=%fused_computation.1 | loop fusion | flops 368640 | bytes 2211841 | tf_op jit(solution)/shard_map/jit(_where)/select_n | solution.py:222
  15.0 2.4 %collective-permute-start.6 = (bf16[3,160,768]{2,1,0:T(8,128)(2,1)S(1)}, bf16[3,160,768]{2,1,0:T(8,128)(2,1)}, u32[]{:S(2)}, u32[]{:S(2)}) collective-permute-start(bf16[3,160,768]{2,1,0:T(8,128)(2,1)S(1)} %broadcast_select_fusion), channel_id=1, source_target_pairs={{9,8},{10,9},{11,10},{25,24},{26,25},{27,26}} | collective-permute-start | bytes 2211848 | tf_op jit(solution)/shard_map/ppermute | solution.py:204
  17.3 0.0 copy-done.7
  17.4 0.2 copy.24
  17.6 0.0 copy-done.4
  17.6 0.2 copy.25
  17.8 0.0 copy-done.5
  17.8 0.2 copy.21
  18.1 0.0 copy-done.9
  18.1 0.1 copy.22.gain
  18.2 3.5 %collective-permute-start.3 = (bf16[3,160,768]{2,1,0:T(8,128)(2,1)S(1)}, bf16[3,160,768]{2,1,0:T(8,128)(2,1)}, u32[]{:S(2)}, u32[]{:S(2)}) collective-permute-start(bf16[3,160,768]{2,1,0:T(8,128)(2,1)S(1)} %broadcast_select_fusion), channel_id=1, source_target_pairs={{8,9},{9,10},{10,11},{24,25},{25,26},{26,27}} | collective-permute-start | bytes 2211848 | tf_op jit(solution)/shard_map/ppermute | solution.py:204
  21.7 0.0 copy-done.10
  21.7 0.1 copy.23.offset
  21.9 0.6 gather_fusion
  22.5 1.3 %prepare.1 = (bf16[3,7,160,144]{3,2,1,0:T(8,128)(2,1)S(1)}, f32[160,128]{1,0:T(8,128)S(1)}, f32[160,128]{1,0:T(8,128)S(1)}) custom-call(f32[7,160,7]{2,1,0:T(8,128)S(1)} %bitcast.20, f32[160,1]{1,0:T(8,128)S(1)} %copy.22.gain, f32[160,1]{1,0:T(8,128)S(1)} %copy.23.offset), custom_call_target="tpu_custom_call" | custom-call | tf_op jit(solution)/shard_map/prepare/pallas_call | solution.py:243
  23.8 0.1 add_convert_fusion.refs_0_
  23.9 0.1 fusion.2.refs_7_.refs_6_
  24.0 0.0 copy-start.8
  24.0 1.3 %collective-permute-start.5 = (bf16[3,160,768]{2,1,0:T(8,128)(2,1)S(1)}, bf16[3,160,768]{2,1,0:T(8,128)(2,1)S(1)}, u32[]{:S(2)}, u32[]{:S(2)}) collective-permute-start(bf16[3,160,768]{2,1,0:T(8,128)(2,1)S(1)} %broadcast_select_fusion), channel_id=1, source_target_pairs={{0,4},{1,5},{2,6},{3,7},{8,12},{9,13},{10,14},{11,15},{16,20},{17,... | collective-permute-start | bytes 2211848 | tf_op jit(solution)/shard_map/ppermute | solution.py:204
  25.4 0.0 collective-permute-done.1.refs_3_
  25.4 3.8 %collective-permute-done.6 = bf16[3,160,768]{2,1,0:T(8,128)(2,1)} collective-permute-done((bf16[3,160,768]{2,1,0:T(8,128)(2,1)S(1)}, bf16[3,160,768]{2,1,0:T(8,128)(2,1)}, u32[]{:S(2)}, u32[]{:S(2)}) %collective-permute-start.6) | collective-permute-done | bytes 737312 | tf_op jit(solution)/shard_map/ppermute | solution.py:204
  29.2 1.2 %broadcast_select_fusion.1 = bf16[3,160,768]{2,1,0:T(8,128)(2,1)S(1)} fusion(bf16[3,160,768]{2,1,0:T(8,128)(2,1)S(1)} %collective-permute-done.1.refs_3_, bf16[3,160,768]{2,1,0:T(8,128)(2,1)} %collective-permute-done.6, pred[]{:T(512)} %eq.10), kind=kLoop, calls=%fused_computation.2 | loop fusion | flops 368640 | bytes 2211841 | tf_op jit(solution)/shard_map/jit(_where)/select_n | solution.py:226
  30.4 1.3 %collective-permute-start.7 = (bf16[3,160,768]{2,1,0:T(8,128)(2,1)S(1)}, bf16[3,160,768]{2,1,0:T(8,128)(2,1)S(1)}, u32[]{:S(2)}, u32[]{:S(2)}) collective-permute-start(bf16[3,160,768]{2,1,0:T(8,128)(2,1)S(1)} %broadcast_select_fusion.1), channel_id=1, source_target_pairs={{0,4},{1,5},{2,6},{3,7},{8,12},{9,13},{10,14},{11,15},{16,20},{17,... | collective-permute-start | bytes 2211848 | tf_op jit(solution)/shard_map/ppermute | solution.py:204
  31.8 0.0 collective-permute-done.refs_1_
  31.8 0.0 collective-permute-done.3
  31.8 1.2 %broadcast_select_fusion.2 = bf16[3,160,768]{2,1,0:T(8,128)(2,1)S(1)} fusion(bf16[3,160,768]{2,1,0:T(8,128)(2,1)S(1)} %collective-permute-done.refs_1_, bf16[3,160,768]{2,1,0:T(8,128)(2,1)} %collective-permute-done.3, pred[]{:T(512)} %eq.10), kind=kLoop, calls=%fused_computation.3 | loop fusion | flops 368640 | bytes 2211841 | tf_op jit(solution)/shard_map/jit(_where)/select_n | solution.py:225
  33.0 1.3 %collective-permute-start.4 = (bf16[3,160,768]{2,1,0:T(8,128)(2,1)S(1)}, bf16[3,160,768]{2,1,0:T(8,128)(2,1)S(1)}, u32[]{:S(2)}, u32[]{:S(2)}) collective-permute-start(bf16[3,160,768]{2,1,0:T(8,128)(2,1)S(1)} %broadcast_select_fusion.2), channel_id=1, source_target_pairs={{0,4},{1,5},{2,6},{3,7},{8,12},{9,13},{10,14},{11,15},{16,20},{17,... | collective-permute-start | bytes 2211848 | tf_op jit(solution)/shard_map/ppermute | solution.py:204
  34.4 0.1 compare_convert_fusion.refs_10_.refs_9_
  34.4 0.0 collective-permute-done.5
  34.4 0.1 broadcast_select_fusion.6.refs_2_
  34.5 0.0 copy-start.1
  34.5 0.0 copy-start.2
  34.5 0.0 collective-permute-done.7
  34.5 0.1 broadcast_select_fusion.5.refs_3_
  34.6 1.5 %collective-permute-done.4 = bf16[3,160,768]{2,1,0:T(8,128)(2,1)S(1)} collective-permute-done((bf16[3,160,768]{2,1,0:T(8,128)(2,1)S(1)}, bf16[3,160,768]{2,1,0:T(8,128)(2,1)S(1)}, u32[]{:S(2)}, u32[]{:S(2)}) %collective-permute-start.4) | collective-permute-done | bytes 737312 | tf_op jit(solution)/shard_map/ppermute | solution.py:204
  36.1 0.1 broadcast_select_fusion.7.refs_1_
  36.2 0.0 copy-start.3
  36.2 10.7 %control.2 = (bf16[3,160,768]{2,1,0:T(8,128)(2,1)S(1)}, f32[3,160,768]{2,1,0:T(8,128)S(1)}, f32[3,1,768]{2,1,0:T(1,128)S(1)}, f32[3,640,768]{2,1,0:T(8,128)S(1)}) custom-call(s32[4]{0:T(128)S(1)} %add_convert_fusion.refs_0_, bf16[3,160,768]{2,1,0:T(8,128)(2,1)S(1)} %broadcast_select_fusion.7.refs_1_, ...), custom_call_target="tpu_custom_call" | custom-call | tf_op jit(solution)/shard_map/control/pallas_call | solution.py:257
  47.0 3.5 %collective-permute-start.10 = (bf16[3,160,768]{2,1,0:T(8,128)(2,1)S(1)}, bf16[3,160,768]{2,1,0:T(8,128)(2,1)S(1)}, u32[]{:S(2)}, u32[]{:S(2)}) collective-permute-start(bf16[3,160,768]{2,1,0:T(8,128)(2,1)S(1)} %get-tuple-element.24.refs_14_.refs_2_), channel_id=1, source_target_pairs={{0,1},{1,2},{2,3},{8,9},{9,10},{10,11},{16,17},{17,18},{18,19},{24... | collective-permute-start | bytes 2211848 | tf_op jit(solution)/shard_map/ppermute | solution.py:204
  50.5 2.4 %collective-permute-start.11 = (bf16[3,160,768]{2,1,0:T(8,128)(2,1)S(1)}, bf16[3,160,768]{2,1,0:T(8,128)(2,1)S(1)}, u32[]{:S(2)}, u32[]{:S(2)}) collective-permute-start(bf16[3,160,768]{2,1,0:T(8,128)(2,1)S(1)} %get-tuple-element.24.refs_14_.refs_2_), channel_id=1, source_target_pairs={{1,0},{2,1},{3,2},{9,8},{10,9},{11,10},{17,16},{18,17},{19,18},{25... | collective-permute-start | bytes 2211848 | tf_op jit(solution)/shard_map/ppermute | solution.py:204
  52.9 8.3 %tangent.2.refs_2_ = bf16[3,160,768]{2,1,0:T(8,128)(2,1)S(1)} custom-call(s32[4]{0:T(128)S(1)} %add_convert_fusion.refs_0_, bf16[3,160,768]{2,1,0:T(8,128)(2,1)S(1)} %collective-permute-done.refs_1_, bf16[3,160,768]{2,1,0:T(8,128)(2,1)S(1)} %bitcast.19, bf16[3,160,768]{2,1,0:T(8,128)(2,1)S(1)} %collective-permute-done.1.refs_3_, ...), custom_call_target="tpu_custom_call" | custom-call | tf_op jit(solution)/shard_map/tangent/pallas_call | solution.py:273
  61.2 0.0 collective-permute-done.10
  61.2 2.9 %collective-permute-done.11 = bf16[3,160,768]{2,1,0:T(8,128)(2,1)S(1)} collective-permute-done((bf16[3,160,768]{2,1,0:T(8,128)(2,1)S(1)}, bf16[3,160,768]{2,1,0:T(8,128)(2,1)S(1)}, u32[]{:S(2)}, u32[]{:S(2)}) %collective-permute-start.11) | collective-permute-done | bytes 737312 | tf_op jit(solution)/shard_map/ppermute | solution.py:204
  64.1 1.3 %collective-permute-start.13 = (bf16[3,160,768]{2,1,0:T(8,128)(2,1)S(1)}, bf16[3,160,768]{2,1,0:T(8,128)(2,1)S(1)}, u32[]{:S(2)}, u32[]{:S(2)}) collective-permute-start(bf16[3,160,768]{2,1,0:T(8,128)(2,1)S(1)} %collective-permute-done.11), channel_id=1, source_target_pairs={{0,4},{1,5},{2,6},{3,7},{8,12},{9,13},{10,14},{11,15},{16,20},{17,... | collective-permute-start | bytes 2211848 | tf_op jit(solution)/shard_map/ppermute | solution.py:204
  65.5 1.3 %collective-permute-start.12 = (bf16[3,160,768]{2,1,0:T(8,128)(2,1)S(1)}, bf16[3,160,768]{2,1,0:T(8,128)(2,1)S(1)}, u32[]{:S(2)}, u32[]{:S(2)}) collective-permute-start(bf16[3,160,768]{2,1,0:T(8,128)(2,1)S(1)} %collective-permute-done.10), channel_id=1, source_target_pairs={{0,4},{1,5},{2,6},{3,7},{8,12},{9,13},{10,14},{11,15},{16,20},{17,... | collective-permute-start | bytes 2211848 | tf_op jit(solution)/shard_map/ppermute | solution.py:204
  66.8 3.9 %collective-permute-start.8 = (bf16[3,160,768]{2,1,0:T(8,128)(2,1)S(1)}, bf16[3,160,768]{2,1,0:T(8,128)(2,1)S(1)}, u32[]{:S(2)}, u32[]{:S(2)}) collective-permute-start(bf16[3,160,768]{2,1,0:T(8,128)(2,1)S(1)} %tangent.2.refs_2_), channel_id=1, source_target_pairs={{4,5},{5,6},{6,7},{8,9},{9,10},{10,11},{12,13},{13,14},{14,15},{20... | collective-permute-start | bytes 2211848 | tf_op jit(solution)/shard_map/ppermute | solution.py:204
  70.7 2.0 %collective-permute-start.9 = (bf16[3,160,768]{2,1,0:T(8,128)(2,1)S(1)}, bf16[3,160,768]{2,1,0:T(8,128)(2,1)S(1)}, u32[]{:S(2)}, u32[]{:S(2)}) collective-permute-start(bf16[3,160,768]{2,1,0:T(8,128)(2,1)S(1)} %tangent.2.refs_2_), channel_id=1, source_target_pairs={{5,4},{6,5},{7,6},{9,8},{10,9},{11,10},{13,12},{14,13},{15,14},{21... | collective-permute-start | bytes 2211848 | tf_op jit(solution)/shard_map/ppermute | solution.py:204
  72.7 0.0 collective-permute-done.13
  72.7 0.1 broadcast_select_fusion.3.refs_3_
  72.8 0.0 collective-permute-done.12
  72.8 0.1 broadcast_select_fusion.4.refs_1_
  72.9 10.8 %control.3 = (bf16[3,160,768]{2,1,0:T(8,128)(2,1)S(1)}, f32[3,160,768]{2,1,0:T(8,128)S(1)}, f32[3,1,768]{2,1,0:T(1,128)S(1)}, f32[3,640,768]{2,1,0:T(8,128)S(1)}) custom-call(s32[4]{0:T(128)S(1)} %add_convert_fusion.refs_0_, bf16[3,160,768]{2,1,0:T(8,128)(2,1)S(1)} %broadcast_select_fusion.4.refs_1_, ...), custom_call_target="tpu_custom_call" | custom-call | tf_op jit(solution)/shard_map/control/pallas_call | solution.py:257
  83.7 0.0 collective-permute-done.8.refs_1_
  83.7 0.4 collective-permute-done.9.refs_3_
  84.1 9.2 %tangent.3 = bf16[3,160,768]{2,1,0:T(8,128)(2,1)} custom-call(s32[4]{0:T(128)S(1)} %add_convert_fusion.refs_0_, bf16[3,160,768]{2,1,0:T(8,128)(2,1)S(1)} %collective-permute-done.8.refs_1_, bf16[3,160,768]{2,1,0:T(8,128)(2,1)S(1)} %tangent.2.refs_2_, bf16[3,160,768]{2,1,0:T(8,128)(2,1)S(1)} %collective-permute-done.9.refs_3_, ...), custom_call_target="tpu_custom_call" | custom-call | tf_op jit(solution)/shard_map/tangent/pallas_call | solution.py:273
  (17 shorter events, 0.1 us)
Async XLA Ops:
  0.0 21.9 %copy-start = (s32[12]{0:T(128)S(1)}, s32[12]{0:T(128)}, u32[]{:S(2)}) copy-start(s32[12]{0:T(128)} %param.13) | copy-start | bytes 148
  0.0 17.3 %copy-start.7 = (f32[640]{0:T(1024)S(1)}, f32[640]{0:T(1024)}, u32[]{:S(2)}) copy-start(f32[640]{0:T(1024)} %param.18) | copy-start | bytes 7684
  0.0 17.6 %copy-start.4 = (bf16[160,640]{1,0:T(8,128)(2,1)S(1)}, bf16[160,640]{1,0:T(8,128)(2,1)}, u32[]{:S(2)}) copy-start(bf16[160,640]{1,0:T(8,128)(2,1)} %param.17) | copy-start | bytes 614404
  0.0 17.8 %copy-start.5 = (f32[7,7,160]{2,1,0:T(8,128)S(1)}, f32[7,7,160]{2,1,0:T(8,128)}, u32[]{:S(2)}) copy-start(f32[7,7,160]{2,1,0:T(8,128)} %param.14) | copy-start | bytes 94084
  0.0 13.7 %collective-permute-start.2 = (bf16[3,160,768]{2,1,0:T(8,128)(2,1)}, bf16[3,160,768]{2,1,0:T(8,128)(2,1)S(1)}, u32[]{:S(2)}, u32[]{:S(2)}) collective-permute-start(bf16[3,160,768]{2,1,0:T(8,128)(2,1)} %bitcast.16), channel_id=1, source_target_pairs={{0,8},{1,9},{2,10},{3,11},{16,24},{17,25},{18,26},{19,27}} | collective-permute-start | bytes 2211848 | tf_op jit(solution)/shard_map/ppermute | solution.py:204
  1.5 23.9 %collective-permute-start.1 = (bf16[3,160,768]{2,1,0:T(8,128)(2,1)}, bf16[3,160,768]{2,1,0:T(8,128)(2,1)S(1)}, u32[]{:S(2)}, u32[]{:S(2)}) collective-permute-start(bf16[3,160,768]{2,1,0:T(8,128)(2,1)} %bitcast.17), channel_id=1, source_target_pairs={{1,0},{2,1},{3,2},{5,4},{6,5},{7,6},{9,8},{10,9},{11,10},{13,12},{... | collective-permute-start | bytes 2211848 | tf_op jit(solution)/shard_map/ppermute | solution.py:204
  3.8 27.9 %collective-permute-start = (bf16[3,160,768]{2,1,0:T(8,128)(2,1)}, bf16[3,160,768]{2,1,0:T(8,128)(2,1)S(1)}, u32[]{:S(2)}, u32[]{:S(2)}) collective-permute-start(bf16[3,160,768]{2,1,0:T(8,128)(2,1)} %bitcast.18), channel_id=1, source_target_pairs={{0,1},{1,2},{2,3},{4,5},{5,6},{6,7},{8,9},{9,10},{10,11},{12,13},{... | collective-permute-start | bytes 2211848 | tf_op jit(solution)/shard_map/ppermute | solution.py:204
  7.3 10.8 %copy-start.9 = (f32[160]{0:T(256)S(1)}, f32[160]{0:T(256)}, u32[]{:S(2)}) copy-start(f32[160]{0:T(256)} %param.15) | copy-start | bytes 1924
  7.3 14.4 %copy-start.10 = (f32[160]{0:T(256)S(1)}, f32[160]{0:T(256)}, u32[]{:S(2)}) copy-start(f32[160]{0:T(256)} %param.16) | copy-start | bytes 1924
  7.3 14.5 %copy-start.6 = (s32[3,768]{1,0:T(4,128)S(1)}, s32[3,768]{1,0:T(4,128)}, u32[]{:S(2)}) copy-start(s32[3,768]{1,0:T(4,128)} %param.12) | copy-start | bytes 27652
  15.0 14.2 %collective-permute-start.6 = (bf16[3,160,768]{2,1,0:T(8,128)(2,1)S(1)}, bf16[3,160,768]{2,1,0:T(8,128)(2,1)}, u32[]{:S(2)}, u32[]{:S(2)}) collective-permute-start(bf16[3,160,768]{2,1,0:T(8,128)(2,1)S(1)} %broadcast_select_fusion), channel_id=1, source_target_pairs={{9,8},{10,9},{11,10},{25,24},{26,25},{27,26}} | collective-permute-start | bytes 2211848 | tf_op jit(solution)/shard_map/ppermute | solution.py:204
  18.2 13.6 %collective-permute-start.3 = (bf16[3,160,768]{2,1,0:T(8,128)(2,1)S(1)}, bf16[3,160,768]{2,1,0:T(8,128)(2,1)}, u32[]{:S(2)}, u32[]{:S(2)}) collective-permute-start(bf16[3,160,768]{2,1,0:T(8,128)(2,1)S(1)} %broadcast_select_fusion), channel_id=1, source_target_pairs={{8,9},{9,10},{10,11},{24,25},{25,26},{26,27}} | collective-permute-start | bytes 2211848 | tf_op jit(solution)/shard_map/ppermute | solution.py:204
  24.0 10.3 %copy-start.8 = (s32[768]{0:T(1024)S(1)}, s32[768]{0:T(1024)}, u32[]{:S(2)}) copy-start(s32[768]{0:T(1024)} %constant.43.clone) | copy-start | bytes 9220
  24.0 10.4 %collective-permute-start.5 = (bf16[3,160,768]{2,1,0:T(8,128)(2,1)S(1)}, bf16[3,160,768]{2,1,0:T(8,128)(2,1)S(1)}, u32[]{:S(2)}, u32[]{:S(2)}) collective-permute-start(bf16[3,160,768]{2,1,0:T(8,128)(2,1)S(1)} %broadcast_select_fusion), channel_id=1, source_target_pairs={{0,4},{1,5},{2,6},{3,7},{8,12},{9,13},{10,14},{11,15},{16,20},{17,... | collective-permute-start | bytes 2211848 | tf_op jit(solution)/shard_map/ppermute | solution.py:204
  30.4 4.1 %collective-permute-start.7 = (bf16[3,160,768]{2,1,0:T(8,128)(2,1)S(1)}, bf16[3,160,768]{2,1,0:T(8,128)(2,1)S(1)}, u32[]{:S(2)}, u32[]{:S(2)}) collective-permute-start(bf16[3,160,768]{2,1,0:T(8,128)(2,1)S(1)} %broadcast_select_fusion.1), channel_id=1, source_target_pairs={{0,4},{1,5},{2,6},{3,7},{8,12},{9,13},{10,14},{11,15},{16,20},{17,... | collective-permute-start | bytes 2211848 | tf_op jit(solution)/shard_map/ppermute | solution.py:204
  33.0 3.1 %collective-permute-start.4 = (bf16[3,160,768]{2,1,0:T(8,128)(2,1)S(1)}, bf16[3,160,768]{2,1,0:T(8,128)(2,1)S(1)}, u32[]{:S(2)}, u32[]{:S(2)}) collective-permute-start(bf16[3,160,768]{2,1,0:T(8,128)(2,1)S(1)} %broadcast_select_fusion.2), channel_id=1, source_target_pairs={{0,4},{1,5},{2,6},{3,7},{8,12},{9,13},{10,14},{11,15},{16,20},{17,... | collective-permute-start | bytes 2211848 | tf_op jit(solution)/shard_map/ppermute | solution.py:204
  34.5 1.7 %copy-start.1 = (bf16[768,768]{1,0:T(8,128)(2,1)S(1)}, bf16[768,768]{1,0:T(8,128)(2,1)}, u32[]{:S(2)}) copy-start(bf16[768,768]{1,0:T(8,128)(2,1)} %constant.42.clone.refs_11_.refs_10_) | copy-start | bytes 3538948
  34.5 1.7 %copy-start.2 = (bf16[640,160]{0,1:T(8,128)(2,1)S(1)}, bf16[640,160]{0,1:T(8,128)(2,1)}, u32[]{:S(2)}) copy-start(bf16[640,160]{0,1:T(8,128)(2,1)} %param.19) | copy-start | bytes 614404
  36.2 16.7 %copy-start.3 = (bf16[1,3,160,768]{3,2,1,0:T(8,128)(2,1)S(1)}, bf16[1,3,160,768]{3,2,1,0:T(8,128)(2,1)}, u32[]{:S(2)}) copy-start(bf16[1,3,160,768]{3,2,1,0:T(8,128)(2,1)} %param.11) | copy-start | bytes 2211844
  47.0 14.2 %collective-permute-start.10 = (bf16[3,160,768]{2,1,0:T(8,128)(2,1)S(1)}, bf16[3,160,768]{2,1,0:T(8,128)(2,1)S(1)}, u32[]{:S(2)}, u32[]{:S(2)}) collective-permute-start(bf16[3,160,768]{2,1,0:T(8,128)(2,1)S(1)} %get-tuple-element.24.refs_14_.refs_2_), channel_id=1, source_target_pairs={{0,1},{1,2},{2,3},{8,9},{9,10},{10,11},{16,17},{17,18},{18,19},{24... | collective-permute-start | bytes 2211848 | tf_op jit(solution)/shard_map/ppermute | solution.py:204
  50.5 13.7 %collective-permute-start.11 = (bf16[3,160,768]{2,1,0:T(8,128)(2,1)S(1)}, bf16[3,160,768]{2,1,0:T(8,128)(2,1)S(1)}, u32[]{:S(2)}, u32[]{:S(2)}) collective-permute-start(bf16[3,160,768]{2,1,0:T(8,128)(2,1)S(1)} %get-tuple-element.24.refs_14_.refs_2_), channel_id=1, source_target_pairs={{1,0},{2,1},{3,2},{9,8},{10,9},{11,10},{17,16},{18,17},{19,18},{25... | collective-permute-start | bytes 2211848 | tf_op jit(solution)/shard_map/ppermute | solution.py:204
  64.1 8.6 %collective-permute-start.13 = (bf16[3,160,768]{2,1,0:T(8,128)(2,1)S(1)}, bf16[3,160,768]{2,1,0:T(8,128)(2,1)S(1)}, u32[]{:S(2)}, u32[]{:S(2)}) collective-permute-start(bf16[3,160,768]{2,1,0:T(8,128)(2,1)S(1)} %collective-permute-done.11), channel_id=1, source_target_pairs={{0,4},{1,5},{2,6},{3,7},{8,12},{9,13},{10,14},{11,15},{16,20},{17,... | collective-permute-start | bytes 2211848 | tf_op jit(solution)/shard_map/ppermute | solution.py:204
  65.5 7.4 %collective-permute-start.12 = (bf16[3,160,768]{2,1,0:T(8,128)(2,1)S(1)}, bf16[3,160,768]{2,1,0:T(8,128)(2,1)S(1)}, u32[]{:S(2)}, u32[]{:S(2)}) collective-permute-start(bf16[3,160,768]{2,1,0:T(8,128)(2,1)S(1)} %collective-permute-done.10), channel_id=1, source_target_pairs={{0,4},{1,5},{2,6},{3,7},{8,12},{9,13},{10,14},{11,15},{16,20},{17,... | collective-permute-start | bytes 2211848 | tf_op jit(solution)/shard_map/ppermute | solution.py:204
  66.8 16.9 %collective-permute-start.8 = (bf16[3,160,768]{2,1,0:T(8,128)(2,1)S(1)}, bf16[3,160,768]{2,1,0:T(8,128)(2,1)S(1)}, u32[]{:S(2)}, u32[]{:S(2)}) collective-permute-start(bf16[3,160,768]{2,1,0:T(8,128)(2,1)S(1)} %tangent.2.refs_2_), channel_id=1, source_target_pairs={{4,5},{5,6},{6,7},{8,9},{9,10},{10,11},{12,13},{13,14},{14,15},{20... | collective-permute-start | bytes 2211848 | tf_op jit(solution)/shard_map/ppermute | solution.py:204
  70.7 13.4 %collective-permute-start.9 = (bf16[3,160,768]{2,1,0:T(8,128)(2,1)S(1)}, bf16[3,160,768]{2,1,0:T(8,128)(2,1)S(1)}, u32[]{:S(2)}, u32[]{:S(2)}) collective-permute-start(bf16[3,160,768]{2,1,0:T(8,128)(2,1)S(1)} %tangent.2.refs_2_), channel_id=1, source_target_pairs={{5,4},{6,5},{7,6},{9,8},{10,9},{11,10},{13,12},{14,13},{15,14},{21... | collective-permute-start | bytes 2211848 | tf_op jit(solution)/shard_map/ppermute | solution.py:204

commit v3 on v2

v3 whole, which is shorter than its diff:
```python
import math

import jax
import jax.numpy as jnp
import numpy as np
from jax import lax
from jax.experimental import pallas as pl
from jax.experimental.pallas import tpu as pltpu
from jax.sharding import PartitionSpec as P

STEPS = 2
POLAR = 6
HALO = 3
TAPS = 7
GROUP = 16
LANES = 256
CHUNK = 64
BIAS_ROWS = 16
SPARE = 8

gelu_scale = 0.7978845608028654
gelu_cubic = 0.044715
epsilon = 1e-05

f32 = jnp.float32
bf16 = jnp.bfloat16


def fourier(width):
    index = np.arange(width, dtype=np.int32)
    wavenumber = np.where(index <= width // 2, index, index - width // 2).astype(np.int32)
    phase = index[:, None] * wavenumber[None, :] % width
    angle = phase.astype(np.float64) * (2.0 * math.pi / width)
    factor = np.where((index == 0) | (index == width // 2), 1.0 / math.sqrt(width), math.sqrt(2.0 / width))
    table = np.where(index[None, :] <= width // 2, np.cos(angle), np.sin(angle)) * factor[None, :]
    return table.astype(np.float32).astype(bf16)


def unroll(count, most):
    return max(u for u in range(1, most + 1) if count % u == 0)


def prepare_kernel(*refs):
    sources, refs = refs[:6], refs[6:]
    taps, gain_out, offset_out, w_in, land = refs[:5]
    kernel, gain, offset, weight_in, bias, land_mask, arrived = refs[5:]
    copies = [
        pltpu.make_async_copy(source, here, arrived.at[i])
        for i, (source, here) in enumerate(zip(sources, (kernel, gain, offset, weight_in, bias, land_mask)))
    ]
    for copy in copies:
        copy.start()
    for copy in copies:
        copy.wait()
    rows, _, channels, depth = taps.shape
    band = lax.axis_index("lat")
    lane = lax.broadcasted_iota(jnp.int32, (channels, depth), 1)
    here = lax.broadcasted_iota(jnp.int32, (channels, depth), 0)
    block = lane // GROUP
    turned = jnp.where(block < HALO, block + rows + HALO, jnp.where(block < HALO + rows, block, block - rows - HALO))
    block = jnp.where(band % 2 == 1, block, turned)
    block = jnp.where(lane % GROUP == here % GROUP, block, -1)
    for j in range(TAPS):
        lines = [kernel[i, j : j + 1, :] for i in range(TAPS)] + [jnp.zeros((128 - TAPS, channels), f32)]
        turned = jnp.concatenate(lines, axis=0).T
        columns = [jnp.broadcast_to(turned[:, i : i + 1], (channels, depth)) for i in range(TAPS)]
        for r in range(rows):
            total = jnp.zeros((channels, depth), f32)
            for i in range(TAPS):
                total = jnp.where(block == r + i, columns[i], total)
            taps[r, j] = total.astype(bf16)
    gain_out[...] = jnp.broadcast_to(gain[...], (128, channels)).T
    offset_out[...] = jnp.broadcast_to(offset[...], (128, channels)).T
    w_in[:, :channels] = weight_in[...].astype(f32).T.astype(bf16)
    place = lax.broadcasted_iota(jnp.int32, (128, 128), 1)
    for k in range(bias.shape[0]):
        value = jnp.broadcast_to(bias[k : k + 1, :], (128, 128)).T
        high = value.astype(bf16).astype(f32)
        middle = (value - high).astype(bf16).astype(f32)
        low = value - high - middle
        three = jnp.where(place == 0, high, jnp.where(place == 1, middle, jnp.where(place == 2, low, 0.0)))
        w_in[k * 128 : (k + 1) * 128, channels:] = three[:, :BIAS_ROWS].astype(bf16)
    land[...] = land_mask[...].astype(f32)


def filter_kernel(bands, cutoff, table, out):
    rows, width, _ = out.shape
    band = lax.axis_index("lat")
    index = lax.broadcasted_iota(jnp.int32, (1, width), 1)
    wavenumber = jnp.where(index <= width // 2, index, index - width // 2)
    total_rows = rows * bands
    for r in range(rows):
        row = band * rows + r
        place = jnp.clip(jnp.where(row < POLAR, row, row - total_rows + 2 * POLAR), 0, 2 * POLAR - 1)
        kept = (table[...].astype(f32) * (wavenumber <= cutoff[place]).astype(f32)).astype(bf16)
        out[r] = lax.dot_general(
            kept, table[...], (((1,), (1,)), ((), ())), preferred_element_type=f32
        ).astype(bf16)
        if total_rows > 2 * POLAR:
            @pl.when((row >= POLAR) & (row < total_rows - POLAR))
            def _():
                across = lax.broadcasted_iota(jnp.int32, (width, width), 1)
                along = lax.broadcasted_iota(jnp.int32, (width, width), 0)
                out[r] = (across == along).astype(f32).astype(bf16)


def convolve(near, own, far, taps, out):
    rows, channels, width = out.shape

    def group(b, _):
        at = pl.ds(pl.multiple_of(b * GROUP, GROUP), GROUP)
        field = jnp.concatenate([near(at), own(at), far(at)], axis=0)
        field = field.reshape((rows + 2 * HALO) * GROUP, width)
        parts = jnp.dot(taps[:, :, at, :].reshape(rows * TAPS * GROUP, field.shape[0]), field, preferred_element_type=f32)
        for r in range(rows):
            part = [parts[(r * TAPS + j) * GROUP : (r * TAPS + j + 1) * GROUP] for j in range(TAPS)]
            total = part[HALO]
            for j in range(TAPS):
                if j != HALO:
                    total = total + pltpu.roll(part[j], (HALO - j) % width, 1)
            out[r, at, :] = total
        return 0

    groups = channels // GROUP
    lax.fori_loop(0, groups, group, 0, unroll=unroll(groups, 5))


def read(ref):
    return lambda at: ref[:, at, :]


def choose(second, first, other):
    if other is None:
        return read(first)
    return lambda at: jnp.where(second, other[:, at, :], first[:, at, :])


def pipeline(tiles, first, second, third):
    for i in range(tiles + 2):
        if i < tiles:
            first(i)
        if 1 <= i <= tiles:
            second(i - 1)
        if i >= 2:
            third(i - 2)


def add_bias_rows(normed, channels):
    row = lax.broadcasted_iota(jnp.int32, (BIAS_ROWS, normed.shape[1]), 0)
    normed[channels:, :] = jnp.where(row < 3, 1.0, 0.0).astype(bf16)


def polar_filter(raw, filters, out, r):
    channels = raw.shape[0] // filters.shape[0]
    out[r, :channels, :] = jnp.dot(
        raw[r * channels : (r + 1) * channels, :], filters[r], preferred_element_type=f32
    ).astype(bf16)


def control_kernel(swap, *refs):
    near, own, far = refs[:3]
    refs = refs[3:]
    if swap:
        other = [far, None, near]
    else:
        other, refs = refs[:3], refs[3:]
    (
        taps, gain, bias, w_in, w_out, land, filters,
        out, unit_out, scale_out, slope_out, conv, normed, normed_b, hidden, hidden_b, act, act_b, raw,
    ) = refs
    rows, channels, width = out.shape
    hid = w_in.shape[0]
    normed, hidden, act = (normed, normed_b), (hidden, hidden_b), (act, act_b)
    second = lax.axis_index("mem") % 2 == 1
    for block in normed:
        add_bias_rows(block, channels)
    convolve(*(choose(second, a, b) for a, b in zip((near, own, far), other)), taps, conv)
    across = width // LANES

    def place(i):
        return i // across, slice(i % across * LANES, (i % across + 1) * LANES)

    def first(i):
        r, at = place(i)
        for w in range(0, LANES, 128):
            here, there = slice(at.start + w, at.start + w + 128), slice(w, w + 128)
            value = conv[r, :, here]
            centered = value - jnp.mean(value, axis=0, keepdims=True)
            scale = lax.rsqrt(jnp.mean(centered * centered, axis=0, keepdims=True) + epsilon)
            unit = centered * scale
            unit_out[r, :, here] = unit
            scale_out[r, :, here] = scale
            normed[i % 2][:channels, there] = (unit * gain[...] + bias[...]).astype(bf16)
        hidden[i % 2][...] = jnp.dot(w_in[...], normed[i % 2][...], preferred_element_type=f32)

    def pair(i):
        r, at = place(i)
        for c in range(0, hid, CHUNK):
            h = hidden[i % 2][c : c + CHUNK, :]
            square = h * h
            t = jnp.tanh(h * (gelu_scale + (gelu_scale * gelu_cubic) * square))
            half = 0.5 + 0.5 * t
            act[i % 2][c : c + CHUNK, :] = (h * half).astype(bf16)
            lean = h * (2.0 * gelu_scale + (6.0 * gelu_scale * gelu_cubic) * square)
            slope_out[r, c : c + CHUNK, at] = half * (1.0 + (1.0 - half) * lean)

    def third(i):
        r, at = place(i)
        update = jnp.dot(w_out[...], act[i % 2][...], preferred_element_type=f32)
        field = own[r, :, at]
        if other[1] is not None:
            field = jnp.where(second, other[1][r, :, at], field)
        raw[r * channels : (r + 1) * channels, at] = (land[r : r + 1, at] * (field.astype(f32) + update)).astype(bf16)
        if i % across == across - 1:
            polar_filter(raw, filters, out, r)

    pipeline(rows * across, first, pair, third)


def conv_kernel(near, own, far, taps, out):
    convolve(read(near), read(own), read(far), taps, out)


def tangent_kernel(ready, *refs):
    if ready:
        own, conv = refs[:2]
        refs = refs[2:]
    else:
        near, own, far, taps = refs[:4]
        refs = refs[4:]
    gain, w_in, w_out, land, filters, unit_in, scale_in, slope_in, advanced, out = refs[:10]
    refs = refs[10:]
    if not ready:
        conv, refs = refs[0], refs[1:]
    normed, normed_b, hidden, hidden_b, act, act_b, raw = refs
    normed, hidden, act = (normed, normed_b), (hidden, hidden_b), (act, act_b)
    rows, channels, width = advanced.shape
    hid = w_in.shape[0]
    across = width // LANES
    is_control = lax.axis_index("mem") == 0

    def place(i):
        return i // across, slice(i % across * LANES, (i % across + 1) * LANES)

    def first(i):
        r, at = place(i)
        for w in range(0, LANES, 128):
            here, there = slice(at.start + w, at.start + w + 128), slice(w, w + 128)
            value = conv[r, :, here]
            unit = unit_in[r, :, here]
            average = jnp.mean(value, axis=0, keepdims=True)
            along = jnp.mean(value * unit, axis=0, keepdims=True)
            normed[i % 2][:, there] = (gain[...] * scale_in[r, :, here] * (value - average - unit * along)).astype(bf16)
        hidden[i % 2][...] = jnp.dot(w_in[:, :channels], normed[i % 2][...], preferred_element_type=f32)

    def mix(i):
        r, at = place(i)
        for c in range(0, hid, CHUNK):
            act[i % 2][c : c + CHUNK, :] = (slope_in[r, c : c + CHUNK, at] * hidden[i % 2][c : c + CHUNK, :]).astype(bf16)

    def third(i):
        r, at = place(i)
        update = jnp.dot(w_out[...], act[i % 2][...], preferred_element_type=f32)
        raw[r * channels : (r + 1) * channels, at] = (
            land[r : r + 1, at] * (own[r, :channels, at].astype(f32) + update)
        ).astype(bf16)
        if i % across == across - 1:
            polar_filter(raw, filters, out, r)

    if out.shape[1] > channels:
        out[:, channels:, :] = jnp.zeros((rows, out.shape[1] - channels, width), bf16)

    @pl.when(is_control)
    def _():
        out[:, :channels, :] = advanced[...]

    @pl.when(jnp.logical_not(is_control))
    def _():
        if not ready:
            convolve(read(near), read(own), read(far), taps, conv)
        pipeline(rows * across, first, mix, third)


def scratch(rows, channels, width, hid, bias_rows, conv=True):
    return ([pltpu.VMEM((rows, channels, width), f32)] if conv else []) + [
        pltpu.VMEM((channels + bias_rows, LANES), bf16),
        pltpu.VMEM((channels + bias_rows, LANES), bf16),
        pltpu.VMEM((hid, LANES), f32),
        pltpu.VMEM((hid, LANES), f32),
        pltpu.VMEM((hid, LANES), bf16),
        pltpu.VMEM((hid, LANES), bf16),
        pltpu.VMEM((rows * channels, width), bf16),
    ]


SMEM = pl.BlockSpec(memory_space=pltpu.SMEM)
VMEM = pl.BlockSpec(memory_space=pltpu.VMEM)
LIMIT = 24 << 20


def per_device(
    states, land_mask, cutoff, kernel, norm_gain, norm_bias, weight_in, bias_in, weight_out
):
    member = states[0]
    rows, channels, width = member.shape
    hid = weight_in.shape[1]
    bands = lax.axis_size("lat")
    members = lax.axis_size("mem")
    me = lax.axis_index("mem")
    params = pltpu.CompilerParams(vmem_limit_bytes=LIMIT)

    def shape(*dims, kind=f32):
        return jax.ShapeDtypeStruct(dims, kind)

    field = shape(rows, channels, width, kind=bf16)

    def send(block, pairs):
        return lax.ppermute(block, ("mem", "lat"), [(a * bands + i, b * bands + j) for (a, i), (b, j) in pairs])

    def neighbours(which, start):
        pairs = [((m, z), (m, z + 1)) for m in which for z in range(start, bands - 1, 2)]
        return pairs + [(b, a) for a, b in pairs]

    def exchange(block, which):
        far = send(block, neighbours(which, 1))
        return send(block, neighbours(which, 0)), far

    def across(block, pairs):
        return send(block, [((a, z), (b, z)) for a, b in pairs for z in range(bands)])

    evens = list(range(0, members, 2))
    odds = list(range(1, members, 2))
    partners = [(m - 1, m) for m in odds]
    swapped = partners + [(b, a) for a, b in partners]

    table = jnp.asarray(fourier(width))
    w_out = weight_out.T
    sources = (kernel, norm_gain[None], norm_bias[None], weight_in, bias_in.reshape(-1, 128), land_mask)
    taps, gain, offset, w_in, land = pl.pallas_call(
        prepare_kernel,
        out_shape=(
            shape(rows, TAPS, channels, (rows + 2 * HALO) * GROUP, kind=bf16),
            shape(channels, 128),
            shape(channels, 128),
            shape(hid, channels + BIAS_ROWS, kind=bf16),
            shape(rows, width),
        ),
        in_specs=[pl.BlockSpec(memory_space=pltpu.MemorySpace.HBM)] * 6,
        out_specs=(VMEM,) * 5,
        scratch_shapes=[pltpu.VMEM(x.shape, x.dtype) for x in sources] + [pltpu.SemaphoreType.DMA((6,))],
        compiler_params=params,
        name="prepare",
    )(*sources)
    filters = pl.pallas_call(
        lambda *refs: filter_kernel(bands, *refs),
        out_shape=shape(rows, width, width, kind=bf16),
        in_specs=[SMEM, VMEM],
        out_specs=VMEM,
        compiler_params=params,
        name="filters",
    )(cutoff, table)

    def control_step(*halos):
        return pl.pallas_call(
            lambda *refs: control_kernel(len(halos) == 3, *refs),
            out_shape=(field, shape(rows, channels, width), shape(rows, 1, width), shape(rows, hid, width)),
            in_specs=[VMEM] * (7 + len(halos)),
            out_specs=(VMEM,) * 4,
            scratch_shapes=scratch(rows, channels, width, hid, BIAS_ROWS),
            compiler_params=params,
            name="control",
        )(*halos, taps, gain, offset, w_in, w_out, land, filters)

    def conv_step(near, own, far):
        return pl.pallas_call(
            conv_kernel,
            out_shape=shape(rows, channels, width),
            in_specs=[VMEM] * 4,
            out_specs=VMEM,
            compiler_params=params,
            name="conv",
        )(near, own, far, taps)

    def tangent_step(ready, spare, inputs, unit, scale, slope, advanced):
        return pl.pallas_call(
            lambda *refs: tangent_kernel(ready, *refs),
            out_shape=shape(rows, channels + spare, width, kind=bf16),
            in_specs=[VMEM] * (9 + len(inputs)),
            out_specs=VMEM,
            scratch_shapes=scratch(rows, channels, width, hid, 0, not ready),
            compiler_params=params,
            name="tangent",
        )(*inputs, gain, w_in, w_out, land, filters, unit, scale, slope, advanced)

    near, far = exchange(member, range(1, members))
    control = member
    count = 2
    while count < members:
        sent = across(control, [(m, m + count) for m in range(0, count, 2) if m + count < members])
        control = jnp.where((me >= count) & (me < 2 * count), sent, control)
        count *= 2
    control, taps = lax.optimization_barrier((control, taps))
    control_other = across(control, partners)
    control_near, control_far = exchange(control, evens)
    conv = conv_step(near, member, far)
    control_near, control_far, conv, filters = lax.optimization_barrier((control_near, control_far, conv, filters))
    other = (across(control_near, partners), control_other, across(control_far, partners))
    control, unit, scale, slope = control_step(control_near, control, control_far, *other)
    for step in range(1, STEPS):
        halo = send(control, neighbours(evens, 0) + neighbours(odds, 1))
        inputs = (member, conv) if step == 1 else (near, member, far, taps)
        member = tangent_step(step == 1, SPARE, inputs, unit, scale, slope, control)
        halo, _ = lax.optimization_barrier((halo, member))
        other = across(halo, swapped)
        near, far = exchange(member, range(1, members))
        control, unit, scale, slope = control_step(halo, control, other)
    return tangent_step(False, 0, (near, member, far, taps), unit, scale, slope, control)[None]


def solution(mesh):
    in_specs = (
        P(("runs", "mem"), "lat", None, None),
        P("lat", None),
        P(),
        P(),
        P(),
        P(),
        P(),
        P(),
        P(),
    )
    out_specs = P(("runs", "mem"), "lat", None, None)
    return jax.shard_map(
        per_device, mesh=mesh, in_specs=in_specs, out_specs=out_specs, check_vma=False
    )
```

time: 93.9 us -> 81.3 us (0.87)
  starting transfers between devices: 31.6 us -> 24.5 us
  Pallas kernels: 40.3 us -> 33.3 us
  other arithmetic: 4.42 us -> 1.2 us
  local copies, waits for them, and re-layouts: 1.54 us -> 4.51 us
  waiting for transfers between devices: 15 us -> 17 us
    ppermute x14 -> x12, starting transfers between devices: 31.6 us -> 24.5 us  [send(): lax.ppermute(block, ('mem', 'lat'), [(a * bands + i, b * bands + j) for (...]
    pallas_call x5 -> x7, Pallas kernels: 40.3 us -> 33.3 us  [the longest x2 14.8 us: control_step(): pl.pallas_call(lambda *refs: control_kernel(len(halos) == 3, *refs), out_...]
    unnamed x24 -> x20, local copies, waits for them, and re-layouts: 0.48 us -> 4.51 us
    select_n x8 -> x0, other arithmetic: 2.87 us -> none  [the longest x1 1.21 us: per_device(): control_up = jnp.where(me == 0, up, control_up)]
    ppermute x14 -> x12, waiting for transfers between devices: 15 us -> 17 us  [send(): lax.ppermute(block, ('mem', 'lat'), [(a * bands + i, b * bands + j) for (...]
  transfers between devices with their start and end apart: 14 -> 12, of which waited for: 5 -> 8; matrix products, arithmetic and copies ran while one was open for 6% -> 1% of each run, Pallas kernels for 22% -> 24%
where the time goes in v3:
time: 81.3 us; the launch traced here: 80.8 us
  Pallas kernels  33.3 us (41%)
  starting transfers between devices  24.5 us (30%)
  waiting for transfers between devices  17 us (21%)
  local copies, waits for them, and re-layouts  4.51 us (6%)
  other arithmetic  1.2 us (1%)
    ppermute x12, starting transfers between devices, send(): lax.ppermute(block, ('mem', 'lat'), [(a * bands + i, b * bands + j) for (...  24.5 us
    ppermute x12, waiting for transfers between devices, send(): lax.ppermute(block, ('mem', 'lat'), [(a * bands + i, b * bands + j) for (...  17 us
    pallas_call x2, Pallas kernels, control_step(): pl.pallas_call(lambda *refs: control_kernel(len(halos) == 3, *refs), out_...  14.8 us
    pallas_call x2, Pallas kernels, tangent_step(): pl.pallas_call(lambda *refs: tangent_kernel(ready, *refs), out_shape=shap...  9.45 us
    unnamed x20, local copies, waits for them, and re-layouts  4.51 us
    pallas_call x1, Pallas kernels, per_device(): pl.pallas_call(lambda *refs: filter_kernel(bands, *refs), out_shape=shape...  3.49 us
    pallas_call x1, Pallas kernels, conv_step(): pl.pallas_call(conv_kernel, out_shape=shape(rows, channels, width), in_sp...  2.85 us
    pallas_call x1, Pallas kernels, per_device(): pl.pallas_call(prepare_kernel, out_shape=(shape(rows, TAPS, channels, (ro...  2.68 us
  transfers between devices with their start and end apart: 12, of which 8 were waited for; matrix products, arithmetic and copies ran while one was open for 1% of the time, Pallas kernels for 24%

profile of v3, /device:TPU:10, one launch (start us, length us, event | category | flops | bytes accessed | tf_op | source)
XLA Modules:
  0.0 80.8 jit_solution(10635715871866827068)
XLA Ops:
  0.0 0.0 copy-start.2
  0.0 1.4 %collective-permute-start = (bf16[3,160,768]{2,1,0:T(8,128)(2,1)}, bf16[3,160,768]{2,1,0:T(8,128)(2,1)S(1)}, u32[]{:S(2)}, u32[]{:S(2)}) collective-permute-start(bf16[3,160,768]{2,1,0:T(8,128)(2,1)} %bitcast.7), channel_id=1, source_target_pairs={{0,8},{1,9},{2,10},{3,11},{16,24},{17,25},{18,26},{19,27}} | collective-permute-start | bytes 2211848 | tf_op jit(solution)/shard_map/ppermute | solution.py:318
  1.4 3.5 %collective-permute-start.4 = (bf16[3,160,768]{2,1,0:T(8,128)(2,1)}, bf16[3,160,768]{2,1,0:T(8,128)(2,1)S(1)}, u32[]{:S(2)}, u32[]{:S(2)}) collective-permute-start(bf16[3,160,768]{2,1,0:T(8,128)(2,1)} %bitcast.8), channel_id=1, source_target_pairs={{5,6},{9,10},{13,14},{6,5},{10,9},{14,13},{21,22},{25,26},{29,30},... | collective-permute-start | bytes 2211848 | tf_op jit(solution)/shard_map/ppermute | solution.py:318
  4.9 1.9 %collective-permute-start.3 = (bf16[3,160,768]{2,1,0:T(8,128)(2,1)}, bf16[3,160,768]{2,1,0:T(8,128)(2,1)S(1)}, u32[]{:S(2)}, u32[]{:S(2)}) collective-permute-start(bf16[3,160,768]{2,1,0:T(8,128)(2,1)} %bitcast.9), channel_id=1, source_target_pairs={{4,5},{6,7},{8,9},{10,11},{12,13},{14,15},{5,4},{7,6},{9,8},{11,10... | collective-permute-start | bytes 2211848 | tf_op jit(solution)/shard_map/ppermute | solution.py:318
  6.9 0.0 copy-start.3
  6.9 0.9 %copy-done.3 = bf16[160,640]{1,0:T(8,128)(2,1)S(1)} copy-done((bf16[160,640]{1,0:T(8,128)(2,1)S(1)}, bf16[160,640]{1,0:T(8,128)(2,1)}, u32[]{:S(2)}) %copy-start.3) | copy-done | bytes 204824
  7.8 0.0 copy-start.4
  7.8 0.8 %copy-done.4 = f32[7,7,160]{2,1,0:T(8,128)S(1)} copy-done((f32[7,7,160]{2,1,0:T(8,128)S(1)}, f32[7,7,160]{2,1,0:T(8,128)}, u32[]{:S(2)}) %copy-start.4) | copy-done | bytes 31384
  8.6 0.0 copy-start.5
  8.6 0.7 copy-done.5
  9.3 0.0 copy-start.6
  9.3 0.7 copy-done.6
  10.0 0.0 copy-start.7
  10.0 0.7 copy-done.7
  10.7 0.0 copy-start.8
  10.7 0.7 copy-done.8
  11.4 0.0 copy-start.9
  11.4 2.7 %prepare.1 = (bf16[3,7,160,144]{3,2,1,0:T(8,128)(2,1)S(1)}, f32[160,128]{1,0:T(8,128)S(1)}, f32[160,128]{1,0:T(8,128)S(1)}, bf16[640,176]{1,0:T(8,128)(2,1)S(1)}, f32[3,768]{1,0:T(4,128)S(1)}) custom-call(f32[7,7,160]{2,1,0:T(8,128)S(1)} %copy-done.4, f32[1,160]{1,0:T(1,128)S(1)} %bitcast.17, f32[1,160]{1,0:T(1,128)S(1)} %bitcast.18, ...), custom_call_target="tpu_custom_call" | custom-call | tf_op jit(solution)/shard_map/prepare/pallas_call | solution.py:339
  14.1 0.0 collective-permute-done
  14.1 1.2 %broadcast_select_fusion.refs_1_ = bf16[3,160,768]{2,1,0:T(8,128)(2,1)S(1)} fusion(bf16[3,160,768]{2,1,0:T(8,128)(2,1)S(1)} %collective-permute-done, pred[]{:T(512)S(6)} %and.4, bf16[1,3,160,768]{3,2,1,0:T(8,128)(2,1)} %param.10), kind=kLoop, calls=%fused_computation | loop fusion | flops 368640 | bytes 2211841 | tf_op jit(solution)/shard_map/jit(_where)/select_n | solution.py:400
  15.3 0.0 copy-start
  15.3 3.2 %collective-permute-start.2 = (bf16[3,160,768]{2,1,0:T(8,128)(2,1)S(1)}, bf16[3,160,768]{2,1,0:T(8,128)(2,1)S(1)}, u32[]{:S(2)}, u32[]{:S(2)}) collective-permute-start(bf16[3,160,768]{2,1,0:T(8,128)(2,1)S(1)} %broadcast_select_fusion.refs_1_), channel_id=1, source_target_pairs={{1,2},{9,10},{2,1},{10,9},{17,18},{25,26},{18,17},{26,25}} | collective-permute-start | bytes 2211848 | tf_op jit(solution)/shard_map/ppermute | solution.py:318
  18.5 1.9 %collective-permute-start.1 = (bf16[3,160,768]{2,1,0:T(8,128)(2,1)S(1)}, bf16[3,160,768]{2,1,0:T(8,128)(2,1)S(1)}, u32[]{:S(2)}, u32[]{:S(2)}) collective-permute-start(bf16[3,160,768]{2,1,0:T(8,128)(2,1)S(1)} %broadcast_select_fusion.refs_1_), channel_id=1, source_target_pairs={{0,1},{2,3},{8,9},{10,11},{1,0},{3,2},{9,8},{11,10},{16,17},{18,19... | collective-permute-start | bytes 2211848 | tf_op jit(solution)/shard_map/ppermute | solution.py:318
  20.5 0.0 copy-done.2
  20.5 0.0 copy-done.9
  20.5 3.5 %filters.1.refs_12_.refs_6_.refs_9_.refs_8_ = bf16[3,768,768]{2,1,0:T(8,128)(2,1)S(1)} custom-call(s32[12]{0:T(128)S(1)} %copy-done.9, bf16[768,768]{1,0:T(8,128)(2,1)S(1)} %copy-done.2), custom_call_target="tpu_custom_call" | custom-call | tf_op jit(solution)/shard_map/filters/pallas_call | solution.py:354
  24.0 0.0 copy-start.1
  24.0 1.5 %collective-permute-start.6 = (bf16[3,160,768]{2,1,0:T(8,128)(2,1)S(1)}, bf16[3,160,768]{2,1,0:T(8,128)(2,1)S(1)}, u32[]{:S(2)}, u32[]{:S(2)}) collective-permute-start(bf16[3,160,768]{2,1,0:T(8,128)(2,1)S(1)} %broadcast_select_fusion.refs_1_), channel_id=1, source_target_pairs={{0,4},{1,5},{2,6},{3,7},{8,12},{9,13},{10,14},{11,15},{16,20},{17,... | collective-permute-start | bytes 2211848 | tf_op jit(solution)/shard_map/ppermute | solution.py:318
  25.5 0.0 collective-permute-done.4.far
  25.5 0.0 collective-permute-done.3.near
  25.5 0.0 copy-done
  25.5 2.8 %conv.1.refs_1_ = f32[3,160,768]{2,1,0:T(8,128)S(1)} custom-call(bf16[3,160,768]{2,1,0:T(8,128)(2,1)S(1)} %collective-permute-done.3.near, bf16[3,160,768]{2,1,0:T(8,128)(2,1)S(1)} %bitcast.10, bf16[3,160,768]{2,1,0:T(8,128)(2,1)S(1)} %collective-permute-done.4.far, bf16[3,7,160,144]{3,2,1,0:T(8,128)(2,1)S(1)} %get-tuple-element.27.taps.refs_6_.refs_3_), custom_call_target="tpu_custom_call" | custom-call | tf_op jit(solution)/shard_map/conv/pallas_call | solution.py:375
  28.3 0.7 collective-permute-done.2.refs_2_
  29.1 3.2 %collective-permute-done.1.refs_0_ = bf16[3,160,768]{2,1,0:T(8,128)(2,1)S(1)} collective-permute-done((bf16[3,160,768]{2,1,0:T(8,128)(2,1)S(1)}, bf16[3,160,768]{2,1,0:T(8,128)(2,1)S(1)}, u32[]{:S(2)}, u32[]{:S(2)}) %collective-permute-start.1) | collective-permute-done | bytes 737312 | tf_op jit(solution)/shard_map/ppermute | solution.py:318
  32.3 1.3 %collective-permute-start.5 = (bf16[3,160,768]{2,1,0:T(8,128)(2,1)S(1)}, bf16[3,160,768]{2,1,0:T(8,128)(2,1)S(1)}, u32[]{:S(2)}, u32[]{:S(2)}) collective-permute-start(bf16[3,160,768]{2,1,0:T(8,128)(2,1)S(1)} %collective-permute-done.1.refs_0_), channel_id=1, source_target_pairs={{0,4},{1,5},{2,6},{3,7},{8,12},{9,13},{10,14},{11,15},{16,20},{17,... | collective-permute-start | bytes 2211848 | tf_op jit(solution)/shard_map/ppermute | solution.py:318
  33.6 1.5 %collective-permute-start.7 = (bf16[3,160,768]{2,1,0:T(8,128)(2,1)S(1)}, bf16[3,160,768]{2,1,0:T(8,128)(2,1)S(1)}, u32[]{:S(2)}, u32[]{:S(2)}) collective-permute-start(bf16[3,160,768]{2,1,0:T(8,128)(2,1)S(1)} %collective-permute-done.2.refs_2_), channel_id=1, source_target_pairs={{0,4},{1,5},{2,6},{3,7},{8,12},{9,13},{10,14},{11,15},{16,20},{17,... | collective-permute-start | bytes 2211848 | tf_op jit(solution)/shard_map/ppermute | solution.py:318
  35.1 0.0 collective-permute-done.6.refs_4_
  35.2 0.2 collective-permute-done.5.refs_3_
  35.4 1.3 %collective-permute-done.7.refs_5_ = bf16[3,160,768]{2,1,0:T(8,128)(2,1)S(1)} collective-permute-done((bf16[3,160,768]{2,1,0:T(8,128)(2,1)S(1)}, bf16[3,160,768]{2,1,0:T(8,128)(2,1)S(1)}, u32[]{:S(2)}, u32[]{:S(2)}) %collective-permute-start.7) | collective-permute-done | bytes 737312 | tf_op jit(solution)/shard_map/ppermute | solution.py:318
  36.7 0.0 copy-done.1
  36.7 7.5 %control.2 = (bf16[3,160,768]{2,1,0:T(8,128)(2,1)S(1)}, f32[3,160,768]{2,1,0:T(8,128)S(1)}, f32[3,1,768]{2,1,0:T(1,128)S(1)}, f32[3,640,768]{2,1,0:T(8,128)S(1)}) custom-call(bf16[3,160,768]{2,1,0:T(8,128)(2,1)S(1)} %collective-permute-done.1.refs_0_, bf16[3,160,768]{2,1,0:T(8,128)(2,1)S(1)} %broadcast_select_fusion.refs_1_, ...), custom_call_target="tpu_custom_call" | custom-call | tf_op jit(solution)/shard_map/control/pallas_call | solution.py:364
  44.2 2.2 %collective-permute-start.10 = (bf16[3,160,768]{2,1,0:T(8,128)(2,1)S(1)}, bf16[3,160,768]{2,1,0:T(8,128)(2,1)S(1)}, u32[]{:S(2)}, u32[]{:S(2)}) collective-permute-start(bf16[3,160,768]{2,1,0:T(8,128)(2,1)S(1)} %get-tuple-element.39.refs_10_.refs_1_), channel_id=1, source_target_pairs={{0,1},{2,3},{8,9},{10,11},{1,0},{3,2},{9,8},{11,10},{5,6},{13,14},... | collective-permute-start | bytes 2211848 | tf_op jit(solution)/shard_map/ppermute | solution.py:318
  46.4 2.8 %tangent.2.refs_1_ = bf16[3,168,768]{2,1,0:T(8,128)(2,1)S(1)} custom-call(bf16[3,160,768]{2,1,0:T(8,128)(2,1)S(1)} %bitcast.11, f32[3,160,768]{2,1,0:T(8,128)S(1)} %conv.1.refs_1_, f32[160,128]{1,0:T(8,128)S(1)} %get-tuple-element.29.refs_7_.refs_2_.refs_4_, bf16[640,176]{1,0:T(8,128)(2,1)S(1)} %get-tuple-element.30.refs_9_.refs_3_.refs_6_.refs_5_, ...), custom_call_target="tpu_custom_call" | custom-call | tf_op jit(solution)/shard_map/tangent/pallas_call | solution.py:385
  49.3 2.4 %collective-permute-start.9 = (bf16[3,168,768]{2,1,0:T(8,128)(2,1)S(1)}, bf16[3,168,768]{2,1,0:T(8,128)(2,1)S(1)}, u32[]{:S(2)}, u32[]{:S(2)}) collective-permute-start(bf16[3,168,768]{2,1,0:T(8,128)(2,1)S(1)} %tangent.2.refs_1_), channel_id=1, source_target_pairs={{5,6},{9,10},{13,14},{6,5},{10,9},{14,13},{21,22},{25,26},{29,30},... | collective-permute-start | bytes 2322440 | tf_op jit(solution)/shard_map/ppermute | solution.py:318
  51.6 2.2 %collective-permute-start.8 = (bf16[3,168,768]{2,1,0:T(8,128)(2,1)S(1)}, bf16[3,168,768]{2,1,0:T(8,128)(2,1)S(1)}, u32[]{:S(2)}, u32[]{:S(2)}) collective-permute-start(bf16[3,168,768]{2,1,0:T(8,128)(2,1)S(1)} %tangent.2.refs_1_), channel_id=1, source_target_pairs={{4,5},{6,7},{8,9},{10,11},{12,13},{14,15},{5,4},{7,6},{9,8},{11,10... | collective-permute-start | bytes 2322440 | tf_op jit(solution)/shard_map/ppermute | solution.py:318
  53.9 4.0 %collective-permute-done.10.refs_0_ = bf16[3,160,768]{2,1,0:T(8,128)(2,1)S(1)} collective-permute-done((bf16[3,160,768]{2,1,0:T(8,128)(2,1)S(1)}, bf16[3,160,768]{2,1,0:T(8,128)(2,1)S(1)}, u32[]{:S(2)}, u32[]{:S(2)}) %collective-permute-start.10) | collective-permute-done | bytes 737312 | tf_op jit(solution)/shard_map/ppermute | solution.py:318
  57.8 1.4 %collective-permute-start.11 = (bf16[3,160,768]{2,1,0:T(8,128)(2,1)S(1)}, bf16[3,160,768]{2,1,0:T(8,128)(2,1)S(1)}, u32[]{:S(2)}, u32[]{:S(2)}) collective-permute-start(bf16[3,160,768]{2,1,0:T(8,128)(2,1)S(1)} %collective-permute-done.10.refs_0_), channel_id=1, source_target_pairs={{0,4},{1,5},{2,6},{3,7},{8,12},{9,13},{10,14},{11,15},{4,0},{5,1},... | collective-permute-start | bytes 2211848 | tf_op jit(solution)/shard_map/ppermute | solution.py:318
  59.3 1.8 %collective-permute-done.11.refs_2_ = bf16[3,160,768]{2,1,0:T(8,128)(2,1)S(1)} collective-permute-done((bf16[3,160,768]{2,1,0:T(8,128)(2,1)S(1)}, bf16[3,160,768]{2,1,0:T(8,128)(2,1)S(1)}, u32[]{:S(2)}, u32[]{:S(2)}) %collective-permute-start.11) | collective-permute-done | bytes 737312 | tf_op jit(solution)/shard_map/ppermute | solution.py:318
  61.1 7.4 %control.3 = (bf16[3,160,768]{2,1,0:T(8,128)(2,1)S(1)}, f32[3,160,768]{2,1,0:T(8,128)S(1)}, f32[3,1,768]{2,1,0:T(1,128)S(1)}, f32[3,640,768]{2,1,0:T(8,128)S(1)}) custom-call(bf16[3,160,768]{2,1,0:T(8,128)(2,1)S(1)} %collective-permute-done.10.refs_0_, bf16[3,160,768]{2,1,0:T(8,128)(2,1)S(1)} %get-tuple-element.39.refs_10_.refs_1_, ...), custom_call_target="tpu_custom_call" | custom-call | tf_op jit(solution)/shard_map/control/pallas_call | solution.py:364
  68.5 2.9 %collective-permute-done.9.refs_2_ = bf16[3,168,768]{2,1,0:T(8,128)(2,1)S(1)} collective-permute-done((bf16[3,168,768]{2,1,0:T(8,128)(2,1)S(1)}, bf16[3,168,768]{2,1,0:T(8,128)(2,1)S(1)}, u32[]{:S(2)}, u32[]{:S(2)}) %collective-permute-start.9) | collective-permute-done | bytes 774176 | tf_op jit(solution)/shard_map/ppermute | solution.py:318
  71.4 2.8 %collective-permute-done.8.refs_0_ = bf16[3,168,768]{2,1,0:T(8,128)(2,1)S(1)} collective-permute-done((bf16[3,168,768]{2,1,0:T(8,128)(2,1)S(1)}, bf16[3,168,768]{2,1,0:T(8,128)(2,1)S(1)}, u32[]{:S(2)}, u32[]{:S(2)}) %collective-permute-start.8) | collective-permute-done | bytes 774176 | tf_op jit(solution)/shard_map/ppermute | solution.py:318
  74.2 6.6 %tangent.3 = bf16[3,160,768]{2,1,0:T(8,128)(2,1)} custom-call(bf16[3,168,768]{2,1,0:T(8,128)(2,1)S(1)} %collective-permute-done.8.refs_0_, bf16[3,168,768]{2,1,0:T(8,128)(2,1)S(1)} %tangent.2.refs_1_, bf16[3,168,768]{2,1,0:T(8,128)(2,1)S(1)} %collective-permute-done.9.refs_2_, bf16[3,7,160,144]{3,2,1,0:T(8,128)(2,1)S(1)} %get-tuple-element.27.taps.refs_6_.refs_3_, ...), custom_call_target="tpu_custom_call" | custom-call | tf_op jit(solution)/shard_map/tangent/pallas_call | solution.py:385
Async XLA Ops:
  0.0 20.5 %copy-start.2 = (bf16[768,768]{1,0:T(8,128)(2,1)S(1)}, bf16[768,768]{1,0:T(8,128)(2,1)}, u32[]{:S(2)}) copy-start(bf16[768,768]{1,0:T(8,128)(2,1)} %constant.11.clone.refs_1_) | copy-start | bytes 3538948
  0.0 14.1 %collective-permute-start = (bf16[3,160,768]{2,1,0:T(8,128)(2,1)}, bf16[3,160,768]{2,1,0:T(8,128)(2,1)S(1)}, u32[]{:S(2)}, u32[]{:S(2)}) collective-permute-start(bf16[3,160,768]{2,1,0:T(8,128)(2,1)} %bitcast.7), channel_id=1, source_target_pairs={{0,8},{1,9},{2,10},{3,11},{16,24},{17,25},{18,26},{19,27}} | collective-permute-start | bytes 2211848 | tf_op jit(solution)/shard_map/ppermute | solution.py:318
  1.4 24.0 %collective-permute-start.4 = (bf16[3,160,768]{2,1,0:T(8,128)(2,1)}, bf16[3,160,768]{2,1,0:T(8,128)(2,1)S(1)}, u32[]{:S(2)}, u32[]{:S(2)}) collective-permute-start(bf16[3,160,768]{2,1,0:T(8,128)(2,1)} %bitcast.8), channel_id=1, source_target_pairs={{5,6},{9,10},{13,14},{6,5},{10,9},{14,13},{21,22},{25,26},{29,30},... | collective-permute-start | bytes 2211848 | tf_op jit(solution)/shard_map/ppermute | solution.py:318
  4.9 20.6 %collective-permute-start.3 = (bf16[3,160,768]{2,1,0:T(8,128)(2,1)}, bf16[3,160,768]{2,1,0:T(8,128)(2,1)S(1)}, u32[]{:S(2)}, u32[]{:S(2)}) collective-permute-start(bf16[3,160,768]{2,1,0:T(8,128)(2,1)} %bitcast.9), channel_id=1, source_target_pairs={{4,5},{6,7},{8,9},{10,11},{12,13},{14,15},{5,4},{7,6},{9,8},{11,10... | collective-permute-start | bytes 2211848 | tf_op jit(solution)/shard_map/ppermute | solution.py:318
  6.9 0.9 %copy-start.3 = (bf16[160,640]{1,0:T(8,128)(2,1)S(1)}, bf16[160,640]{1,0:T(8,128)(2,1)}, u32[]{:S(2)}) copy-start(bf16[160,640]{1,0:T(8,128)(2,1)} %refs_3_.1) | copy-start | bytes 614404
  7.8 0.8 %copy-start.4 = (f32[7,7,160]{2,1,0:T(8,128)S(1)}, f32[7,7,160]{2,1,0:T(8,128)}, u32[]{:S(2)}) copy-start(f32[7,7,160]{2,1,0:T(8,128)} %refs_0_.2) | copy-start | bytes 94084
  8.6 0.7 copy-start.5
  9.3 0.7 copy-start.6
  10.0 0.7 copy-start.7
  10.7 0.7 copy-start.8
  11.4 9.1 %copy-start.9 = (s32[12]{0:T(128)S(1)}, s32[12]{0:T(128)}, u32[]{:S(2)}) copy-start(s32[12]{0:T(128)} %refs_0_.3) | copy-start | bytes 148
  15.3 10.2 %copy-start = (bf16[1,3,160,768]{3,2,1,0:T(8,128)(2,1)S(1)}, bf16[1,3,160,768]{3,2,1,0:T(8,128)(2,1)}, u32[]{:S(2)}) copy-start(bf16[1,3,160,768]{3,2,1,0:T(8,128)(2,1)} %param.10) | copy-start | bytes 2211844
  15.3 13.8 %collective-permute-start.2 = (bf16[3,160,768]{2,1,0:T(8,128)(2,1)S(1)}, bf16[3,160,768]{2,1,0:T(8,128)(2,1)S(1)}, u32[]{:S(2)}, u32[]{:S(2)}) collective-permute-start(bf16[3,160,768]{2,1,0:T(8,128)(2,1)S(1)} %broadcast_select_fusion.refs_1_), channel_id=1, source_target_pairs={{1,2},{9,10},{2,1},{10,9},{17,18},{25,26},{18,17},{26,25}} | collective-permute-start | bytes 2211848 | tf_op jit(solution)/shard_map/ppermute | solution.py:318
  18.5 13.8 %collective-permute-start.1 = (bf16[3,160,768]{2,1,0:T(8,128)(2,1)S(1)}, bf16[3,160,768]{2,1,0:T(8,128)(2,1)S(1)}, u32[]{:S(2)}, u32[]{:S(2)}) collective-permute-start(bf16[3,160,768]{2,1,0:T(8,128)(2,1)S(1)} %broadcast_select_fusion.refs_1_), channel_id=1, source_target_pairs={{0,1},{2,3},{8,9},{10,11},{1,0},{3,2},{9,8},{11,10},{16,17},{18,19... | collective-permute-start | bytes 2211848 | tf_op jit(solution)/shard_map/ppermute | solution.py:318
  24.0 12.8 %copy-start.1 = (bf16[640,160]{0,1:T(8,128)(2,1)S(1)}, bf16[640,160]{0,1:T(8,128)(2,1)}, u32[]{:S(2)}) copy-start(bf16[640,160]{0,1:T(8,128)(2,1)} %param.18) | copy-start | bytes 614404
  24.0 11.2 %collective-permute-start.6 = (bf16[3,160,768]{2,1,0:T(8,128)(2,1)S(1)}, bf16[3,160,768]{2,1,0:T(8,128)(2,1)S(1)}, u32[]{:S(2)}, u32[]{:S(2)}) collective-permute-start(bf16[3,160,768]{2,1,0:T(8,128)(2,1)S(1)} %broadcast_select_fusion.refs_1_), channel_id=1, source_target_pairs={{0,4},{1,5},{2,6},{3,7},{8,12},{9,13},{10,14},{11,15},{16,20},{17,... | collective-permute-start | bytes 2211848 | tf_op jit(solution)/shard_map/ppermute | solution.py:318
  32.3 3.1 %collective-permute-start.5 = (bf16[3,160,768]{2,1,0:T(8,128)(2,1)S(1)}, bf16[3,160,768]{2,1,0:T(8,128)(2,1)S(1)}, u32[]{:S(2)}, u32[]{:S(2)}) collective-permute-start(bf16[3,160,768]{2,1,0:T(8,128)(2,1)S(1)} %collective-permute-done.1.refs_0_), channel_id=1, source_target_pairs={{0,4},{1,5},{2,6},{3,7},{8,12},{9,13},{10,14},{11,15},{16,20},{17,... | collective-permute-start | bytes 2211848 | tf_op jit(solution)/shard_map/ppermute | solution.py:318
  33.6 3.1 %collective-permute-start.7 = (bf16[3,160,768]{2,1,0:T(8,128)(2,1)S(1)}, bf16[3,160,768]{2,1,0:T(8,128)(2,1)S(1)}, u32[]{:S(2)}, u32[]{:S(2)}) collective-permute-start(bf16[3,160,768]{2,1,0:T(8,128)(2,1)S(1)} %collective-permute-done.2.refs_2_), channel_id=1, source_target_pairs={{0,4},{1,5},{2,6},{3,7},{8,12},{9,13},{10,14},{11,15},{16,20},{17,... | collective-permute-start | bytes 2211848 | tf_op jit(solution)/shard_map/ppermute | solution.py:318
  44.2 13.6 %collective-permute-start.10 = (bf16[3,160,768]{2,1,0:T(8,128)(2,1)S(1)}, bf16[3,160,768]{2,1,0:T(8,128)(2,1)S(1)}, u32[]{:S(2)}, u32[]{:S(2)}) collective-permute-start(bf16[3,160,768]{2,1,0:T(8,128)(2,1)S(1)} %get-tuple-element.39.refs_10_.refs_1_), channel_id=1, source_target_pairs={{0,1},{2,3},{8,9},{10,11},{1,0},{3,2},{9,8},{11,10},{5,6},{13,14},... | collective-permute-start | bytes 2211848 | tf_op jit(solution)/shard_map/ppermute | solution.py:318
  49.3 22.1 %collective-permute-start.9 = (bf16[3,168,768]{2,1,0:T(8,128)(2,1)S(1)}, bf16[3,168,768]{2,1,0:T(8,128)(2,1)S(1)}, u32[]{:S(2)}, u32[]{:S(2)}) collective-permute-start(bf16[3,168,768]{2,1,0:T(8,128)(2,1)S(1)} %tangent.2.refs_1_), channel_id=1, source_target_pairs={{5,6},{9,10},{13,14},{6,5},{10,9},{14,13},{21,22},{25,26},{29,30},... | collective-permute-start | bytes 2322440 | tf_op jit(solution)/shard_map/ppermute | solution.py:318
  51.6 22.5 %collective-permute-start.8 = (bf16[3,168,768]{2,1,0:T(8,128)(2,1)S(1)}, bf16[3,168,768]{2,1,0:T(8,128)(2,1)S(1)}, u32[]{:S(2)}, u32[]{:S(2)}) collective-permute-start(bf16[3,168,768]{2,1,0:T(8,128)(2,1)S(1)} %tangent.2.refs_1_), channel_id=1, source_target_pairs={{4,5},{6,7},{8,9},{10,11},{12,13},{14,15},{5,4},{7,6},{9,8},{11,10... | collective-permute-start | bytes 2322440 | tf_op jit(solution)/shard_map/ppermute | solution.py:318
  57.8 3.3 %collective-permute-start.11 = (bf16[3,160,768]{2,1,0:T(8,128)(2,1)S(1)}, bf16[3,160,768]{2,1,0:T(8,128)(2,1)S(1)}, u32[]{:S(2)}, u32[]{:S(2)}) collective-permute-start(bf16[3,160,768]{2,1,0:T(8,128)(2,1)S(1)} %collective-permute-done.10.refs_0_), channel_id=1, source_target_pairs={{0,4},{1,5},{2,6},{3,7},{8,12},{9,13},{10,14},{11,15},{4,0},{5,1},... | collective-permute-start | bytes 2211848 | tf_op jit(solution)/shard_map/ppermute | solution.py:318

commit v4 on v3

--- a/solution.py
+++ b/solution.py
@@ -58,7 +58,7 @@
     here = lax.broadcasted_iota(jnp.int32, (channels, depth), 0)
     block = lane // GROUP
     turned = jnp.where(block < HALO, block + rows + HALO, jnp.where(block < HALO + rows, block, block - rows - HALO))
-    block = jnp.where(band % 2 == 1, block, turned)
+    block = jnp.where((band + lax.axis_index("mem")) % 2 == 1, block, turned)
     block = jnp.where(lane % GROUP == here % GROUP, block, -1)
     for j in range(TAPS):
         lines = [kernel[i, j : j + 1, :] for i in range(TAPS)] + [jnp.zeros((128 - TAPS, channels), f32)]
@@ -129,10 +129,8 @@
     return lambda at: ref[:, at, :]
 
 
-def choose(second, first, other):
-    if other is None:
-        return read(first)
-    return lambda at: jnp.where(second, other[:, at, :], first[:, at, :])
+def choose(odd, first, other):
+    return lambda at: jnp.where(odd, other[:, at, :], first[:, at, :])
 
 
 def pipeline(tiles, first, second, third):
@@ -157,12 +155,11 @@
     ).astype(bf16)
 
 
-def control_kernel(swap, *refs):
-    near, own, far = refs[:3]
+def control_kernel(*refs):
+    first_halo, own, second_halo = refs[:3]
     refs = refs[3:]
-    if swap:
-        other = [far, None, near]
-    else:
+    other = None
+    if len(refs) > 19:
         other, refs = refs[:3], refs[3:]
     (
         taps, gain, bias, w_in, w_out, land, filters,
@@ -171,10 +168,13 @@
     rows, channels, width = out.shape
     hid = w_in.shape[0]
     normed, hidden, act = (normed, normed_b), (hidden, hidden_b), (act, act_b)
-    second = lax.axis_index("mem") % 2 == 1
+    odd = lax.axis_index("mem") % 2 == 1
     for block in normed:
         add_bias_rows(block, channels)
-    convolve(*(choose(second, a, b) for a, b in zip((near, own, far), other)), taps, conv)
+    blocks = [read(first_halo), read(own), read(second_halo)]
+    if other is not None:
+        blocks = [choose(odd, a, b) for a, b in zip((first_halo, own, second_halo), other)]
+    convolve(*blocks, taps, conv)
     across = width // LANES
 
     def place(i):
@@ -208,8 +208,8 @@
         r, at = place(i)
         update = jnp.dot(w_out[...], act[i % 2][...], preferred_element_type=f32)
         field = own[r, :, at]
-        if other[1] is not None:
-            field = jnp.where(second, other[1][r, :, at], field)
+        if other is not None:
+            field = jnp.where(odd, other[1][r, :, at], field)
         raw[r * channels : (r + 1) * channels, at] = (land[r : r + 1, at] * (field.astype(f32) + update)).astype(bf16)
         if i % across == across - 1:
             polar_filter(raw, filters, out, r)
@@ -322,8 +322,9 @@
         return pairs + [(b, a) for a, b in pairs]
 
     def exchange(block, which):
-        far = send(block, neighbours(which, 1))
-        return send(block, neighbours(which, 0)), far
+        even, odd = [m for m in which if m % 2 == 0], [m for m in which if m % 2 == 1]
+        first = send(block, neighbours(even, 0) + neighbours(odd, 1))
+        return first, send(block, neighbours(even, 1) + neighbours(odd, 0))
 
     def across(block, pairs):
         return send(block, [((a, z), (b, z)) for a, b in pairs for z in range(bands)])
@@ -362,7 +363,7 @@
 
     def control_step(*halos):
         return pl.pallas_call(
-            lambda *refs: control_kernel(len(halos) == 3, *refs),
+            control_kernel,
             out_shape=(field, shape(rows, channels, width), shape(rows, 1, width), shape(rows, hid, width)),
             in_specs=[VMEM] * (7 + len(halos)),
             out_specs=(VMEM,) * 4,
@@ -404,10 +405,10 @@
     control_near, control_far = exchange(control, evens)
     conv = conv_step(near, member, far)
     control_near, control_far, conv, filters = lax.optimization_barrier((control_near, control_far, conv, filters))
-    other = (across(control_near, partners), control_other, across(control_far, partners))
+    other = (across(control_far, partners), control_other, across(control_near, partners))
     control, unit, scale, slope = control_step(control_near, control, control_far, *other)
     for step in range(1, STEPS):
-        halo = send(control, neighbours(evens, 0) + neighbours(odds, 1))
+        halo = exchange(control, range(members))[0]
         inputs = (member, conv) if step == 1 else (near, member, far, taps)
         member = tangent_step(step == 1, SPARE, inputs, unit, scale, slope, control)
         halo, _ = lax.optimization_barrier((halo, member))

time: 81.3 us -> 80.9 us (level)
  starting transfers between devices: 24.5 us -> 23.1 us
  waiting for transfers between devices: 17 us -> 18 us
    ppermute x12, starting transfers between devices: 24.5 us -> 23.1 us  [send(): lax.ppermute(block, ('mem', 'lat'), [(a * bands + i, b * bands + j) for (...]
    ppermute x12, waiting for transfers between devices: 17 us -> 18 us  [send(): lax.ppermute(block, ('mem', 'lat'), [(a * bands + i, b * bands + j) for (...]
where the time goes in v4:
time: 80.9 us; the launch traced here: 80.3 us
  Pallas kernels  33.3 us (41%)
  starting transfers between devices  23.1 us (29%)
  waiting for transfers between devices  18 us (22%)
  local copies, waits for them, and re-layouts  4.51 us (6%)
  other arithmetic  1.2 us (1%)
    ppermute x12, starting transfers between devices, send(): lax.ppermute(block, ('mem', 'lat'), [(a * bands + i, b * bands + j) for (...  23.1 us
    ppermute x12, waiting for transfers between devices, send(): lax.ppermute(block, ('mem', 'lat'), [(a * bands + i, b * bands + j) for (...  18 us
    pallas_call x2, Pallas kernels, control_step(): pl.pallas_call(control_kernel, out_shape=(field, shape(rows, channels, wi...  14.8 us
    pallas_call x2, Pallas kernels, tangent_step(): pl.pallas_call(lambda *refs: tangent_kernel(ready, *refs), out_shape=shap...  9.45 us
    unnamed x20, local copies, waits for them, and re-layouts  4.51 us
    pallas_call x1, Pallas kernels, per_device(): pl.pallas_call(lambda *refs: filter_kernel(bands, *refs), out_shape=shape...  3.49 us
    pallas_call x1, Pallas kernels, conv_step(): pl.pallas_call(conv_kernel, out_shape=shape(rows, channels, width), in_sp...  2.85 us
    pallas_call x1, Pallas kernels, per_device(): pl.pallas_call(prepare_kernel, out_shape=(shape(rows, TAPS, channels, (ro...  2.68 us
  transfers between devices with their start and end apart: 12, of which 8 were waited for; matrix products, arithmetic and copies ran while one was open for 1% of the time, Pallas kernels for 24%

profile of v4, /device:TPU:10, one launch (start us, length us, event | category | flops | bytes accessed | tf_op | source)
XLA Modules:
  0.0 80.3 jit_solution(14492701389260595686)
XLA Ops:
  0.0 0.0 copy-start.2
  0.0 1.4 %collective-permute-start = (bf16[3,160,768]{2,1,0:T(8,128)(2,1)}, bf16[3,160,768]{2,1,0:T(8,128)(2,1)S(1)}, u32[]{:S(2)}, u32[]{:S(2)}) collective-permute-start(bf16[3,160,768]{2,1,0:T(8,128)(2,1)} %bitcast.7), channel_id=1, source_target_pairs={{0,8},{1,9},{2,10},{3,11},{16,24},{17,25},{18,26},{19,27}} | collective-permute-start | bytes 2211848 | tf_op jit(solution)/shard_map/ppermute | solution.py:318
  1.4 3.5 %collective-permute-start.4 = (bf16[3,160,768]{2,1,0:T(8,128)(2,1)}, bf16[3,160,768]{2,1,0:T(8,128)(2,1)S(1)}, u32[]{:S(2)}, u32[]{:S(2)}) collective-permute-start(bf16[3,160,768]{2,1,0:T(8,128)(2,1)} %bitcast.8), channel_id=1, source_target_pairs={{9,10},{10,9},{4,5},{6,7},{12,13},{14,15},{5,4},{7,6},{13,12},{15,... | collective-permute-start | bytes 2211848 | tf_op jit(solution)/shard_map/ppermute | solution.py:318
  4.9 1.9 %collective-permute-start.3 = (bf16[3,160,768]{2,1,0:T(8,128)(2,1)}, bf16[3,160,768]{2,1,0:T(8,128)(2,1)S(1)}, u32[]{:S(2)}, u32[]{:S(2)}) collective-permute-start(bf16[3,160,768]{2,1,0:T(8,128)(2,1)} %bitcast.9), channel_id=1, source_target_pairs={{8,9},{10,11},{9,8},{11,10},{5,6},{13,14},{6,5},{14,13},{24,25},{2... | collective-permute-start | bytes 2211848 | tf_op jit(solution)/shard_map/ppermute | solution.py:318
  6.9 0.0 copy-start.3
  6.9 0.9 %copy-done.3 = bf16[160,640]{1,0:T(8,128)(2,1)S(1)} copy-done((bf16[160,640]{1,0:T(8,128)(2,1)S(1)}, bf16[160,640]{1,0:T(8,128)(2,1)}, u32[]{:S(2)}) %copy-start.3) | copy-done | bytes 204824
  7.8 0.0 copy-start.4
  7.8 0.8 %copy-done.4 = f32[7,7,160]{2,1,0:T(8,128)S(1)} copy-done((f32[7,7,160]{2,1,0:T(8,128)S(1)}, f32[7,7,160]{2,1,0:T(8,128)}, u32[]{:S(2)}) %copy-start.4) | copy-done | bytes 31384
  8.6 0.0 copy-start.5
  8.6 0.7 copy-done.5
  9.3 0.0 copy-start.6
  9.3 0.7 copy-done.6
  10.0 0.0 copy-start.7
  10.0 0.7 copy-done.7
  10.7 0.0 copy-start.8
  10.7 0.7 copy-done.8
  11.4 0.0 copy-start.9
  11.4 2.7 %prepare.1 = (bf16[3,7,160,144]{3,2,1,0:T(8,128)(2,1)S(1)}, f32[160,128]{1,0:T(8,128)S(1)}, f32[160,128]{1,0:T(8,128)S(1)}, bf16[640,176]{1,0:T(8,128)(2,1)S(1)}, f32[3,768]{1,0:T(4,128)S(1)}) custom-call(f32[7,7,160]{2,1,0:T(8,128)S(1)} %copy-done.4, f32[1,160]{1,0:T(1,128)S(1)} %bitcast.17, f32[1,160]{1,0:T(1,128)S(1)} %bitcast.18, ...), custom_call_target="tpu_custom_call" | custom-call | tf_op jit(solution)/shard_map/prepare/pallas_call | solution.py:340
  14.1 0.0 collective-permute-done
  14.1 1.2 %broadcast_select_fusion.refs_1_ = bf16[3,160,768]{2,1,0:T(8,128)(2,1)S(1)} fusion(bf16[3,160,768]{2,1,0:T(8,128)(2,1)S(1)} %collective-permute-done, pred[]{:T(512)S(6)} %and.4, bf16[1,3,160,768]{3,2,1,0:T(8,128)(2,1)} %param.10), kind=kLoop, calls=%fused_computation | loop fusion | flops 368640 | bytes 2211841 | tf_op jit(solution)/shard_map/jit(_where)/select_n | solution.py:401
  15.3 0.0 copy-start
  15.3 3.2 %collective-permute-start.2 = (bf16[3,160,768]{2,1,0:T(8,128)(2,1)S(1)}, bf16[3,160,768]{2,1,0:T(8,128)(2,1)S(1)}, u32[]{:S(2)}, u32[]{:S(2)}) collective-permute-start(bf16[3,160,768]{2,1,0:T(8,128)(2,1)S(1)} %broadcast_select_fusion.refs_1_), channel_id=1, source_target_pairs={{1,2},{9,10},{2,1},{10,9},{17,18},{25,26},{18,17},{26,25}} | collective-permute-start | bytes 2211848 | tf_op jit(solution)/shard_map/ppermute | solution.py:318
  18.5 1.9 %collective-permute-start.1 = (bf16[3,160,768]{2,1,0:T(8,128)(2,1)S(1)}, bf16[3,160,768]{2,1,0:T(8,128)(2,1)S(1)}, u32[]{:S(2)}, u32[]{:S(2)}) collective-permute-start(bf16[3,160,768]{2,1,0:T(8,128)(2,1)S(1)} %broadcast_select_fusion.refs_1_), channel_id=1, source_target_pairs={{0,1},{2,3},{8,9},{10,11},{1,0},{3,2},{9,8},{11,10},{16,17},{18,19... | collective-permute-start | bytes 2211848 | tf_op jit(solution)/shard_map/ppermute | solution.py:318
  20.5 0.0 copy-done.2
  20.5 0.0 copy-done.9
  20.5 3.5 %filters.1.refs_12_.refs_6_.refs_9_.refs_8_ = bf16[3,768,768]{2,1,0:T(8,128)(2,1)S(1)} custom-call(s32[12]{0:T(128)S(1)} %copy-done.9, bf16[768,768]{1,0:T(8,128)(2,1)S(1)} %copy-done.2), custom_call_target="tpu_custom_call" | custom-call | tf_op jit(solution)/shard_map/filters/pallas_call | solution.py:355
  24.0 0.0 copy-start.1
  24.0 1.5 %collective-permute-start.6 = (bf16[3,160,768]{2,1,0:T(8,128)(2,1)S(1)}, bf16[3,160,768]{2,1,0:T(8,128)(2,1)S(1)}, u32[]{:S(2)}, u32[]{:S(2)}) collective-permute-start(bf16[3,160,768]{2,1,0:T(8,128)(2,1)S(1)} %broadcast_select_fusion.refs_1_), channel_id=1, source_target_pairs={{0,4},{1,5},{2,6},{3,7},{8,12},{9,13},{10,14},{11,15},{16,20},{17,... | collective-permute-start | bytes 2211848 | tf_op jit(solution)/shard_map/ppermute | solution.py:318
  25.5 0.0 collective-permute-done.4.far
  25.5 0.0 collective-permute-done.3.near
  25.5 0.0 copy-done
  25.5 2.8 %conv.1.refs_1_ = f32[3,160,768]{2,1,0:T(8,128)S(1)} custom-call(bf16[3,160,768]{2,1,0:T(8,128)(2,1)S(1)} %collective-permute-done.3.near, bf16[3,160,768]{2,1,0:T(8,128)(2,1)S(1)} %bitcast.10, bf16[3,160,768]{2,1,0:T(8,128)(2,1)S(1)} %collective-permute-done.4.far, bf16[3,7,160,144]{3,2,1,0:T(8,128)(2,1)S(1)} %get-tuple-element.27.taps.refs_6_.refs_3_), custom_call_target="tpu_custom_call" | custom-call | tf_op jit(solution)/shard_map/conv/pallas_call | solution.py:376
  28.3 2.4 %collective-permute-done.2.refs_2_ = bf16[3,160,768]{2,1,0:T(8,128)(2,1)S(1)} collective-permute-done((bf16[3,160,768]{2,1,0:T(8,128)(2,1)S(1)}, bf16[3,160,768]{2,1,0:T(8,128)(2,1)S(1)}, u32[]{:S(2)}, u32[]{:S(2)}) %collective-permute-start.2) | collective-permute-done | bytes 737312 | tf_op jit(solution)/shard_map/ppermute | solution.py:318
  30.8 1.1 %collective-permute-done.1.refs_0_ = bf16[3,160,768]{2,1,0:T(8,128)(2,1)S(1)} collective-permute-done((bf16[3,160,768]{2,1,0:T(8,128)(2,1)S(1)}, bf16[3,160,768]{2,1,0:T(8,128)(2,1)S(1)}, u32[]{:S(2)}, u32[]{:S(2)}) %collective-permute-start.1) | collective-permute-done | bytes 737312 | tf_op jit(solution)/shard_map/ppermute | solution.py:318
  31.9 1.3 %collective-permute-start.7 = (bf16[3,160,768]{2,1,0:T(8,128)(2,1)S(1)}, bf16[3,160,768]{2,1,0:T(8,128)(2,1)S(1)}, u32[]{:S(2)}, u32[]{:S(2)}) collective-permute-start(bf16[3,160,768]{2,1,0:T(8,128)(2,1)S(1)} %collective-permute-done.1.refs_0_), channel_id=1, source_target_pairs={{0,4},{1,5},{2,6},{3,7},{8,12},{9,13},{10,14},{11,15},{16,20},{17,... | collective-permute-start | bytes 2211848 | tf_op jit(solution)/shard_map/ppermute | solution.py:318
  33.2 1.5 %collective-permute-start.5 = (bf16[3,160,768]{2,1,0:T(8,128)(2,1)S(1)}, bf16[3,160,768]{2,1,0:T(8,128)(2,1)S(1)}, u32[]{:S(2)}, u32[]{:S(2)}) collective-permute-start(bf16[3,160,768]{2,1,0:T(8,128)(2,1)S(1)} %collective-permute-done.2.refs_2_), channel_id=1, source_target_pairs={{0,4},{1,5},{2,6},{3,7},{8,12},{9,13},{10,14},{11,15},{16,20},{17,... | collective-permute-start | bytes 2211848 | tf_op jit(solution)/shard_map/ppermute | solution.py:318
  34.7 0.0 collective-permute-done.6.refs_4_
  34.8 0.2 collective-permute-done.7.refs_5_
  35.0 1.3 %collective-permute-done.5.refs_3_ = bf16[3,160,768]{2,1,0:T(8,128)(2,1)S(1)} collective-permute-done((bf16[3,160,768]{2,1,0:T(8,128)(2,1)S(1)}, bf16[3,160,768]{2,1,0:T(8,128)(2,1)S(1)}, u32[]{:S(2)}, u32[]{:S(2)}) %collective-permute-start.5) | collective-permute-done | bytes 737312 | tf_op jit(solution)/shard_map/ppermute | solution.py:318
  36.3 0.0 copy-done.1
  36.3 7.5 %control.2 = (bf16[3,160,768]{2,1,0:T(8,128)(2,1)S(1)}, f32[3,160,768]{2,1,0:T(8,128)S(1)}, f32[3,1,768]{2,1,0:T(1,128)S(1)}, f32[3,640,768]{2,1,0:T(8,128)S(1)}) custom-call(bf16[3,160,768]{2,1,0:T(8,128)(2,1)S(1)} %collective-permute-done.1.refs_0_, bf16[3,160,768]{2,1,0:T(8,128)(2,1)S(1)} %broadcast_select_fusion.refs_1_, ...), custom_call_target="tpu_custom_call" | custom-call | tf_op jit(solution)/shard_map/control/pallas_call | solution.py:365
  43.8 1.9 %collective-permute-start.10 = (bf16[3,160,768]{2,1,0:T(8,128)(2,1)S(1)}, bf16[3,160,768]{2,1,0:T(8,128)(2,1)S(1)}, u32[]{:S(2)}, u32[]{:S(2)}) collective-permute-start(bf16[3,160,768]{2,1,0:T(8,128)(2,1)S(1)} %get-tuple-element.39.refs_10_.refs_1_), channel_id=1, source_target_pairs={{0,1},{2,3},{8,9},{10,11},{1,0},{3,2},{9,8},{11,10},{5,6},{13,14},... | collective-permute-start | bytes 2211848 | tf_op jit(solution)/shard_map/ppermute | solution.py:318
  45.7 2.8 %tangent.2.refs_1_ = bf16[3,168,768]{2,1,0:T(8,128)(2,1)S(1)} custom-call(bf16[3,160,768]{2,1,0:T(8,128)(2,1)S(1)} %bitcast.11, f32[3,160,768]{2,1,0:T(8,128)S(1)} %conv.1.refs_1_, f32[160,128]{1,0:T(8,128)S(1)} %get-tuple-element.29.refs_7_.refs_2_.refs_4_, bf16[640,176]{1,0:T(8,128)(2,1)S(1)} %get-tuple-element.30.refs_9_.refs_3_.refs_6_.refs_5_, ...), custom_call_target="tpu_custom_call" | custom-call | tf_op jit(solution)/shard_map/tangent/pallas_call | solution.py:386
  48.6 2.7 %collective-permute-start.9 = (bf16[3,168,768]{2,1,0:T(8,128)(2,1)S(1)}, bf16[3,168,768]{2,1,0:T(8,128)(2,1)S(1)}, u32[]{:S(2)}, u32[]{:S(2)}) collective-permute-start(bf16[3,168,768]{2,1,0:T(8,128)(2,1)S(1)} %tangent.2.refs_1_), channel_id=1, source_target_pairs={{9,10},{10,9},{4,5},{6,7},{12,13},{14,15},{5,4},{7,6},{13,12},{15,... | collective-permute-start | bytes 2322440 | tf_op jit(solution)/shard_map/ppermute | solution.py:318
  51.3 2.1 %collective-permute-start.8 = (bf16[3,168,768]{2,1,0:T(8,128)(2,1)S(1)}, bf16[3,168,768]{2,1,0:T(8,128)(2,1)S(1)}, u32[]{:S(2)}, u32[]{:S(2)}) collective-permute-start(bf16[3,168,768]{2,1,0:T(8,128)(2,1)S(1)} %tangent.2.refs_1_), channel_id=1, source_target_pairs={{8,9},{10,11},{9,8},{11,10},{5,6},{13,14},{6,5},{14,13},{24,25},{2... | collective-permute-start | bytes 2322440 | tf_op jit(solution)/shard_map/ppermute | solution.py:318
  53.5 6.8 %collective-permute-done.10.refs_0_ = bf16[3,160,768]{2,1,0:T(8,128)(2,1)S(1)} collective-permute-done((bf16[3,160,768]{2,1,0:T(8,128)(2,1)S(1)}, bf16[3,160,768]{2,1,0:T(8,128)(2,1)S(1)}, u32[]{:S(2)}, u32[]{:S(2)}) %collective-permute-start.10) | collective-permute-done | bytes 737312 | tf_op jit(solution)/shard_map/ppermute | solution.py:318
  60.3 0.0 collective-permute-start.11
  60.3 2.2 %collective-permute-done.11.refs_2_ = bf16[3,160,768]{2,1,0:T(8,128)(2,1)S(1)} collective-permute-done((bf16[3,160,768]{2,1,0:T(8,128)(2,1)S(1)}, bf16[3,160,768]{2,1,0:T(8,128)(2,1)S(1)}, u32[]{:S(2)}, u32[]{:S(2)}) %collective-permute-start.11) | collective-permute-done | bytes 737312 | tf_op jit(solution)/shard_map/ppermute | solution.py:318
  62.5 7.4 %control.3 = (bf16[3,160,768]{2,1,0:T(8,128)(2,1)S(1)}, f32[3,160,768]{2,1,0:T(8,128)S(1)}, f32[3,1,768]{2,1,0:T(1,128)S(1)}, f32[3,640,768]{2,1,0:T(8,128)S(1)}) custom-call(bf16[3,160,768]{2,1,0:T(8,128)(2,1)S(1)} %collective-permute-done.10.refs_0_, bf16[3,160,768]{2,1,0:T(8,128)(2,1)S(1)} %get-tuple-element.39.refs_10_.refs_1_, ...), custom_call_target="tpu_custom_call" | custom-call | tf_op jit(solution)/shard_map/control/pallas_call | solution.py:365
  69.9 0.8 %collective-permute-done.9.refs_2_ = bf16[3,168,768]{2,1,0:T(8,128)(2,1)S(1)} collective-permute-done((bf16[3,168,768]{2,1,0:T(8,128)(2,1)S(1)}, bf16[3,168,768]{2,1,0:T(8,128)(2,1)S(1)}, u32[]{:S(2)}, u32[]{:S(2)}) %collective-permute-start.9) | collective-permute-done | bytes 774176 | tf_op jit(solution)/shard_map/ppermute | solution.py:318
  70.7 3.1 %collective-permute-done.8.refs_0_ = bf16[3,168,768]{2,1,0:T(8,128)(2,1)S(1)} collective-permute-done((bf16[3,168,768]{2,1,0:T(8,128)(2,1)S(1)}, bf16[3,168,768]{2,1,0:T(8,128)(2,1)S(1)}, u32[]{:S(2)}, u32[]{:S(2)}) %collective-permute-start.8) | collective-permute-done | bytes 774176 | tf_op jit(solution)/shard_map/ppermute | solution.py:318
  73.7 6.6 %tangent.3 = bf16[3,160,768]{2,1,0:T(8,128)(2,1)} custom-call(bf16[3,168,768]{2,1,0:T(8,128)(2,1)S(1)} %collective-permute-done.8.refs_0_, bf16[3,168,768]{2,1,0:T(8,128)(2,1)S(1)} %tangent.2.refs_1_, bf16[3,168,768]{2,1,0:T(8,128)(2,1)S(1)} %collective-permute-done.9.refs_2_, bf16[3,7,160,144]{3,2,1,0:T(8,128)(2,1)S(1)} %get-tuple-element.27.taps.refs_6_.refs_3_, ...), custom_call_target="tpu_custom_call" | custom-call | tf_op jit(solution)/shard_map/tangent/pallas_call | solution.py:386
Async XLA Ops:
  0.0 20.5 %copy-start.2 = (bf16[768,768]{1,0:T(8,128)(2,1)S(1)}, bf16[768,768]{1,0:T(8,128)(2,1)}, u32[]{:S(2)}) copy-start(bf16[768,768]{1,0:T(8,128)(2,1)} %constant.11.clone.refs_1_) | copy-start | bytes 3538948
  0.0 14.1 %collective-permute-start = (bf16[3,160,768]{2,1,0:T(8,128)(2,1)}, bf16[3,160,768]{2,1,0:T(8,128)(2,1)S(1)}, u32[]{:S(2)}, u32[]{:S(2)}) collective-permute-start(bf16[3,160,768]{2,1,0:T(8,128)(2,1)} %bitcast.7), channel_id=1, source_target_pairs={{0,8},{1,9},{2,10},{3,11},{16,24},{17,25},{18,26},{19,27}} | collective-permute-start | bytes 2211848 | tf_op jit(solution)/shard_map/ppermute | solution.py:318
  1.4 24.0 %collective-permute-start.4 = (bf16[3,160,768]{2,1,0:T(8,128)(2,1)}, bf16[3,160,768]{2,1,0:T(8,128)(2,1)S(1)}, u32[]{:S(2)}, u32[]{:S(2)}) collective-permute-start(bf16[3,160,768]{2,1,0:T(8,128)(2,1)} %bitcast.8), channel_id=1, source_target_pairs={{9,10},{10,9},{4,5},{6,7},{12,13},{14,15},{5,4},{7,6},{13,12},{15,... | collective-permute-start | bytes 2211848 | tf_op jit(solution)/shard_map/ppermute | solution.py:318
  4.9 20.6 %collective-permute-start.3 = (bf16[3,160,768]{2,1,0:T(8,128)(2,1)}, bf16[3,160,768]{2,1,0:T(8,128)(2,1)S(1)}, u32[]{:S(2)}, u32[]{:S(2)}) collective-permute-start(bf16[3,160,768]{2,1,0:T(8,128)(2,1)} %bitcast.9), channel_id=1, source_target_pairs={{8,9},{10,11},{9,8},{11,10},{5,6},{13,14},{6,5},{14,13},{24,25},{2... | collective-permute-start | bytes 2211848 | tf_op jit(solution)/shard_map/ppermute | solution.py:318
  6.9 0.9 %copy-start.3 = (bf16[160,640]{1,0:T(8,128)(2,1)S(1)}, bf16[160,640]{1,0:T(8,128)(2,1)}, u32[]{:S(2)}) copy-start(bf16[160,640]{1,0:T(8,128)(2,1)} %refs_3_.1) | copy-start | bytes 614404
  7.8 0.8 %copy-start.4 = (f32[7,7,160]{2,1,0:T(8,128)S(1)}, f32[7,7,160]{2,1,0:T(8,128)}, u32[]{:S(2)}) copy-start(f32[7,7,160]{2,1,0:T(8,128)} %refs_0_.2) | copy-start | bytes 94084
  8.6 0.7 copy-start.5
  9.3 0.7 copy-start.6
  10.0 0.7 copy-start.7
  10.7 0.7 copy-start.8
  11.4 9.1 %copy-start.9 = (s32[12]{0:T(128)S(1)}, s32[12]{0:T(128)}, u32[]{:S(2)}) copy-start(s32[12]{0:T(128)} %refs_0_.3) | copy-start | bytes 148
  15.3 10.2 %copy-start = (bf16[1,3,160,768]{3,2,1,0:T(8,128)(2,1)S(1)}, bf16[1,3,160,768]{3,2,1,0:T(8,128)(2,1)}, u32[]{:S(2)}) copy-start(bf16[1,3,160,768]{3,2,1,0:T(8,128)(2,1)} %param.10) | copy-start | bytes 2211844
  15.3 15.5 %collective-permute-start.2 = (bf16[3,160,768]{2,1,0:T(8,128)(2,1)S(1)}, bf16[3,160,768]{2,1,0:T(8,128)(2,1)S(1)}, u32[]{:S(2)}, u32[]{:S(2)}) collective-permute-start(bf16[3,160,768]{2,1,0:T(8,128)(2,1)S(1)} %broadcast_select_fusion.refs_1_), channel_id=1, source_target_pairs={{1,2},{9,10},{2,1},{10,9},{17,18},{25,26},{18,17},{26,25}} | collective-permute-start | bytes 2211848 | tf_op jit(solution)/shard_map/ppermute | solution.py:318
  18.5 13.4 %collective-permute-start.1 = (bf16[3,160,768]{2,1,0:T(8,128)(2,1)S(1)}, bf16[3,160,768]{2,1,0:T(8,128)(2,1)S(1)}, u32[]{:S(2)}, u32[]{:S(2)}) collective-permute-start(bf16[3,160,768]{2,1,0:T(8,128)(2,1)S(1)} %broadcast_select_fusion.refs_1_), channel_id=1, source_target_pairs={{0,1},{2,3},{8,9},{10,11},{1,0},{3,2},{9,8},{11,10},{16,17},{18,19... | collective-permute-start | bytes 2211848 | tf_op jit(solution)/shard_map/ppermute | solution.py:318
  24.0 12.4 %copy-start.1 = (bf16[640,160]{0,1:T(8,128)(2,1)S(1)}, bf16[640,160]{0,1:T(8,128)(2,1)}, u32[]{:S(2)}) copy-start(bf16[640,160]{0,1:T(8,128)(2,1)} %param.18) | copy-start | bytes 614404
  24.0 10.8 %collective-permute-start.6 = (bf16[3,160,768]{2,1,0:T(8,128)(2,1)S(1)}, bf16[3,160,768]{2,1,0:T(8,128)(2,1)S(1)}, u32[]{:S(2)}, u32[]{:S(2)}) collective-permute-start(bf16[3,160,768]{2,1,0:T(8,128)(2,1)S(1)} %broadcast_select_fusion.refs_1_), channel_id=1, source_target_pairs={{0,4},{1,5},{2,6},{3,7},{8,12},{9,13},{10,14},{11,15},{16,20},{17,... | collective-permute-start | bytes 2211848 | tf_op jit(solution)/shard_map/ppermute | solution.py:318
  31.9 3.1 %collective-permute-start.7 = (bf16[3,160,768]{2,1,0:T(8,128)(2,1)S(1)}, bf16[3,160,768]{2,1,0:T(8,128)(2,1)S(1)}, u32[]{:S(2)}, u32[]{:S(2)}) collective-permute-start(bf16[3,160,768]{2,1,0:T(8,128)(2,1)S(1)} %collective-permute-done.1.refs_0_), channel_id=1, source_target_pairs={{0,4},{1,5},{2,6},{3,7},{8,12},{9,13},{10,14},{11,15},{16,20},{17,... | collective-permute-start | bytes 2211848 | tf_op jit(solution)/shard_map/ppermute | solution.py:318
  33.2 3.1 %collective-permute-start.5 = (bf16[3,160,768]{2,1,0:T(8,128)(2,1)S(1)}, bf16[3,160,768]{2,1,0:T(8,128)(2,1)S(1)}, u32[]{:S(2)}, u32[]{:S(2)}) collective-permute-start(bf16[3,160,768]{2,1,0:T(8,128)(2,1)S(1)} %collective-permute-done.2.refs_2_), channel_id=1, source_target_pairs={{0,4},{1,5},{2,6},{3,7},{8,12},{9,13},{10,14},{11,15},{16,20},{17,... | collective-permute-start | bytes 2211848 | tf_op jit(solution)/shard_map/ppermute | solution.py:318
  43.8 16.5 %collective-permute-start.10 = (bf16[3,160,768]{2,1,0:T(8,128)(2,1)S(1)}, bf16[3,160,768]{2,1,0:T(8,128)(2,1)S(1)}, u32[]{:S(2)}, u32[]{:S(2)}) collective-permute-start(bf16[3,160,768]{2,1,0:T(8,128)(2,1)S(1)} %get-tuple-element.39.refs_10_.refs_1_), channel_id=1, source_target_pairs={{0,1},{2,3},{8,9},{10,11},{1,0},{3,2},{9,8},{11,10},{5,6},{13,14},... | collective-permute-start | bytes 2211848 | tf_op jit(solution)/shard_map/ppermute | solution.py:318
  48.6 22.1 %collective-permute-start.9 = (bf16[3,168,768]{2,1,0:T(8,128)(2,1)S(1)}, bf16[3,168,768]{2,1,0:T(8,128)(2,1)S(1)}, u32[]{:S(2)}, u32[]{:S(2)}) collective-permute-start(bf16[3,168,768]{2,1,0:T(8,128)(2,1)S(1)} %tangent.2.refs_1_), channel_id=1, source_target_pairs={{9,10},{10,9},{4,5},{6,7},{12,13},{14,15},{5,4},{7,6},{13,12},{15,... | collective-permute-start | bytes 2322440 | tf_op jit(solution)/shard_map/ppermute | solution.py:318
  51.3 22.4 %collective-permute-start.8 = (bf16[3,168,768]{2,1,0:T(8,128)(2,1)S(1)}, bf16[3,168,768]{2,1,0:T(8,128)(2,1)S(1)}, u32[]{:S(2)}, u32[]{:S(2)}) collective-permute-start(bf16[3,168,768]{2,1,0:T(8,128)(2,1)S(1)} %tangent.2.refs_1_), channel_id=1, source_target_pairs={{8,9},{10,11},{9,8},{11,10},{5,6},{13,14},{6,5},{14,13},{24,25},{2... | collective-permute-start | bytes 2322440 | tf_op jit(solution)/shard_map/ppermute | solution.py:318
  60.3 2.2 %collective-permute-start.11 = (bf16[3,160,768]{2,1,0:T(8,128)(2,1)S(1)}, bf16[3,160,768]{2,1,0:T(8,128)(2,1)S(1)}, u32[]{:S(2)}, u32[]{:S(2)}) collective-permute-start(bf16[3,160,768]{2,1,0:T(8,128)(2,1)S(1)} %collective-permute-done.10.refs_0_), channel_id=1, source_target_pairs={{0,4},{1,5},{2,6},{3,7},{8,12},{9,13},{10,14},{11,15},{4,0},{5,1},... | collective-permute-start | bytes 2211848 | tf_op jit(solution)/shard_map/ppermute | solution.py:318

commit v5 on v4

--- a/solution.py
+++ b/solution.py
@@ -104,12 +104,12 @@
                 out[r] = (across == along).astype(f32).astype(bf16)
 
 
-def convolve(near, own, far, taps, out):
+def convolve(first, own, second, taps, out, most=10):
     rows, channels, width = out.shape
 
     def group(b, _):
         at = pl.ds(pl.multiple_of(b * GROUP, GROUP), GROUP)
-        field = jnp.concatenate([near(at), own(at), far(at)], axis=0)
+        field = jnp.concatenate([first(at), own(at), second(at)], axis=0)
         field = field.reshape((rows + 2 * HALO) * GROUP, width)
         parts = jnp.dot(taps[:, :, at, :].reshape(rows * TAPS * GROUP, field.shape[0]), field, preferred_element_type=f32)
         for r in range(rows):
@@ -122,7 +122,7 @@
         return 0
 
     groups = channels // GROUP
-    lax.fori_loop(0, groups, group, 0, unroll=unroll(groups, 5))
+    lax.fori_loop(0, groups, group, 0, unroll=unroll(groups, most))
 
 
 def read(ref):
@@ -133,14 +133,27 @@
     return lambda at: jnp.where(odd, other[:, at, :], first[:, at, :])
 
 
-def pipeline(tiles, first, second, third):
-    for i in range(tiles + 2):
-        if i < tiles:
-            first(i)
-        if 1 <= i <= tiles:
-            second(i - 1)
-        if i >= 2:
-            third(i - 2)
+def pipeline(rows, across, compact, first, second, third):
+    def run(tiles):
+        for i in range(len(tiles) + 2):
+            for stage, lag in ((first, 0), (second, 1), (third, 2)):
+                if lag <= i < len(tiles) + lag:
+                    r, c = tiles[i - lag]
+                    stage((i - lag) % 2, r, slice(c * LANES, (c + 1) * LANES))
+
+    if compact:
+
+        def one(r, _):
+            run([(r, c) for c in range(across)])
+            return 0
+
+        lax.fori_loop(0, rows, one, 0)
+    else:
+        run([(r, c) for r in range(rows) for c in range(across)])
+
+
+def row_of(r, channels):
+    return pl.ds(pl.multiple_of(r * channels, GROUP), channels)
 
 
 def add_bias_rows(normed, channels):
@@ -151,7 +164,7 @@
 def polar_filter(raw, filters, out, r):
     channels = raw.shape[0] // filters.shape[0]
     out[r, :channels, :] = jnp.dot(
-        raw[r * channels : (r + 1) * channels, :], filters[r], preferred_element_type=f32
+        raw[row_of(r, channels), :], filters[r], preferred_element_type=f32
     ).astype(bf16)
 
 
@@ -174,14 +187,10 @@
     blocks = [read(first_halo), read(own), read(second_halo)]
     if other is not None:
         blocks = [choose(odd, a, b) for a, b in zip((first_halo, own, second_halo), other)]
-    convolve(*blocks, taps, conv)
+    convolve(*blocks, taps, conv, 10 if other is not None else 2)
     across = width // LANES
 
-    def place(i):
-        return i // across, slice(i % across * LANES, (i % across + 1) * LANES)
-
-    def first(i):
-        r, at = place(i)
+    def first(slot, r, at):
         for w in range(0, LANES, 128):
             here, there = slice(at.start + w, at.start + w + 128), slice(w, w + 128)
             value = conv[r, :, here]
@@ -190,35 +199,33 @@
             unit = centered * scale
             unit_out[r, :, here] = unit
             scale_out[r, :, here] = scale
-            normed[i % 2][:channels, there] = (unit * gain[...] + bias[...]).astype(bf16)
-        hidden[i % 2][...] = jnp.dot(w_in[...], normed[i % 2][...], preferred_element_type=f32)
-
-    def pair(i):
-        r, at = place(i)
+            normed[slot][:channels, there] = (unit * gain[...] + bias[...]).astype(bf16)
+        hidden[slot][...] = jnp.dot(w_in[...], normed[slot][...], preferred_element_type=f32)
+
+    def pair(slot, r, at):
         for c in range(0, hid, CHUNK):
-            h = hidden[i % 2][c : c + CHUNK, :]
+            h = hidden[slot][c : c + CHUNK, :]
             square = h * h
             t = jnp.tanh(h * (gelu_scale + (gelu_scale * gelu_cubic) * square))
             half = 0.5 + 0.5 * t
-            act[i % 2][c : c + CHUNK, :] = (h * half).astype(bf16)
+            act[slot][c : c + CHUNK, :] = (h * half).astype(bf16)
             lean = h * (2.0 * gelu_scale + (6.0 * gelu_scale * gelu_cubic) * square)
             slope_out[r, c : c + CHUNK, at] = half * (1.0 + (1.0 - half) * lean)
 
-    def third(i):
-        r, at = place(i)
-        update = jnp.dot(w_out[...], act[i % 2][...], preferred_element_type=f32)
+    def third(slot, r, at):
+        update = jnp.dot(w_out[...], act[slot][...], preferred_element_type=f32)
         field = own[r, :, at]
         if other is not None:
             field = jnp.where(odd, other[1][r, :, at], field)
-        raw[r * channels : (r + 1) * channels, at] = (land[r : r + 1, at] * (field.astype(f32) + update)).astype(bf16)
-        if i % across == across - 1:
+        raw[row_of(r, channels), at] = (land[pl.ds(r, 1), at] * (field.astype(f32) + update)).astype(bf16)
+        if at.stop == width:
             polar_filter(raw, filters, out, r)
 
-    pipeline(rows * across, first, pair, third)
-
-
-def conv_kernel(near, own, far, taps, out):
-    convolve(read(near), read(own), read(far), taps, out)
+    pipeline(rows, across, other is None, first, pair, third)
+
+
+def conv_kernel(first, own, second, taps, out):
+    convolve(read(first), read(own), read(second), taps, out, 5)
 
 
 def tangent_kernel(ready, *refs):
@@ -239,32 +246,26 @@
     across = width // LANES
     is_control = lax.axis_index("mem") == 0
 
-    def place(i):
-        return i // across, slice(i % across * LANES, (i % across + 1) * LANES)
-
-    def first(i):
-        r, at = place(i)
+    def first(slot, r, at):
         for w in range(0, LANES, 128):
             here, there = slice(at.start + w, at.start + w + 128), slice(w, w + 128)
             value = conv[r, :, here]
             unit = unit_in[r, :, here]
             average = jnp.mean(value, axis=0, keepdims=True)
             along = jnp.mean(value * unit, axis=0, keepdims=True)
-            normed[i % 2][:, there] = (gain[...] * scale_in[r, :, here] * (value - average - unit * along)).astype(bf16)
-        hidden[i % 2][...] = jnp.dot(w_in[:, :channels], normed[i % 2][...], preferred_element_type=f32)
-
-    def mix(i):
-        r, at = place(i)
+            normed[slot][:, there] = (gain[...] * scale_in[r, :, here] * (value - average - unit * along)).astype(bf16)
+        hidden[slot][...] = jnp.dot(w_in[:, :channels], normed[slot][...], preferred_element_type=f32)
+
+    def mix(slot, r, at):
         for c in range(0, hid, CHUNK):
-            act[i % 2][c : c + CHUNK, :] = (slope_in[r, c : c + CHUNK, at] * hidden[i % 2][c : c + CHUNK, :]).astype(bf16)
-
-    def third(i):
-        r, at = place(i)
-        update = jnp.dot(w_out[...], act[i % 2][...], preferred_element_type=f32)
-        raw[r * channels : (r + 1) * channels, at] = (
-            land[r : r + 1, at] * (own[r, :channels, at].astype(f32) + update)
+            act[slot][c : c + CHUNK, :] = (slope_in[r, c : c + CHUNK, at] * hidden[slot][c : c + CHUNK, :]).astype(bf16)
+
+    def third(slot, r, at):
+        update = jnp.dot(w_out[...], act[slot][...], preferred_element_type=f32)
+        raw[row_of(r, channels), at] = (
+            land[pl.ds(r, 1), at] * (own[r, :channels, at].astype(f32) + update)
         ).astype(bf16)
-        if i % across == across - 1:
+        if at.stop == width:
             polar_filter(raw, filters, out, r)
 
     if out.shape[1] > channels:
@@ -278,7 +279,7 @@
     def _():
         if not ready:
             convolve(read(near), read(own), read(far), taps, conv)
-        pipeline(rows * across, first, mix, third)
+        pipeline(rows, across, False, first, mix, third)
 
 
 def scratch(rows, channels, width, hid, bias_rows, conv=True):

time: 80.9 us -> 79.3 us (0.980)
  waiting for transfers between devices: 18 us -> 16.7 us
    ppermute x12, waiting for transfers between devices: 18 us -> 16.7 us  [send(): lax.ppermute(block, ('mem', 'lat'), [(a * bands + i, b * bands + j) for (...]
    pallas_call x2, Pallas kernels: 9.45 us -> 8.47 us  [tangent_step(): pl.pallas_call(lambda *refs: tangent_kernel(ready, *refs), out_shape=shap...]
    pallas_call x2, Pallas kernels: 14.8 us -> 15.6 us  [control_step(): pl.pallas_call(control_kernel, out_shape=(field, shape(rows, channels, wi...]
  transfers between devices with their start and end apart: 12 -> 12, of which waited for: 8 -> 7; matrix products, arithmetic and copies ran while one was open for 1% -> 2% of each run, Pallas kernels for 24% -> 26%
where the time goes in v5:
time: 79.3 us; the launch traced here: 78.7 us
  Pallas kernels  33.1 us (42%)
  starting transfers between devices  22.9 us (29%)
  waiting for transfers between devices  16.7 us (21%)
  local copies, waits for them, and re-layouts  4.51 us (6%)
  other arithmetic  1.2 us (2%)
    ppermute x12, starting transfers between devices, send(): lax.ppermute(block, ('mem', 'lat'), [(a * bands + i, b * bands + j) for (...  22.9 us
    ppermute x12, waiting for transfers between devices, send(): lax.ppermute(block, ('mem', 'lat'), [(a * bands + i, b * bands + j) for (...  16.7 us
    pallas_call x2, Pallas kernels, control_step(): pl.pallas_call(control_kernel, out_shape=(field, shape(rows, channels, wi...  15.6 us
    pallas_call x2, Pallas kernels, tangent_step(): pl.pallas_call(lambda *refs: tangent_kernel(ready, *refs), out_shape=shap...  8.47 us
    unnamed x20, local copies, waits for them, and re-layouts  4.51 us
    pallas_call x1, Pallas kernels, per_device(): pl.pallas_call(lambda *refs: filter_kernel(bands, *refs), out_shape=shape...  3.49 us
    pallas_call x1, Pallas kernels, conv_step(): pl.pallas_call(conv_kernel, out_shape=shape(rows, channels, width), in_sp...  2.85 us
    pallas_call x1, Pallas kernels, per_device(): pl.pallas_call(prepare_kernel, out_shape=(shape(rows, TAPS, channels, (ro...  2.68 us
  transfers between devices with their start and end apart: 12, of which 7 were waited for; matrix products, arithmetic and copies ran while one was open for 2% of the time, Pallas kernels for 26%

profile of v5, /device:TPU:10, one launch (start us, length us, event | category | flops | bytes accessed | tf_op | source)
XLA Modules:
  0.0 78.7 jit_solution(2662435405736515004)
XLA Ops:
  0.0 0.0 copy-start.2
  0.0 1.4 %collective-permute-start = (bf16[3,160,768]{2,1,0:T(8,128)(2,1)}, bf16[3,160,768]{2,1,0:T(8,128)(2,1)S(1)}, u32[]{:S(2)}, u32[]{:S(2)}) collective-permute-start(bf16[3,160,768]{2,1,0:T(8,128)(2,1)} %bitcast.7), channel_id=1, source_target_pairs={{0,8},{1,9},{2,10},{3,11},{16,24},{17,25},{18,26},{19,27}} | collective-permute-start | bytes 2211848 | tf_op jit(solution)/shard_map/ppermute | solution.py:319
  1.4 3.5 %collective-permute-start.4 = (bf16[3,160,768]{2,1,0:T(8,128)(2,1)}, bf16[3,160,768]{2,1,0:T(8,128)(2,1)S(1)}, u32[]{:S(2)}, u32[]{:S(2)}) collective-permute-start(bf16[3,160,768]{2,1,0:T(8,128)(2,1)} %bitcast.8), channel_id=1, source_target_pairs={{9,10},{10,9},{4,5},{6,7},{12,13},{14,15},{5,4},{7,6},{13,12},{15,... | collective-permute-start | bytes 2211848 | tf_op jit(solution)/shard_map/ppermute | solution.py:319
  4.9 1.9 %collective-permute-start.3 = (bf16[3,160,768]{2,1,0:T(8,128)(2,1)}, bf16[3,160,768]{2,1,0:T(8,128)(2,1)S(1)}, u32[]{:S(2)}, u32[]{:S(2)}) collective-permute-start(bf16[3,160,768]{2,1,0:T(8,128)(2,1)} %bitcast.9), channel_id=1, source_target_pairs={{8,9},{10,11},{9,8},{11,10},{5,6},{13,14},{6,5},{14,13},{24,25},{2... | collective-permute-start | bytes 2211848 | tf_op jit(solution)/shard_map/ppermute | solution.py:319
  6.9 0.0 copy-start.3
  6.9 0.9 %copy-done.3 = bf16[160,640]{1,0:T(8,128)(2,1)S(1)} copy-done((bf16[160,640]{1,0:T(8,128)(2,1)S(1)}, bf16[160,640]{1,0:T(8,128)(2,1)}, u32[]{:S(2)}) %copy-start.3) | copy-done | bytes 204824
  7.8 0.0 copy-start.4
  7.8 0.8 %copy-done.4 = f32[7,7,160]{2,1,0:T(8,128)S(1)} copy-done((f32[7,7,160]{2,1,0:T(8,128)S(1)}, f32[7,7,160]{2,1,0:T(8,128)}, u32[]{:S(2)}) %copy-start.4) | copy-done | bytes 31384
  8.6 0.0 copy-start.5
  8.6 0.7 copy-done.5
  9.3 0.0 copy-start.6
  9.3 0.7 copy-done.6
  10.0 0.0 copy-start.7
  10.0 0.7 copy-done.7
  10.7 0.0 copy-start.8
  10.7 0.7 copy-done.8
  11.4 0.0 copy-start.9
  11.4 2.7 %prepare.1 = (bf16[3,7,160,144]{3,2,1,0:T(8,128)(2,1)S(1)}, f32[160,128]{1,0:T(8,128)S(1)}, f32[160,128]{1,0:T(8,128)S(1)}, bf16[640,176]{1,0:T(8,128)(2,1)S(1)}, f32[3,768]{1,0:T(4,128)S(1)}) custom-call(f32[7,7,160]{2,1,0:T(8,128)S(1)} %copy-done.4, f32[1,160]{1,0:T(1,128)S(1)} %bitcast.17, f32[1,160]{1,0:T(1,128)S(1)} %bitcast.18, ...), custom_call_target="tpu_custom_call" | custom-call | tf_op jit(solution)/shard_map/prepare/pallas_call | solution.py:341
  14.1 0.0 collective-permute-done
  14.1 1.2 %broadcast_select_fusion.refs_1_ = bf16[3,160,768]{2,1,0:T(8,128)(2,1)S(1)} fusion(bf16[3,160,768]{2,1,0:T(8,128)(2,1)S(1)} %collective-permute-done, pred[]{:T(512)S(6)} %and.4, bf16[1,3,160,768]{3,2,1,0:T(8,128)(2,1)} %param.10), kind=kLoop, calls=%fused_computation | loop fusion | flops 368640 | bytes 2211841 | tf_op jit(solution)/shard_map/jit(_where)/select_n | solution.py:402
  15.3 0.0 copy-start
  15.3 3.2 %collective-permute-start.2 = (bf16[3,160,768]{2,1,0:T(8,128)(2,1)S(1)}, bf16[3,160,768]{2,1,0:T(8,128)(2,1)S(1)}, u32[]{:S(2)}, u32[]{:S(2)}) collective-permute-start(bf16[3,160,768]{2,1,0:T(8,128)(2,1)S(1)} %broadcast_select_fusion.refs_1_), channel_id=1, source_target_pairs={{1,2},{9,10},{2,1},{10,9},{17,18},{25,26},{18,17},{26,25}} | collective-permute-start | bytes 2211848 | tf_op jit(solution)/shard_map/ppermute | solution.py:319
  18.5 1.9 %collective-permute-start.1 = (bf16[3,160,768]{2,1,0:T(8,128)(2,1)S(1)}, bf16[3,160,768]{2,1,0:T(8,128)(2,1)S(1)}, u32[]{:S(2)}, u32[]{:S(2)}) collective-permute-start(bf16[3,160,768]{2,1,0:T(8,128)(2,1)S(1)} %broadcast_select_fusion.refs_1_), channel_id=1, source_target_pairs={{0,1},{2,3},{8,9},{10,11},{1,0},{3,2},{9,8},{11,10},{16,17},{18,19... | collective-permute-start | bytes 2211848 | tf_op jit(solution)/shard_map/ppermute | solution.py:319
  20.5 0.0 copy-done.2
  20.5 0.0 copy-done.9
  20.5 3.5 %filters.1.refs_12_.refs_6_.refs_9_.refs_8_ = bf16[3,768,768]{2,1,0:T(8,128)(2,1)S(1)} custom-call(s32[12]{0:T(128)S(1)} %copy-done.9, bf16[768,768]{1,0:T(8,128)(2,1)S(1)} %copy-done.2), custom_call_target="tpu_custom_call" | custom-call | tf_op jit(solution)/shard_map/filters/pallas_call | solution.py:356
  24.0 0.0 copy-start.1
  24.0 1.5 %collective-permute-start.6 = (bf16[3,160,768]{2,1,0:T(8,128)(2,1)S(1)}, bf16[3,160,768]{2,1,0:T(8,128)(2,1)S(1)}, u32[]{:S(2)}, u32[]{:S(2)}) collective-permute-start(bf16[3,160,768]{2,1,0:T(8,128)(2,1)S(1)} %broadcast_select_fusion.refs_1_), channel_id=1, source_target_pairs={{0,4},{1,5},{2,6},{3,7},{8,12},{9,13},{10,14},{11,15},{16,20},{17,... | collective-permute-start | bytes 2211848 | tf_op jit(solution)/shard_map/ppermute | solution.py:319
  25.5 0.0 collective-permute-done.4.second
  25.5 0.0 collective-permute-done.3.first
  25.5 0.0 copy-done
  25.5 2.8 %conv.1.refs_1_ = f32[3,160,768]{2,1,0:T(8,128)S(1)} custom-call(bf16[3,160,768]{2,1,0:T(8,128)(2,1)S(1)} %collective-permute-done.3.first, bf16[3,160,768]{2,1,0:T(8,128)(2,1)S(1)} %bitcast.10, bf16[3,160,768]{2,1,0:T(8,128)(2,1)S(1)} %collective-permute-done.4.second, bf16[3,7,160,144]{3,2,1,0:T(8,128)(2,1)S(1)} %get-tuple-element.27.taps.refs_6_.refs_3_), custom_call_target="tpu_custom_call" | custom-call | tf_op jit(solution)/shard_map/conv/pallas_call | solution.py:377
  28.3 2.4 %collective-permute-done.2.refs_2_ = bf16[3,160,768]{2,1,0:T(8,128)(2,1)S(1)} collective-permute-done((bf16[3,160,768]{2,1,0:T(8,128)(2,1)S(1)}, bf16[3,160,768]{2,1,0:T(8,128)(2,1)S(1)}, u32[]{:S(2)}, u32[]{:S(2)}) %collective-permute-start.2) | collective-permute-done | bytes 737312 | tf_op jit(solution)/shard_map/ppermute | solution.py:319
  30.8 1.1 %collective-permute-done.1.refs_0_ = bf16[3,160,768]{2,1,0:T(8,128)(2,1)S(1)} collective-permute-done((bf16[3,160,768]{2,1,0:T(8,128)(2,1)S(1)}, bf16[3,160,768]{2,1,0:T(8,128)(2,1)S(1)}, u32[]{:S(2)}, u32[]{:S(2)}) %collective-permute-start.1) | collective-permute-done | bytes 737312 | tf_op jit(solution)/shard_map/ppermute | solution.py:319
  31.9 1.3 %collective-permute-start.7 = (bf16[3,160,768]{2,1,0:T(8,128)(2,1)S(1)}, bf16[3,160,768]{2,1,0:T(8,128)(2,1)S(1)}, u32[]{:S(2)}, u32[]{:S(2)}) collective-permute-start(bf16[3,160,768]{2,1,0:T(8,128)(2,1)S(1)} %collective-permute-done.1.refs_0_), channel_id=1, source_target_pairs={{0,4},{1,5},{2,6},{3,7},{8,12},{9,13},{10,14},{11,15},{16,20},{17,... | collective-permute-start | bytes 2211848 | tf_op jit(solution)/shard_map/ppermute | solution.py:319
  33.2 1.5 %collective-permute-start.5 = (bf16[3,160,768]{2,1,0:T(8,128)(2,1)S(1)}, bf16[3,160,768]{2,1,0:T(8,128)(2,1)S(1)}, u32[]{:S(2)}, u32[]{:S(2)}) collective-permute-start(bf16[3,160,768]{2,1,0:T(8,128)(2,1)S(1)} %collective-permute-done.2.refs_2_), channel_id=1, source_target_pairs={{0,4},{1,5},{2,6},{3,7},{8,12},{9,13},{10,14},{11,15},{16,20},{17,... | collective-permute-start | bytes 2211848 | tf_op jit(solution)/shard_map/ppermute | solution.py:319
  34.7 0.0 collective-permute-done.6.refs_4_
  34.8 0.2 collective-permute-done.7.refs_5_
  35.0 1.3 %collective-permute-done.5.refs_3_ = bf16[3,160,768]{2,1,0:T(8,128)(2,1)S(1)} collective-permute-done((bf16[3,160,768]{2,1,0:T(8,128)(2,1)S(1)}, bf16[3,160,768]{2,1,0:T(8,128)(2,1)S(1)}, u32[]{:S(2)}, u32[]{:S(2)}) %collective-permute-start.5) | collective-permute-done | bytes 737312 | tf_op jit(solution)/shard_map/ppermute | solution.py:319
  36.3 0.0 copy-done.1
  36.3 6.8 %control.2 = (bf16[3,160,768]{2,1,0:T(8,128)(2,1)S(1)}, f32[3,160,768]{2,1,0:T(8,128)S(1)}, f32[3,1,768]{2,1,0:T(1,128)S(1)}, f32[3,640,768]{2,1,0:T(8,128)S(1)}) custom-call(bf16[3,160,768]{2,1,0:T(8,128)(2,1)S(1)} %collective-permute-done.1.refs_0_, bf16[3,160,768]{2,1,0:T(8,128)(2,1)S(1)} %broadcast_select_fusion.refs_1_, ...), custom_call_target="tpu_custom_call" | custom-call | tf_op jit(solution)/shard_map/control/pallas_call | solution.py:366
  43.1 1.9 %collective-permute-start.10 = (bf16[3,160,768]{2,1,0:T(8,128)(2,1)S(1)}, bf16[3,160,768]{2,1,0:T(8,128)(2,1)S(1)}, u32[]{:S(2)}, u32[]{:S(2)}) collective-permute-start(bf16[3,160,768]{2,1,0:T(8,128)(2,1)S(1)} %get-tuple-element.39.refs_10_.refs_1_), channel_id=1, source_target_pairs={{0,1},{2,3},{8,9},{10,11},{1,0},{3,2},{9,8},{11,10},{5,6},{13,14},... | collective-permute-start | bytes 2211848 | tf_op jit(solution)/shard_map/ppermute | solution.py:319
  45.1 2.8 %tangent.2.refs_1_ = bf16[3,168,768]{2,1,0:T(8,128)(2,1)S(1)} custom-call(bf16[3,160,768]{2,1,0:T(8,128)(2,1)S(1)} %bitcast.11, f32[3,160,768]{2,1,0:T(8,128)S(1)} %conv.1.refs_1_, f32[160,128]{1,0:T(8,128)S(1)} %get-tuple-element.29.refs_7_.refs_2_.refs_4_, bf16[640,176]{1,0:T(8,128)(2,1)S(1)} %get-tuple-element.30.refs_9_.refs_3_.refs_6_.refs_5_, ...), custom_call_target="tpu_custom_call" | custom-call | tf_op jit(solution)/shard_map/tangent/pallas_call | solution.py:387
  47.9 2.7 %collective-permute-start.9 = (bf16[3,168,768]{2,1,0:T(8,128)(2,1)S(1)}, bf16[3,168,768]{2,1,0:T(8,128)(2,1)S(1)}, u32[]{:S(2)}, u32[]{:S(2)}) collective-permute-start(bf16[3,168,768]{2,1,0:T(8,128)(2,1)S(1)} %tangent.2.refs_1_), channel_id=1, source_target_pairs={{9,10},{10,9},{4,5},{6,7},{12,13},{14,15},{5,4},{7,6},{13,12},{15,... | collective-permute-start | bytes 2322440 | tf_op jit(solution)/shard_map/ppermute | solution.py:319
  50.7 1.9 %collective-permute-start.8 = (bf16[3,168,768]{2,1,0:T(8,128)(2,1)S(1)}, bf16[3,168,768]{2,1,0:T(8,128)(2,1)S(1)}, u32[]{:S(2)}, u32[]{:S(2)}) collective-permute-start(bf16[3,168,768]{2,1,0:T(8,128)(2,1)S(1)} %tangent.2.refs_1_), channel_id=1, source_target_pairs={{8,9},{10,11},{9,8},{11,10},{5,6},{13,14},{6,5},{14,13},{24,25},{2... | collective-permute-start | bytes 2322440 | tf_op jit(solution)/shard_map/ppermute | solution.py:319
  52.6 7.0 %collective-permute-done.10.refs_0_ = bf16[3,160,768]{2,1,0:T(8,128)(2,1)S(1)} collective-permute-done((bf16[3,160,768]{2,1,0:T(8,128)(2,1)S(1)}, bf16[3,160,768]{2,1,0:T(8,128)(2,1)S(1)}, u32[]{:S(2)}, u32[]{:S(2)}) %collective-permute-start.10) | collective-permute-done | bytes 737312 | tf_op jit(solution)/shard_map/ppermute | solution.py:319
  59.6 0.0 collective-permute-start.11
  59.6 2.2 %collective-permute-done.11.refs_2_ = bf16[3,160,768]{2,1,0:T(8,128)(2,1)S(1)} collective-permute-done((bf16[3,160,768]{2,1,0:T(8,128)(2,1)S(1)}, bf16[3,160,768]{2,1,0:T(8,128)(2,1)S(1)}, u32[]{:S(2)}, u32[]{:S(2)}) %collective-permute-start.11) | collective-permute-done | bytes 737312 | tf_op jit(solution)/shard_map/ppermute | solution.py:319
  61.8 8.9 %control.3 = (bf16[3,160,768]{2,1,0:T(8,128)(2,1)S(1)}, f32[3,160,768]{2,1,0:T(8,128)S(1)}, f32[3,1,768]{2,1,0:T(1,128)S(1)}, f32[3,640,768]{2,1,0:T(8,128)S(1)}) custom-call(bf16[3,160,768]{2,1,0:T(8,128)(2,1)S(1)} %collective-permute-done.10.refs_0_, bf16[3,160,768]{2,1,0:T(8,128)(2,1)S(1)} %get-tuple-element.39.refs_10_.refs_1_, ...), custom_call_target="tpu_custom_call" | custom-call | tf_op jit(solution)/shard_map/control/pallas_call | solution.py:366
  70.7 0.0 collective-permute-done.9.refs_2_
  70.7 2.4 %collective-permute-done.8.refs_0_ = bf16[3,168,768]{2,1,0:T(8,128)(2,1)S(1)} collective-permute-done((bf16[3,168,768]{2,1,0:T(8,128)(2,1)S(1)}, bf16[3,168,768]{2,1,0:T(8,128)(2,1)S(1)}, u32[]{:S(2)}, u32[]{:S(2)}) %collective-permute-start.8) | collective-permute-done | bytes 774176 | tf_op jit(solution)/shard_map/ppermute | solution.py:319
  73.1 5.6 %tangent.3 = bf16[3,160,768]{2,1,0:T(8,128)(2,1)} custom-call(bf16[3,168,768]{2,1,0:T(8,128)(2,1)S(1)} %collective-permute-done.8.refs_0_, bf16[3,168,768]{2,1,0:T(8,128)(2,1)S(1)} %tangent.2.refs_1_, bf16[3,168,768]{2,1,0:T(8,128)(2,1)S(1)} %collective-permute-done.9.refs_2_, bf16[3,7,160,144]{3,2,1,0:T(8,128)(2,1)S(1)} %get-tuple-element.27.taps.refs_6_.refs_3_, ...), custom_call_target="tpu_custom_call" | custom-call | tf_op jit(solution)/shard_map/tangent/pallas_call | solution.py:387
Async XLA Ops:
  0.0 20.5 %copy-start.2 = (bf16[768,768]{1,0:T(8,128)(2,1)S(1)}, bf16[768,768]{1,0:T(8,128)(2,1)}, u32[]{:S(2)}) copy-start(bf16[768,768]{1,0:T(8,128)(2,1)} %constant.11.clone.refs_1_) | copy-start | bytes 3538948
  0.0 14.1 %collective-permute-start = (bf16[3,160,768]{2,1,0:T(8,128)(2,1)}, bf16[3,160,768]{2,1,0:T(8,128)(2,1)S(1)}, u32[]{:S(2)}, u32[]{:S(2)}) collective-permute-start(bf16[3,160,768]{2,1,0:T(8,128)(2,1)} %bitcast.7), channel_id=1, source_target_pairs={{0,8},{1,9},{2,10},{3,11},{16,24},{17,25},{18,26},{19,27}} | collective-permute-start | bytes 2211848 | tf_op jit(solution)/shard_map/ppermute | solution.py:319
  1.4 24.0 %collective-permute-start.4 = (bf16[3,160,768]{2,1,0:T(8,128)(2,1)}, bf16[3,160,768]{2,1,0:T(8,128)(2,1)S(1)}, u32[]{:S(2)}, u32[]{:S(2)}) collective-permute-start(bf16[3,160,768]{2,1,0:T(8,128)(2,1)} %bitcast.8), channel_id=1, source_target_pairs={{9,10},{10,9},{4,5},{6,7},{12,13},{14,15},{5,4},{7,6},{13,12},{15,... | collective-permute-start | bytes 2211848 | tf_op jit(solution)/shard_map/ppermute | solution.py:319
  4.9 20.6 %collective-permute-start.3 = (bf16[3,160,768]{2,1,0:T(8,128)(2,1)}, bf16[3,160,768]{2,1,0:T(8,128)(2,1)S(1)}, u32[]{:S(2)}, u32[]{:S(2)}) collective-permute-start(bf16[3,160,768]{2,1,0:T(8,128)(2,1)} %bitcast.9), channel_id=1, source_target_pairs={{8,9},{10,11},{9,8},{11,10},{5,6},{13,14},{6,5},{14,13},{24,25},{2... | collective-permute-start | bytes 2211848 | tf_op jit(solution)/shard_map/ppermute | solution.py:319
  6.9 0.9 %copy-start.3 = (bf16[160,640]{1,0:T(8,128)(2,1)S(1)}, bf16[160,640]{1,0:T(8,128)(2,1)}, u32[]{:S(2)}) copy-start(bf16[160,640]{1,0:T(8,128)(2,1)} %refs_3_.1) | copy-start | bytes 614404
  7.8 0.8 %copy-start.4 = (f32[7,7,160]{2,1,0:T(8,128)S(1)}, f32[7,7,160]{2,1,0:T(8,128)}, u32[]{:S(2)}) copy-start(f32[7,7,160]{2,1,0:T(8,128)} %refs_0_.2) | copy-start | bytes 94084
  8.6 0.7 copy-start.5
  9.3 0.7 copy-start.6
  10.0 0.7 copy-start.7
  10.7 0.7 copy-start.8
  11.4 9.1 %copy-start.9 = (s32[12]{0:T(128)S(1)}, s32[12]{0:T(128)}, u32[]{:S(2)}) copy-start(s32[12]{0:T(128)} %refs_0_.3) | copy-start | bytes 148
  15.3 10.2 %copy-start = (bf16[1,3,160,768]{3,2,1,0:T(8,128)(2,1)S(1)}, bf16[1,3,160,768]{3,2,1,0:T(8,128)(2,1)}, u32[]{:S(2)}) copy-start(bf16[1,3,160,768]{3,2,1,0:T(8,128)(2,1)} %param.10) | copy-start | bytes 2211844
  15.3 15.5 %collective-permute-start.2 = (bf16[3,160,768]{2,1,0:T(8,128)(2,1)S(1)}, bf16[3,160,768]{2,1,0:T(8,128)(2,1)S(1)}, u32[]{:S(2)}, u32[]{:S(2)}) collective-permute-start(bf16[3,160,768]{2,1,0:T(8,128)(2,1)S(1)} %broadcast_select_fusion.refs_1_), channel_id=1, source_target_pairs={{1,2},{9,10},{2,1},{10,9},{17,18},{25,26},{18,17},{26,25}} | collective-permute-start | bytes 2211848 | tf_op jit(solution)/shard_map/ppermute | solution.py:319
  18.5 13.4 %collective-permute-start.1 = (bf16[3,160,768]{2,1,0:T(8,128)(2,1)S(1)}, bf16[3,160,768]{2,1,0:T(8,128)(2,1)S(1)}, u32[]{:S(2)}, u32[]{:S(2)}) collective-permute-start(bf16[3,160,768]{2,1,0:T(8,128)(2,1)S(1)} %broadcast_select_fusion.refs_1_), channel_id=1, source_target_pairs={{0,1},{2,3},{8,9},{10,11},{1,0},{3,2},{9,8},{11,10},{16,17},{18,19... | collective-permute-start | bytes 2211848 | tf_op jit(solution)/shard_map/ppermute | solution.py:319
  24.0 12.4 %copy-start.1 = (bf16[640,160]{0,1:T(8,128)(2,1)S(1)}, bf16[640,160]{0,1:T(8,128)(2,1)}, u32[]{:S(2)}) copy-start(bf16[640,160]{0,1:T(8,128)(2,1)} %param.18) | copy-start | bytes 614404
  24.0 10.8 %collective-permute-start.6 = (bf16[3,160,768]{2,1,0:T(8,128)(2,1)S(1)}, bf16[3,160,768]{2,1,0:T(8,128)(2,1)S(1)}, u32[]{:S(2)}, u32[]{:S(2)}) collective-permute-start(bf16[3,160,768]{2,1,0:T(8,128)(2,1)S(1)} %broadcast_select_fusion.refs_1_), channel_id=1, source_target_pairs={{0,4},{1,5},{2,6},{3,7},{8,12},{9,13},{10,14},{11,15},{16,20},{17,... | collective-permute-start | bytes 2211848 | tf_op jit(solution)/shard_map/ppermute | solution.py:319
  31.9 3.1 %collective-permute-start.7 = (bf16[3,160,768]{2,1,0:T(8,128)(2,1)S(1)}, bf16[3,160,768]{2,1,0:T(8,128)(2,1)S(1)}, u32[]{:S(2)}, u32[]{:S(2)}) collective-permute-start(bf16[3,160,768]{2,1,0:T(8,128)(2,1)S(1)} %collective-permute-done.1.refs_0_), channel_id=1, source_target_pairs={{0,4},{1,5},{2,6},{3,7},{8,12},{9,13},{10,14},{11,15},{16,20},{17,... | collective-permute-start | bytes 2211848 | tf_op jit(solution)/shard_map/ppermute | solution.py:319
  33.2 3.1 %collective-permute-start.5 = (bf16[3,160,768]{2,1,0:T(8,128)(2,1)S(1)}, bf16[3,160,768]{2,1,0:T(8,128)(2,1)S(1)}, u32[]{:S(2)}, u32[]{:S(2)}) collective-permute-start(bf16[3,160,768]{2,1,0:T(8,128)(2,1)S(1)} %collective-permute-done.2.refs_2_), channel_id=1, source_target_pairs={{0,4},{1,5},{2,6},{3,7},{8,12},{9,13},{10,14},{11,15},{16,20},{17,... | collective-permute-start | bytes 2211848 | tf_op jit(solution)/shard_map/ppermute | solution.py:319
  43.1 16.5 %collective-permute-start.10 = (bf16[3,160,768]{2,1,0:T(8,128)(2,1)S(1)}, bf16[3,160,768]{2,1,0:T(8,128)(2,1)S(1)}, u32[]{:S(2)}, u32[]{:S(2)}) collective-permute-start(bf16[3,160,768]{2,1,0:T(8,128)(2,1)S(1)} %get-tuple-element.39.refs_10_.refs_1_), channel_id=1, source_target_pairs={{0,1},{2,3},{8,9},{10,11},{1,0},{3,2},{9,8},{11,10},{5,6},{13,14},... | collective-permute-start | bytes 2211848 | tf_op jit(solution)/shard_map/ppermute | solution.py:319
  47.9 22.8 %collective-permute-start.9 = (bf16[3,168,768]{2,1,0:T(8,128)(2,1)S(1)}, bf16[3,168,768]{2,1,0:T(8,128)(2,1)S(1)}, u32[]{:S(2)}, u32[]{:S(2)}) collective-permute-start(bf16[3,168,768]{2,1,0:T(8,128)(2,1)S(1)} %tangent.2.refs_1_), channel_id=1, source_target_pairs={{9,10},{10,9},{4,5},{6,7},{12,13},{14,15},{5,4},{7,6},{13,12},{15,... | collective-permute-start | bytes 2322440 | tf_op jit(solution)/shard_map/ppermute | solution.py:319
  50.7 22.4 %collective-permute-start.8 = (bf16[3,168,768]{2,1,0:T(8,128)(2,1)S(1)}, bf16[3,168,768]{2,1,0:T(8,128)(2,1)S(1)}, u32[]{:S(2)}, u32[]{:S(2)}) collective-permute-start(bf16[3,168,768]{2,1,0:T(8,128)(2,1)S(1)} %tangent.2.refs_1_), channel_id=1, source_target_pairs={{8,9},{10,11},{9,8},{11,10},{5,6},{13,14},{6,5},{14,13},{24,25},{2... | collective-permute-start | bytes 2322440 | tf_op jit(solution)/shard_map/ppermute | solution.py:319
  59.6 2.2 %collective-permute-start.11 = (bf16[3,160,768]{2,1,0:T(8,128)(2,1)S(1)}, bf16[3,160,768]{2,1,0:T(8,128)(2,1)S(1)}, u32[]{:S(2)}, u32[]{:S(2)}) collective-permute-start(bf16[3,160,768]{2,1,0:T(8,128)(2,1)S(1)} %collective-permute-done.10.refs_0_), channel_id=1, source_target_pairs={{0,4},{1,5},{2,6},{3,7},{8,12},{9,13},{10,14},{11,15},{4,0},{5,1},... | collective-permute-start | bytes 2211848 | tf_op jit(solution)/shard_map/ppermute | solution.py:319

commit v6 on v5

--- a/solution.py
+++ b/solution.py
@@ -168,6 +168,16 @@
     ).astype(bf16)
 
 
+def gelu_parts(h, both=True):
+    square = h * h
+    half = 0.5 + 0.5 * jnp.tanh(h * (gelu_scale + (gelu_scale * gelu_cubic) * square))
+    return half, h * (2.0 * gelu_scale + (6.0 * gelu_scale * gelu_cubic) * square) if both else None
+
+
+def gelu_slope(half, lean):
+    return half * (1.0 + (1.0 - half) * lean)
+
+
 def control_kernel(*refs):
     first_halo, own, second_halo = refs[:3]
     refs = refs[3:]
@@ -205,12 +215,12 @@
     def pair(slot, r, at):
         for c in range(0, hid, CHUNK):
             h = hidden[slot][c : c + CHUNK, :]
-            square = h * h
-            t = jnp.tanh(h * (gelu_scale + (gelu_scale * gelu_cubic) * square))
-            half = 0.5 + 0.5 * t
+            half, lean = gelu_parts(h, other is None)
             act[slot][c : c + CHUNK, :] = (h * half).astype(bf16)
-            lean = h * (2.0 * gelu_scale + (6.0 * gelu_scale * gelu_cubic) * square)
-            slope_out[r, c : c + CHUNK, at] = half * (1.0 + (1.0 - half) * lean)
+            if other is None:
+                slope_out[r, c : c + CHUNK, at] = gelu_slope(half, lean)
+            else:
+                slope_out[r, c : c + CHUNK, at] = h
 
     def third(slot, r, at):
         update = jnp.dot(w_out[...], act[slot][...], preferred_element_type=f32)
@@ -258,7 +268,10 @@
 
     def mix(slot, r, at):
         for c in range(0, hid, CHUNK):
-            act[slot][c : c + CHUNK, :] = (slope_in[r, c : c + CHUNK, at] * hidden[slot][c : c + CHUNK, :]).astype(bf16)
+            slope = slope_in[r, c : c + CHUNK, at]
+            if ready:
+                slope = gelu_slope(*gelu_parts(slope))
+            act[slot][c : c + CHUNK, :] = (slope * hidden[slot][c : c + CHUNK, :]).astype(bf16)
 
     def third(slot, r, at):
         update = jnp.dot(w_out[...], act[slot][...], preferred_element_type=f32)

time: 79.3 us -> 77.9 us (0.982)
  waiting for transfers between devices: 16.7 us -> 14.8 us
    ppermute x12, waiting for transfers between devices: 16.7 us -> 14.8 us  [send(): lax.ppermute(block, ('mem', 'lat'), [(a * bands + i, b * bands + j) for (...]
    pallas_call x2, Pallas kernels: 8.47 us -> 10.2 us  [tangent_step(): pl.pallas_call(lambda *refs: tangent_kernel(ready, *refs), out_shape=shap...]
    pallas_call x2, Pallas kernels: 15.6 us -> 14.3 us  [control_step(): pl.pallas_call(control_kernel, out_shape=(field, shape(rows, channels, wi...]
  transfers between devices with their start and end apart: 12 -> 12, of which waited for: 7 -> 8; matrix products, arithmetic and copies ran while one was open for 2% -> 2% of each run, Pallas kernels for 26% -> 29%
where the time goes in v6:
time: 77.9 us; the launch traced here: 77.4 us
  Pallas kernels  33.6 us (43%)
  starting transfers between devices  23.1 us (30%)
  waiting for transfers between devices  14.8 us (19%)
  local copies, waits for them, and re-layouts  4.51 us (6%)
  other arithmetic  1.2 us (2%)
    ppermute x12, starting transfers between devices, send(): lax.ppermute(block, ('mem', 'lat'), [(a * bands + i, b * bands + j) for (...  23.1 us
    ppermute x12, waiting for transfers between devices, send(): lax.ppermute(block, ('mem', 'lat'), [(a * bands + i, b * bands + j) for (...  14.8 us
    pallas_call x2, Pallas kernels, control_step(): pl.pallas_call(control_kernel, out_shape=(field, shape(rows, channels, wi...  14.3 us
    pallas_call x2, Pallas kernels, tangent_step(): pl.pallas_call(lambda *refs: tangent_kernel(ready, *refs), out_shape=shap...  10.2 us
    unnamed x20, local copies, waits for them, and re-layouts  4.51 us
    pallas_call x1, Pallas kernels, per_device(): pl.pallas_call(lambda *refs: filter_kernel(bands, *refs), out_shape=shape...  3.49 us
    pallas_call x1, Pallas kernels, conv_step(): pl.pallas_call(conv_kernel, out_shape=shape(rows, channels, width), in_sp...  2.85 us
    pallas_call x1, Pallas kernels, per_device(): pl.pallas_call(prepare_kernel, out_shape=(shape(rows, TAPS, channels, (ro...  2.68 us
  transfers between devices with their start and end apart: 12, of which 8 were waited for; matrix products, arithmetic and copies ran while one was open for 2% of the time, Pallas kernels for 29%

profile of v6, /device:TPU:10, one launch (start us, length us, event | category | flops | bytes accessed | tf_op | source)
XLA Modules:
  0.0 77.4 jit_solution(9489762186152391067)
XLA Ops:
  0.0 0.0 copy-start.2
  0.0 1.4 %collective-permute-start = (bf16[3,160,768]{2,1,0:T(8,128)(2,1)}, bf16[3,160,768]{2,1,0:T(8,128)(2,1)S(1)}, u32[]{:S(2)}, u32[]{:S(2)}) collective-permute-start(bf16[3,160,768]{2,1,0:T(8,128)(2,1)} %bitcast.7), channel_id=1, source_target_pairs={{0,8},{1,9},{2,10},{3,11},{16,24},{17,25},{18,26},{19,27}} | collective-permute-start | bytes 2211848 | tf_op jit(solution)/shard_map/ppermute | solution.py:332
  1.4 3.5 %collective-permute-start.4 = (bf16[3,160,768]{2,1,0:T(8,128)(2,1)}, bf16[3,160,768]{2,1,0:T(8,128)(2,1)S(1)}, u32[]{:S(2)}, u32[]{:S(2)}) collective-permute-start(bf16[3,160,768]{2,1,0:T(8,128)(2,1)} %bitcast.8), channel_id=1, source_target_pairs={{9,10},{10,9},{4,5},{6,7},{12,13},{14,15},{5,4},{7,6},{13,12},{15,... | collective-permute-start | bytes 2211848 | tf_op jit(solution)/shard_map/ppermute | solution.py:332
  4.9 1.9 %collective-permute-start.3 = (bf16[3,160,768]{2,1,0:T(8,128)(2,1)}, bf16[3,160,768]{2,1,0:T(8,128)(2,1)S(1)}, u32[]{:S(2)}, u32[]{:S(2)}) collective-permute-start(bf16[3,160,768]{2,1,0:T(8,128)(2,1)} %bitcast.9), channel_id=1, source_target_pairs={{8,9},{10,11},{9,8},{11,10},{5,6},{13,14},{6,5},{14,13},{24,25},{2... | collective-permute-start | bytes 2211848 | tf_op jit(solution)/shard_map/ppermute | solution.py:332
  6.9 0.0 copy-start.3
  6.9 0.9 %copy-done.3 = bf16[160,640]{1,0:T(8,128)(2,1)S(1)} copy-done((bf16[160,640]{1,0:T(8,128)(2,1)S(1)}, bf16[160,640]{1,0:T(8,128)(2,1)}, u32[]{:S(2)}) %copy-start.3) | copy-done | bytes 204824
  7.8 0.0 copy-start.4
  7.8 0.8 %copy-done.4 = f32[7,7,160]{2,1,0:T(8,128)S(1)} copy-done((f32[7,7,160]{2,1,0:T(8,128)S(1)}, f32[7,7,160]{2,1,0:T(8,128)}, u32[]{:S(2)}) %copy-start.4) | copy-done | bytes 31384
  8.6 0.0 copy-start.5
  8.6 0.7 copy-done.5
  9.3 0.0 copy-start.6
  9.3 0.7 copy-done.6
  10.0 0.0 copy-start.7
  10.0 0.7 copy-done.7
  10.7 0.0 copy-start.8
  10.7 0.7 copy-done.8
  11.4 0.0 copy-start.9
  11.4 2.7 %prepare.1 = (bf16[3,7,160,144]{3,2,1,0:T(8,128)(2,1)S(1)}, f32[160,128]{1,0:T(8,128)S(1)}, f32[160,128]{1,0:T(8,128)S(1)}, bf16[640,176]{1,0:T(8,128)(2,1)S(1)}, f32[3,768]{1,0:T(4,128)S(1)}) custom-call(f32[7,7,160]{2,1,0:T(8,128)S(1)} %copy-done.4, f32[1,160]{1,0:T(1,128)S(1)} %bitcast.17, f32[1,160]{1,0:T(1,128)S(1)} %bitcast.18, ...), custom_call_target="tpu_custom_call" | custom-call | tf_op jit(solution)/shard_map/prepare/pallas_call | solution.py:354
  14.1 0.0 collective-permute-done
  14.1 1.2 %broadcast_select_fusion.refs_1_ = bf16[3,160,768]{2,1,0:T(8,128)(2,1)S(1)} fusion(bf16[3,160,768]{2,1,0:T(8,128)(2,1)S(1)} %collective-permute-done, pred[]{:T(512)S(6)} %and.4, bf16[1,3,160,768]{3,2,1,0:T(8,128)(2,1)} %param.10), kind=kLoop, calls=%fused_computation | loop fusion | flops 368640 | bytes 2211841 | tf_op jit(solution)/shard_map/jit(_where)/select_n | solution.py:415
  15.3 0.0 copy-start
  15.3 3.2 %collective-permute-start.2 = (bf16[3,160,768]{2,1,0:T(8,128)(2,1)S(1)}, bf16[3,160,768]{2,1,0:T(8,128)(2,1)S(1)}, u32[]{:S(2)}, u32[]{:S(2)}) collective-permute-start(bf16[3,160,768]{2,1,0:T(8,128)(2,1)S(1)} %broadcast_select_fusion.refs_1_), channel_id=1, source_target_pairs={{1,2},{9,10},{2,1},{10,9},{17,18},{25,26},{18,17},{26,25}} | collective-permute-start | bytes 2211848 | tf_op jit(solution)/shard_map/ppermute | solution.py:332
  18.5 1.9 %collective-permute-start.1 = (bf16[3,160,768]{2,1,0:T(8,128)(2,1)S(1)}, bf16[3,160,768]{2,1,0:T(8,128)(2,1)S(1)}, u32[]{:S(2)}, u32[]{:S(2)}) collective-permute-start(bf16[3,160,768]{2,1,0:T(8,128)(2,1)S(1)} %broadcast_select_fusion.refs_1_), channel_id=1, source_target_pairs={{0,1},{2,3},{8,9},{10,11},{1,0},{3,2},{9,8},{11,10},{16,17},{18,19... | collective-permute-start | bytes 2211848 | tf_op jit(solution)/shard_map/ppermute | solution.py:332
  20.5 0.0 copy-done.2
  20.5 0.0 copy-done.9
  20.5 3.5 %filters.1.refs_12_.refs_6_.refs_9_.refs_8_ = bf16[3,768,768]{2,1,0:T(8,128)(2,1)S(1)} custom-call(s32[12]{0:T(128)S(1)} %copy-done.9, bf16[768,768]{1,0:T(8,128)(2,1)S(1)} %copy-done.2), custom_call_target="tpu_custom_call" | custom-call | tf_op jit(solution)/shard_map/filters/pallas_call | solution.py:369
  24.0 0.0 copy-start.1
  24.0 1.5 %collective-permute-start.6 = (bf16[3,160,768]{2,1,0:T(8,128)(2,1)S(1)}, bf16[3,160,768]{2,1,0:T(8,128)(2,1)S(1)}, u32[]{:S(2)}, u32[]{:S(2)}) collective-permute-start(bf16[3,160,768]{2,1,0:T(8,128)(2,1)S(1)} %broadcast_select_fusion.refs_1_), channel_id=1, source_target_pairs={{0,4},{1,5},{2,6},{3,7},{8,12},{9,13},{10,14},{11,15},{16,20},{17,... | collective-permute-start | bytes 2211848 | tf_op jit(solution)/shard_map/ppermute | solution.py:332
  25.5 0.0 collective-permute-done.4.second
  25.5 0.0 collective-permute-done.3.first
  25.5 0.0 copy-done
  25.5 2.8 %conv.1.refs_1_ = f32[3,160,768]{2,1,0:T(8,128)S(1)} custom-call(bf16[3,160,768]{2,1,0:T(8,128)(2,1)S(1)} %collective-permute-done.3.first, bf16[3,160,768]{2,1,0:T(8,128)(2,1)S(1)} %bitcast.10, bf16[3,160,768]{2,1,0:T(8,128)(2,1)S(1)} %collective-permute-done.4.second, bf16[3,7,160,144]{3,2,1,0:T(8,128)(2,1)S(1)} %get-tuple-element.27.taps.refs_6_.refs_3_), custom_call_target="tpu_custom_call" | custom-call | tf_op jit(solution)/shard_map/conv/pallas_call | solution.py:390
  28.3 2.4 %collective-permute-done.2.refs_2_ = bf16[3,160,768]{2,1,0:T(8,128)(2,1)S(1)} collective-permute-done((bf16[3,160,768]{2,1,0:T(8,128)(2,1)S(1)}, bf16[3,160,768]{2,1,0:T(8,128)(2,1)S(1)}, u32[]{:S(2)}, u32[]{:S(2)}) %collective-permute-start.2) | collective-permute-done | bytes 737312 | tf_op jit(solution)/shard_map/ppermute | solution.py:332
  30.8 1.1 %collective-permute-done.1.refs_0_ = bf16[3,160,768]{2,1,0:T(8,128)(2,1)S(1)} collective-permute-done((bf16[3,160,768]{2,1,0:T(8,128)(2,1)S(1)}, bf16[3,160,768]{2,1,0:T(8,128)(2,1)S(1)}, u32[]{:S(2)}, u32[]{:S(2)}) %collective-permute-start.1) | collective-permute-done | bytes 737312 | tf_op jit(solution)/shard_map/ppermute | solution.py:332
  31.9 1.3 %collective-permute-start.7 = (bf16[3,160,768]{2,1,0:T(8,128)(2,1)S(1)}, bf16[3,160,768]{2,1,0:T(8,128)(2,1)S(1)}, u32[]{:S(2)}, u32[]{:S(2)}) collective-permute-start(bf16[3,160,768]{2,1,0:T(8,128)(2,1)S(1)} %collective-permute-done.1.refs_0_), channel_id=1, source_target_pairs={{0,4},{1,5},{2,6},{3,7},{8,12},{9,13},{10,14},{11,15},{16,20},{17,... | collective-permute-start | bytes 2211848 | tf_op jit(solution)/shard_map/ppermute | solution.py:332
  33.2 1.5 %collective-permute-start.5 = (bf16[3,160,768]{2,1,0:T(8,128)(2,1)S(1)}, bf16[3,160,768]{2,1,0:T(8,128)(2,1)S(1)}, u32[]{:S(2)}, u32[]{:S(2)}) collective-permute-start(bf16[3,160,768]{2,1,0:T(8,128)(2,1)S(1)} %collective-permute-done.2.refs_2_), channel_id=1, source_target_pairs={{0,4},{1,5},{2,6},{3,7},{8,12},{9,13},{10,14},{11,15},{16,20},{17,... | collective-permute-start | bytes 2211848 | tf_op jit(solution)/shard_map/ppermute | solution.py:332
  34.7 0.0 collective-permute-done.6.refs_4_
  34.8 0.2 collective-permute-done.7.refs_5_
  35.0 1.3 %collective-permute-done.5.refs_3_ = bf16[3,160,768]{2,1,0:T(8,128)(2,1)S(1)} collective-permute-done((bf16[3,160,768]{2,1,0:T(8,128)(2,1)S(1)}, bf16[3,160,768]{2,1,0:T(8,128)(2,1)S(1)}, u32[]{:S(2)}, u32[]{:S(2)}) %collective-permute-start.5) | collective-permute-done | bytes 737312 | tf_op jit(solution)/shard_map/ppermute | solution.py:332
  36.3 0.0 copy-done.1
  36.3 5.4 %control.2 = (bf16[3,160,768]{2,1,0:T(8,128)(2,1)S(1)}, f32[3,160,768]{2,1,0:T(8,128)S(1)}, f32[3,1,768]{2,1,0:T(1,128)S(1)}, f32[3,640,768]{2,1,0:T(8,128)S(1)}) custom-call(bf16[3,160,768]{2,1,0:T(8,128)(2,1)S(1)} %collective-permute-done.1.refs_0_, bf16[3,160,768]{2,1,0:T(8,128)(2,1)S(1)} %broadcast_select_fusion.refs_1_, ...), custom_call_target="tpu_custom_call" | custom-call | tf_op jit(solution)/shard_map/control/pallas_call | solution.py:379
  41.8 1.9 %collective-permute-start.10 = (bf16[3,160,768]{2,1,0:T(8,128)(2,1)S(1)}, bf16[3,160,768]{2,1,0:T(8,128)(2,1)S(1)}, u32[]{:S(2)}, u32[]{:S(2)}) collective-permute-start(bf16[3,160,768]{2,1,0:T(8,128)(2,1)S(1)} %get-tuple-element.39.refs_10_.refs_1_), channel_id=1, source_target_pairs={{0,1},{2,3},{8,9},{10,11},{1,0},{3,2},{9,8},{11,10},{5,6},{13,14},... | collective-permute-start | bytes 2211848 | tf_op jit(solution)/shard_map/ppermute | solution.py:332
  43.7 4.6 %tangent.2.refs_1_ = bf16[3,168,768]{2,1,0:T(8,128)(2,1)S(1)} custom-call(bf16[3,160,768]{2,1,0:T(8,128)(2,1)S(1)} %bitcast.11, f32[3,160,768]{2,1,0:T(8,128)S(1)} %conv.1.refs_1_, f32[160,128]{1,0:T(8,128)S(1)} %get-tuple-element.29.refs_7_.refs_2_.refs_4_, bf16[640,176]{1,0:T(8,128)(2,1)S(1)} %get-tuple-element.30.refs_9_.refs_3_.refs_6_.refs_5_, ...), custom_call_target="tpu_custom_call" | custom-call | tf_op jit(solution)/shard_map/tangent/pallas_call | solution.py:400
  48.3 2.7 %collective-permute-start.9 = (bf16[3,168,768]{2,1,0:T(8,128)(2,1)S(1)}, bf16[3,168,768]{2,1,0:T(8,128)(2,1)S(1)}, u32[]{:S(2)}, u32[]{:S(2)}) collective-permute-start(bf16[3,168,768]{2,1,0:T(8,128)(2,1)S(1)} %tangent.2.refs_1_), channel_id=1, source_target_pairs={{9,10},{10,9},{4,5},{6,7},{12,13},{14,15},{5,4},{7,6},{13,12},{15,... | collective-permute-start | bytes 2322440 | tf_op jit(solution)/shard_map/ppermute | solution.py:332
  51.1 2.1 %collective-permute-start.8 = (bf16[3,168,768]{2,1,0:T(8,128)(2,1)S(1)}, bf16[3,168,768]{2,1,0:T(8,128)(2,1)S(1)}, u32[]{:S(2)}, u32[]{:S(2)}) collective-permute-start(bf16[3,168,768]{2,1,0:T(8,128)(2,1)S(1)} %tangent.2.refs_1_), channel_id=1, source_target_pairs={{8,9},{10,11},{9,8},{11,10},{5,6},{13,14},{6,5},{14,13},{24,25},{2... | collective-permute-start | bytes 2322440 | tf_op jit(solution)/shard_map/ppermute | solution.py:332
  53.2 3.3 %collective-permute-done.10.refs_0_ = bf16[3,160,768]{2,1,0:T(8,128)(2,1)S(1)} collective-permute-done((bf16[3,160,768]{2,1,0:T(8,128)(2,1)S(1)}, bf16[3,160,768]{2,1,0:T(8,128)(2,1)S(1)}, u32[]{:S(2)}, u32[]{:S(2)}) %collective-permute-start.10) | collective-permute-done | bytes 737312 | tf_op jit(solution)/shard_map/ppermute | solution.py:332
  56.5 0.0 collective-permute-start.11
  56.5 2.2 %collective-permute-done.11.refs_2_ = bf16[3,160,768]{2,1,0:T(8,128)(2,1)S(1)} collective-permute-done((bf16[3,160,768]{2,1,0:T(8,128)(2,1)S(1)}, bf16[3,160,768]{2,1,0:T(8,128)(2,1)S(1)}, u32[]{:S(2)}, u32[]{:S(2)}) %collective-permute-start.11) | collective-permute-done | bytes 737312 | tf_op jit(solution)/shard_map/ppermute | solution.py:332
  58.7 8.9 %control.3 = (bf16[3,160,768]{2,1,0:T(8,128)(2,1)S(1)}, f32[3,160,768]{2,1,0:T(8,128)S(1)}, f32[3,1,768]{2,1,0:T(1,128)S(1)}, f32[3,640,768]{2,1,0:T(8,128)S(1)}) custom-call(bf16[3,160,768]{2,1,0:T(8,128)(2,1)S(1)} %collective-permute-done.10.refs_0_, bf16[3,160,768]{2,1,0:T(8,128)(2,1)S(1)} %get-tuple-element.39.refs_10_.refs_1_, ...), custom_call_target="tpu_custom_call" | custom-call | tf_op jit(solution)/shard_map/control/pallas_call | solution.py:379
  67.6 2.4 %collective-permute-done.9.refs_2_ = bf16[3,168,768]{2,1,0:T(8,128)(2,1)S(1)} collective-permute-done((bf16[3,168,768]{2,1,0:T(8,128)(2,1)S(1)}, bf16[3,168,768]{2,1,0:T(8,128)(2,1)S(1)}, u32[]{:S(2)}, u32[]{:S(2)}) %collective-permute-start.9) | collective-permute-done | bytes 774176 | tf_op jit(solution)/shard_map/ppermute | solution.py:332
  70.0 1.7 %collective-permute-done.8.refs_0_ = bf16[3,168,768]{2,1,0:T(8,128)(2,1)S(1)} collective-permute-done((bf16[3,168,768]{2,1,0:T(8,128)(2,1)S(1)}, bf16[3,168,768]{2,1,0:T(8,128)(2,1)S(1)}, u32[]{:S(2)}, u32[]{:S(2)}) %collective-permute-start.8) | collective-permute-done | bytes 774176 | tf_op jit(solution)/shard_map/ppermute | solution.py:332
  71.7 5.6 %tangent.3 = bf16[3,160,768]{2,1,0:T(8,128)(2,1)} custom-call(bf16[3,168,768]{2,1,0:T(8,128)(2,1)S(1)} %collective-permute-done.8.refs_0_, bf16[3,168,768]{2,1,0:T(8,128)(2,1)S(1)} %tangent.2.refs_1_, bf16[3,168,768]{2,1,0:T(8,128)(2,1)S(1)} %collective-permute-done.9.refs_2_, bf16[3,7,160,144]{3,2,1,0:T(8,128)(2,1)S(1)} %get-tuple-element.27.taps.refs_6_.refs_3_, ...), custom_call_target="tpu_custom_call" | custom-call | tf_op jit(solution)/shard_map/tangent/pallas_call | solution.py:400
Async XLA Ops:
  0.0 20.5 %copy-start.2 = (bf16[768,768]{1,0:T(8,128)(2,1)S(1)}, bf16[768,768]{1,0:T(8,128)(2,1)}, u32[]{:S(2)}) copy-start(bf16[768,768]{1,0:T(8,128)(2,1)} %constant.11.clone.refs_1_) | copy-start | bytes 3538948
  0.0 14.1 %collective-permute-start = (bf16[3,160,768]{2,1,0:T(8,128)(2,1)}, bf16[3,160,768]{2,1,0:T(8,128)(2,1)S(1)}, u32[]{:S(2)}, u32[]{:S(2)}) collective-permute-start(bf16[3,160,768]{2,1,0:T(8,128)(2,1)} %bitcast.7), channel_id=1, source_target_pairs={{0,8},{1,9},{2,10},{3,11},{16,24},{17,25},{18,26},{19,27}} | collective-permute-start | bytes 2211848 | tf_op jit(solution)/shard_map/ppermute | solution.py:332
  1.4 24.0 %collective-permute-start.4 = (bf16[3,160,768]{2,1,0:T(8,128)(2,1)}, bf16[3,160,768]{2,1,0:T(8,128)(2,1)S(1)}, u32[]{:S(2)}, u32[]{:S(2)}) collective-permute-start(bf16[3,160,768]{2,1,0:T(8,128)(2,1)} %bitcast.8), channel_id=1, source_target_pairs={{9,10},{10,9},{4,5},{6,7},{12,13},{14,15},{5,4},{7,6},{13,12},{15,... | collective-permute-start | bytes 2211848 | tf_op jit(solution)/shard_map/ppermute | solution.py:332
  4.9 20.6 %collective-permute-start.3 = (bf16[3,160,768]{2,1,0:T(8,128)(2,1)}, bf16[3,160,768]{2,1,0:T(8,128)(2,1)S(1)}, u32[]{:S(2)}, u32[]{:S(2)}) collective-permute-start(bf16[3,160,768]{2,1,0:T(8,128)(2,1)} %bitcast.9), channel_id=1, source_target_pairs={{8,9},{10,11},{9,8},{11,10},{5,6},{13,14},{6,5},{14,13},{24,25},{2... | collective-permute-start | bytes 2211848 | tf_op jit(solution)/shard_map/ppermute | solution.py:332
  6.9 0.9 %copy-start.3 = (bf16[160,640]{1,0:T(8,128)(2,1)S(1)}, bf16[160,640]{1,0:T(8,128)(2,1)}, u32[]{:S(2)}) copy-start(bf16[160,640]{1,0:T(8,128)(2,1)} %refs_3_.1) | copy-start | bytes 614404
  7.8 0.8 %copy-start.4 = (f32[7,7,160]{2,1,0:T(8,128)S(1)}, f32[7,7,160]{2,1,0:T(8,128)}, u32[]{:S(2)}) copy-start(f32[7,7,160]{2,1,0:T(8,128)} %refs_0_.2) | copy-start | bytes 94084
  8.6 0.7 copy-start.5
  9.3 0.7 copy-start.6
  10.0 0.7 copy-start.7
  10.7 0.7 copy-start.8
  11.4 9.1 %copy-start.9 = (s32[12]{0:T(128)S(1)}, s32[12]{0:T(128)}, u32[]{:S(2)}) copy-start(s32[12]{0:T(128)} %refs_0_.3) | copy-start | bytes 148
  15.3 10.2 %copy-start = (bf16[1,3,160,768]{3,2,1,0:T(8,128)(2,1)S(1)}, bf16[1,3,160,768]{3,2,1,0:T(8,128)(2,1)}, u32[]{:S(2)}) copy-start(bf16[1,3,160,768]{3,2,1,0:T(8,128)(2,1)} %param.10) | copy-start | bytes 2211844
  15.3 15.5 %collective-permute-start.2 = (bf16[3,160,768]{2,1,0:T(8,128)(2,1)S(1)}, bf16[3,160,768]{2,1,0:T(8,128)(2,1)S(1)}, u32[]{:S(2)}, u32[]{:S(2)}) collective-permute-start(bf16[3,160,768]{2,1,0:T(8,128)(2,1)S(1)} %broadcast_select_fusion.refs_1_), channel_id=1, source_target_pairs={{1,2},{9,10},{2,1},{10,9},{17,18},{25,26},{18,17},{26,25}} | collective-permute-start | bytes 2211848 | tf_op jit(solution)/shard_map/ppermute | solution.py:332
  18.5 13.4 %collective-permute-start.1 = (bf16[3,160,768]{2,1,0:T(8,128)(2,1)S(1)}, bf16[3,160,768]{2,1,0:T(8,128)(2,1)S(1)}, u32[]{:S(2)}, u32[]{:S(2)}) collective-permute-start(bf16[3,160,768]{2,1,0:T(8,128)(2,1)S(1)} %broadcast_select_fusion.refs_1_), channel_id=1, source_target_pairs={{0,1},{2,3},{8,9},{10,11},{1,0},{3,2},{9,8},{11,10},{16,17},{18,19... | collective-permute-start | bytes 2211848 | tf_op jit(solution)/shard_map/ppermute | solution.py:332
  24.0 12.4 %copy-start.1 = (bf16[640,160]{0,1:T(8,128)(2,1)S(1)}, bf16[640,160]{0,1:T(8,128)(2,1)}, u32[]{:S(2)}) copy-start(bf16[640,160]{0,1:T(8,128)(2,1)} %param.18) | copy-start | bytes 614404
  24.0 10.8 %collective-permute-start.6 = (bf16[3,160,768]{2,1,0:T(8,128)(2,1)S(1)}, bf16[3,160,768]{2,1,0:T(8,128)(2,1)S(1)}, u32[]{:S(2)}, u32[]{:S(2)}) collective-permute-start(bf16[3,160,768]{2,1,0:T(8,128)(2,1)S(1)} %broadcast_select_fusion.refs_1_), channel_id=1, source_target_pairs={{0,4},{1,5},{2,6},{3,7},{8,12},{9,13},{10,14},{11,15},{16,20},{17,... | collective-permute-start | bytes 2211848 | tf_op jit(solution)/shard_map/ppermute | solution.py:332
  31.9 3.1 %collective-permute-start.7 = (bf16[3,160,768]{2,1,0:T(8,128)(2,1)S(1)}, bf16[3,160,768]{2,1,0:T(8,128)(2,1)S(1)}, u32[]{:S(2)}, u32[]{:S(2)}) collective-permute-start(bf16[3,160,768]{2,1,0:T(8,128)(2,1)S(1)} %collective-permute-done.1.refs_0_), channel_id=1, source_target_pairs={{0,4},{1,5},{2,6},{3,7},{8,12},{9,13},{10,14},{11,15},{16,20},{17,... | collective-permute-start | bytes 2211848 | tf_op jit(solution)/shard_map/ppermute | solution.py:332
  33.2 3.1 %collective-permute-start.5 = (bf16[3,160,768]{2,1,0:T(8,128)(2,1)S(1)}, bf16[3,160,768]{2,1,0:T(8,128)(2,1)S(1)}, u32[]{:S(2)}, u32[]{:S(2)}) collective-permute-start(bf16[3,160,768]{2,1,0:T(8,128)(2,1)S(1)} %collective-permute-done.2.refs_2_), channel_id=1, source_target_pairs={{0,4},{1,5},{2,6},{3,7},{8,12},{9,13},{10,14},{11,15},{16,20},{17,... | collective-permute-start | bytes 2211848 | tf_op jit(solution)/shard_map/ppermute | solution.py:332
  41.8 14.7 %collective-permute-start.10 = (bf16[3,160,768]{2,1,0:T(8,128)(2,1)S(1)}, bf16[3,160,768]{2,1,0:T(8,128)(2,1)S(1)}, u32[]{:S(2)}, u32[]{:S(2)}) collective-permute-start(bf16[3,160,768]{2,1,0:T(8,128)(2,1)S(1)} %get-tuple-element.39.refs_10_.refs_1_), channel_id=1, source_target_pairs={{0,1},{2,3},{8,9},{10,11},{1,0},{3,2},{9,8},{11,10},{5,6},{13,14},... | collective-permute-start | bytes 2211848 | tf_op jit(solution)/shard_map/ppermute | solution.py:332
  48.3 21.7 %collective-permute-start.9 = (bf16[3,168,768]{2,1,0:T(8,128)(2,1)S(1)}, bf16[3,168,768]{2,1,0:T(8,128)(2,1)S(1)}, u32[]{:S(2)}, u32[]{:S(2)}) collective-permute-start(bf16[3,168,768]{2,1,0:T(8,128)(2,1)S(1)} %tangent.2.refs_1_), channel_id=1, source_target_pairs={{9,10},{10,9},{4,5},{6,7},{12,13},{14,15},{5,4},{7,6},{13,12},{15,... | collective-permute-start | bytes 2322440 | tf_op jit(solution)/shard_map/ppermute | solution.py:332
  51.1 20.7 %collective-permute-start.8 = (bf16[3,168,768]{2,1,0:T(8,128)(2,1)S(1)}, bf16[3,168,768]{2,1,0:T(8,128)(2,1)S(1)}, u32[]{:S(2)}, u32[]{:S(2)}) collective-permute-start(bf16[3,168,768]{2,1,0:T(8,128)(2,1)S(1)} %tangent.2.refs_1_), channel_id=1, source_target_pairs={{8,9},{10,11},{9,8},{11,10},{5,6},{13,14},{6,5},{14,13},{24,25},{2... | collective-permute-start | bytes 2322440 | tf_op jit(solution)/shard_map/ppermute | solution.py:332
  56.5 2.2 %collective-permute-start.11 = (bf16[3,160,768]{2,1,0:T(8,128)(2,1)S(1)}, bf16[3,160,768]{2,1,0:T(8,128)(2,1)S(1)}, u32[]{:S(2)}, u32[]{:S(2)}) collective-permute-start(bf16[3,160,768]{2,1,0:T(8,128)(2,1)S(1)} %collective-permute-done.10.refs_0_), channel_id=1, source_target_pairs={{0,4},{1,5},{2,6},{3,7},{8,12},{9,13},{10,14},{11,15},{4,0},{5,1},... | collective-permute-start | bytes 2211848 | tf_op jit(solution)/shard_map/ppermute | solution.py:332

commit v7 on v6

--- a/solution.py
+++ b/solution.py
@@ -16,7 +16,6 @@
 LANES = 256
 CHUNK = 64
 BIAS_ROWS = 16
-SPARE = 8
 
 gelu_scale = 0.7978845608028654
 gelu_cubic = 0.044715
@@ -281,9 +280,6 @@
         if at.stop == width:
             polar_filter(raw, filters, out, r)
 
-    if out.shape[1] > channels:
-        out[:, channels:, :] = jnp.zeros((rows, out.shape[1] - channels, width), bf16)
-
     @pl.when(is_control)
     def _():
         out[:, :channels, :] = advanced[...]
@@ -396,10 +392,10 @@
             name="conv",
         )(near, own, far, taps)
 
-    def tangent_step(ready, spare, inputs, unit, scale, slope, advanced):
+    def tangent_step(ready, inputs, unit, scale, slope, advanced):
         return pl.pallas_call(
             lambda *refs: tangent_kernel(ready, *refs),
-            out_shape=shape(rows, channels + spare, width, kind=bf16),
+            out_shape=field,
             in_specs=[VMEM] * (9 + len(inputs)),
             out_specs=VMEM,
             scratch_shapes=scratch(rows, channels, width, hid, 0, not ready),
@@ -424,12 +420,13 @@
     for step in range(1, STEPS):
         halo = exchange(control, range(members))[0]
         inputs = (member, conv) if step == 1 else (near, member, far, taps)
-        member = tangent_step(step == 1, SPARE, inputs, unit, scale, slope, control)
+        member = tangent_step(step == 1, inputs, unit, scale, slope, control)
         halo, _ = lax.optimization_barrier((halo, member))
-        other = across(halo, swapped)
+        halves = [across(part, swapped) for part in jnp.split(halo, 2, axis=1)]
+        other = jnp.concatenate(halves, axis=1)
         near, far = exchange(member, range(1, members))
         control, unit, scale, slope = control_step(halo, control, other)
-    return tangent_step(False, 0, (near, member, far, taps), unit, scale, slope, control)[None]
+    return tangent_step(False, (near, member, far, taps), unit, scale, slope, control)[None]
 
 
 def solution(mesh):

time: 77.9 us -> 77.1 us (0.990)
  waiting for transfers between devices: 14.8 us -> 13.3 us
    ppermute x12 -> x13, waiting for transfers between devices: 14.8 us -> 13.3 us  [send(): lax.ppermute(block, ('mem', 'lat'), [(a * bands + i, b * bands + j) for (...]
    ppermute x12 -> x13, starting transfers between devices: 23.1 us -> 23.6 us  [send(): lax.ppermute(block, ('mem', 'lat'), [(a * bands + i, b * bands + j) for (...]
  transfers between devices with their start and end apart: 12 -> 13, of which waited for: 8 -> 9; matrix products, arithmetic and copies ran while one was open for 2% -> 2% of each run, Pallas kernels for 29% -> 29%
where the time goes in v7:
time: 77.1 us; the launch traced here: 76.6 us
  Pallas kernels  33.5 us (43%)
  starting transfers between devices  23.6 us (31%)
  waiting for transfers between devices  13.3 us (17%)
  local copies, waits for them, and re-layouts  4.56 us (6%)
  other arithmetic  1.25 us (2%)
    ppermute x13, starting transfers between devices, send(): lax.ppermute(block, ('mem', 'lat'), [(a * bands + i, b * bands + j) for (...  23.6 us
    pallas_call x2, Pallas kernels, control_step(): pl.pallas_call(control_kernel, out_shape=(field, shape(rows, channels, wi...  14.3 us
    ppermute x13, waiting for transfers between devices, send(): lax.ppermute(block, ('mem', 'lat'), [(a * bands + i, b * bands + j) for (...  13.3 us
    pallas_call x2, Pallas kernels, tangent_step(): pl.pallas_call(lambda *refs: tangent_kernel(ready, *refs), out_shape=fiel...  10.2 us
    unnamed x20, local copies, waits for them, and re-layouts  4.51 us
    pallas_call x1, Pallas kernels, per_device(): pl.pallas_call(lambda *refs: filter_kernel(bands, *refs), out_shape=shape...  3.49 us
    pallas_call x1, Pallas kernels, conv_step(): pl.pallas_call(conv_kernel, out_shape=shape(rows, channels, width), in_sp...  2.85 us
    pallas_call x1, Pallas kernels, per_device(): pl.pallas_call(prepare_kernel, out_shape=(shape(rows, TAPS, channels, (ro...  2.68 us
  transfers between devices with their start and end apart: 13, of which 9 were waited for; matrix products, arithmetic and copies ran while one was open for 2% of the time, Pallas kernels for 29%

profile of v7, /device:TPU:10, one launch (start us, length us, event | category | flops | bytes accessed | tf_op | source)
XLA Modules:
  0.0 76.6 jit_solution(14032485994783247256)
XLA Ops:
  0.0 0.0 copy-start.2
  0.0 1.4 %collective-permute-start = (bf16[3,160,768]{2,1,0:T(8,128)(2,1)}, bf16[3,160,768]{2,1,0:T(8,128)(2,1)S(1)}, u32[]{:S(2)}, u32[]{:S(2)}) collective-permute-start(bf16[3,160,768]{2,1,0:T(8,128)(2,1)} %bitcast.7), channel_id=1, source_target_pairs={{0,8},{1,9},{2,10},{3,11},{16,24},{17,25},{18,26},{19,27}} | collective-permute-start | bytes 2211848 | tf_op jit(solution)/shard_map/ppermute | solution.py:328
  1.4 3.5 %collective-permute-start.4 = (bf16[3,160,768]{2,1,0:T(8,128)(2,1)}, bf16[3,160,768]{2,1,0:T(8,128)(2,1)S(1)}, u32[]{:S(2)}, u32[]{:S(2)}) collective-permute-start(bf16[3,160,768]{2,1,0:T(8,128)(2,1)} %bitcast.8), channel_id=1, source_target_pairs={{9,10},{10,9},{4,5},{6,7},{12,13},{14,15},{5,4},{7,6},{13,12},{15,... | collective-permute-start | bytes 2211848 | tf_op jit(solution)/shard_map/ppermute | solution.py:328
  4.9 1.9 %collective-permute-start.3 = (bf16[3,160,768]{2,1,0:T(8,128)(2,1)}, bf16[3,160,768]{2,1,0:T(8,128)(2,1)S(1)}, u32[]{:S(2)}, u32[]{:S(2)}) collective-permute-start(bf16[3,160,768]{2,1,0:T(8,128)(2,1)} %bitcast.9), channel_id=1, source_target_pairs={{8,9},{10,11},{9,8},{11,10},{5,6},{13,14},{6,5},{14,13},{24,25},{2... | collective-permute-start | bytes 2211848 | tf_op jit(solution)/shard_map/ppermute | solution.py:328
  6.9 0.0 copy-start.3
  6.9 0.9 %copy-done.3 = bf16[160,640]{1,0:T(8,128)(2,1)S(1)} copy-done((bf16[160,640]{1,0:T(8,128)(2,1)S(1)}, bf16[160,640]{1,0:T(8,128)(2,1)}, u32[]{:S(2)}) %copy-start.3) | copy-done | bytes 204824
  7.8 0.0 copy-start.4
  7.8 0.8 %copy-done.4 = f32[7,7,160]{2,1,0:T(8,128)S(1)} copy-done((f32[7,7,160]{2,1,0:T(8,128)S(1)}, f32[7,7,160]{2,1,0:T(8,128)}, u32[]{:S(2)}) %copy-start.4) | copy-done | bytes 31384
  8.6 0.0 copy-start.5
  8.6 0.7 copy-done.5
  9.3 0.0 copy-start.6
  9.3 0.7 copy-done.6
  10.0 0.0 copy-start.7
  10.0 0.7 copy-done.7
  10.7 0.0 copy-start.8
  10.7 0.7 copy-done.8
  11.4 0.0 copy-start.9
  11.4 2.7 %prepare.1 = (bf16[3,7,160,144]{3,2,1,0:T(8,128)(2,1)S(1)}, f32[160,128]{1,0:T(8,128)S(1)}, f32[160,128]{1,0:T(8,128)S(1)}, bf16[640,176]{1,0:T(8,128)(2,1)S(1)}, f32[3,768]{1,0:T(4,128)S(1)}) custom-call(f32[7,7,160]{2,1,0:T(8,128)S(1)} %copy-done.4, f32[1,160]{1,0:T(1,128)S(1)} %bitcast.17, f32[1,160]{1,0:T(1,128)S(1)} %bitcast.18, ...), custom_call_target="tpu_custom_call" | custom-call | tf_op jit(solution)/shard_map/prepare/pallas_call | solution.py:350
  14.1 0.0 collective-permute-done
  14.1 1.2 %broadcast_select_fusion.refs_1_ = bf16[3,160,768]{2,1,0:T(8,128)(2,1)S(1)} fusion(bf16[3,160,768]{2,1,0:T(8,128)(2,1)S(1)} %collective-permute-done, pred[]{:T(512)S(6)} %and.4, bf16[1,3,160,768]{3,2,1,0:T(8,128)(2,1)} %param.10), kind=kLoop, calls=%fused_computation.1 | loop fusion | flops 368640 | bytes 2211841 | tf_op jit(solution)/shard_map/jit(_where)/select_n | solution.py:411
  15.3 0.0 copy-start
  15.3 3.2 %collective-permute-start.2 = (bf16[3,160,768]{2,1,0:T(8,128)(2,1)S(1)}, bf16[3,160,768]{2,1,0:T(8,128)(2,1)S(1)}, u32[]{:S(2)}, u32[]{:S(2)}) collective-permute-start(bf16[3,160,768]{2,1,0:T(8,128)(2,1)S(1)} %broadcast_select_fusion.refs_1_), channel_id=1, source_target_pairs={{1,2},{9,10},{2,1},{10,9},{17,18},{25,26},{18,17},{26,25}} | collective-permute-start | bytes 2211848 | tf_op jit(solution)/shard_map/ppermute | solution.py:328
  18.5 1.9 %collective-permute-start.1 = (bf16[3,160,768]{2,1,0:T(8,128)(2,1)S(1)}, bf16[3,160,768]{2,1,0:T(8,128)(2,1)S(1)}, u32[]{:S(2)}, u32[]{:S(2)}) collective-permute-start(bf16[3,160,768]{2,1,0:T(8,128)(2,1)S(1)} %broadcast_select_fusion.refs_1_), channel_id=1, source_target_pairs={{0,1},{2,3},{8,9},{10,11},{1,0},{3,2},{9,8},{11,10},{16,17},{18,19... | collective-permute-start | bytes 2211848 | tf_op jit(solution)/shard_map/ppermute | solution.py:328
  20.5 0.0 copy-done.2
  20.5 0.0 copy-done.9
  20.5 3.5 %filters.1.refs_12_.refs_6_.refs_9_.refs_8_ = bf16[3,768,768]{2,1,0:T(8,128)(2,1)S(1)} custom-call(s32[12]{0:T(128)S(1)} %copy-done.9, bf16[768,768]{1,0:T(8,128)(2,1)S(1)} %copy-done.2), custom_call_target="tpu_custom_call" | custom-call | tf_op jit(solution)/shard_map/filters/pallas_call | solution.py:365
  24.0 0.0 copy-start.1
  24.0 1.5 %collective-permute-start.6 = (bf16[3,160,768]{2,1,0:T(8,128)(2,1)S(1)}, bf16[3,160,768]{2,1,0:T(8,128)(2,1)S(1)}, u32[]{:S(2)}, u32[]{:S(2)}) collective-permute-start(bf16[3,160,768]{2,1,0:T(8,128)(2,1)S(1)} %broadcast_select_fusion.refs_1_), channel_id=1, source_target_pairs={{0,4},{1,5},{2,6},{3,7},{8,12},{9,13},{10,14},{11,15},{16,20},{17,... | collective-permute-start | bytes 2211848 | tf_op jit(solution)/shard_map/ppermute | solution.py:328
  25.5 0.0 collective-permute-done.4.second
  25.5 0.0 collective-permute-done.3.first
  25.5 0.0 copy-done
  25.5 2.8 %conv.1.refs_1_ = f32[3,160,768]{2,1,0:T(8,128)S(1)} custom-call(bf16[3,160,768]{2,1,0:T(8,128)(2,1)S(1)} %collective-permute-done.3.first, bf16[3,160,768]{2,1,0:T(8,128)(2,1)S(1)} %bitcast.10, bf16[3,160,768]{2,1,0:T(8,128)(2,1)S(1)} %collective-permute-done.4.second, bf16[3,7,160,144]{3,2,1,0:T(8,128)(2,1)S(1)} %get-tuple-element.27.taps.refs_6_.refs_3_), custom_call_target="tpu_custom_call" | custom-call | tf_op jit(solution)/shard_map/conv/pallas_call | solution.py:386
  28.3 2.4 %collective-permute-done.2.refs_2_ = bf16[3,160,768]{2,1,0:T(8,128)(2,1)S(1)} collective-permute-done((bf16[3,160,768]{2,1,0:T(8,128)(2,1)S(1)}, bf16[3,160,768]{2,1,0:T(8,128)(2,1)S(1)}, u32[]{:S(2)}, u32[]{:S(2)}) %collective-permute-start.2) | collective-permute-done | bytes 737312 | tf_op jit(solution)/shard_map/ppermute | solution.py:328
  30.8 1.1 %collective-permute-done.1.refs_0_ = bf16[3,160,768]{2,1,0:T(8,128)(2,1)S(1)} collective-permute-done((bf16[3,160,768]{2,1,0:T(8,128)(2,1)S(1)}, bf16[3,160,768]{2,1,0:T(8,128)(2,1)S(1)}, u32[]{:S(2)}, u32[]{:S(2)}) %collective-permute-start.1) | collective-permute-done | bytes 737312 | tf_op jit(solution)/shard_map/ppermute | solution.py:328
  31.9 1.3 %collective-permute-start.7 = (bf16[3,160,768]{2,1,0:T(8,128)(2,1)S(1)}, bf16[3,160,768]{2,1,0:T(8,128)(2,1)S(1)}, u32[]{:S(2)}, u32[]{:S(2)}) collective-permute-start(bf16[3,160,768]{2,1,0:T(8,128)(2,1)S(1)} %collective-permute-done.1.refs_0_), channel_id=1, source_target_pairs={{0,4},{1,5},{2,6},{3,7},{8,12},{9,13},{10,14},{11,15},{16,20},{17,... | collective-permute-start | bytes 2211848 | tf_op jit(solution)/shard_map/ppermute | solution.py:328
  33.2 1.5 %collective-permute-start.5 = (bf16[3,160,768]{2,1,0:T(8,128)(2,1)S(1)}, bf16[3,160,768]{2,1,0:T(8,128)(2,1)S(1)}, u32[]{:S(2)}, u32[]{:S(2)}) collective-permute-start(bf16[3,160,768]{2,1,0:T(8,128)(2,1)S(1)} %collective-permute-done.2.refs_2_), channel_id=1, source_target_pairs={{0,4},{1,5},{2,6},{3,7},{8,12},{9,13},{10,14},{11,15},{16,20},{17,... | collective-permute-start | bytes 2211848 | tf_op jit(solution)/shard_map/ppermute | solution.py:328
  34.7 0.0 collective-permute-done.6.refs_4_
  34.8 0.2 collective-permute-done.7.refs_5_
  35.0 1.3 %collective-permute-done.5.refs_3_ = bf16[3,160,768]{2,1,0:T(8,128)(2,1)S(1)} collective-permute-done((bf16[3,160,768]{2,1,0:T(8,128)(2,1)S(1)}, bf16[3,160,768]{2,1,0:T(8,128)(2,1)S(1)}, u32[]{:S(2)}, u32[]{:S(2)}) %collective-permute-start.5) | collective-permute-done | bytes 737312 | tf_op jit(solution)/shard_map/ppermute | solution.py:328
  36.3 0.0 copy-done.1
  36.3 5.4 %control.2 = (bf16[3,160,768]{2,1,0:T(8,128)(2,1)S(1)}, f32[3,160,768]{2,1,0:T(8,128)S(1)}, f32[3,1,768]{2,1,0:T(1,128)S(1)}, f32[3,640,768]{2,1,0:T(8,128)S(1)}) custom-call(bf16[3,160,768]{2,1,0:T(8,128)(2,1)S(1)} %collective-permute-done.1.refs_0_, bf16[3,160,768]{2,1,0:T(8,128)(2,1)S(1)} %broadcast_select_fusion.refs_1_, ...), custom_call_target="tpu_custom_call" | custom-call | tf_op jit(solution)/shard_map/control/pallas_call | solution.py:375
  41.8 1.9 %collective-permute-start.10 = (bf16[3,160,768]{2,1,0:T(8,128)(2,1)S(1)}, bf16[3,160,768]{2,1,0:T(8,128)(2,1)S(1)}, u32[]{:S(2)}, u32[]{:S(2)}) collective-permute-start(bf16[3,160,768]{2,1,0:T(8,128)(2,1)S(1)} %get-tuple-element.39.refs_10_.refs_1_), channel_id=1, source_target_pairs={{0,1},{2,3},{8,9},{10,11},{1,0},{3,2},{9,8},{11,10},{5,6},{13,14},... | collective-permute-start | bytes 2211848 | tf_op jit(solution)/shard_map/ppermute | solution.py:328
  43.7 4.6 %tangent.2.refs_1_ = bf16[3,160,768]{2,1,0:T(8,128)(2,1)S(1)} custom-call(bf16[3,160,768]{2,1,0:T(8,128)(2,1)S(1)} %bitcast.11, f32[3,160,768]{2,1,0:T(8,128)S(1)} %conv.1.refs_1_, f32[160,128]{1,0:T(8,128)S(1)} %get-tuple-element.29.refs_7_.refs_2_.refs_4_, bf16[640,176]{1,0:T(8,128)(2,1)S(1)} %get-tuple-element.30.refs_9_.refs_3_.refs_6_.refs_5_, ...), custom_call_target="tpu_custom_call" | custom-call | tf_op jit(solution)/shard_map/tangent/pallas_call | solution.py:396
  48.3 2.7 %collective-permute-start.9 = (bf16[3,160,768]{2,1,0:T(8,128)(2,1)S(1)}, bf16[3,160,768]{2,1,0:T(8,128)(2,1)S(1)}, u32[]{:S(2)}, u32[]{:S(2)}) collective-permute-start(bf16[3,160,768]{2,1,0:T(8,128)(2,1)S(1)} %tangent.2.refs_1_), channel_id=1, source_target_pairs={{9,10},{10,9},{4,5},{6,7},{12,13},{14,15},{5,4},{7,6},{13,12},{15,... | collective-permute-start | bytes 2211848 | tf_op jit(solution)/shard_map/ppermute | solution.py:328
  51.1 2.1 %collective-permute-start.8 = (bf16[3,160,768]{2,1,0:T(8,128)(2,1)S(1)}, bf16[3,160,768]{2,1,0:T(8,128)(2,1)S(1)}, u32[]{:S(2)}, u32[]{:S(2)}) collective-permute-start(bf16[3,160,768]{2,1,0:T(8,128)(2,1)S(1)} %tangent.2.refs_1_), channel_id=1, source_target_pairs={{8,9},{10,11},{9,8},{11,10},{5,6},{13,14},{6,5},{14,13},{24,25},{2... | collective-permute-start | bytes 2211848 | tf_op jit(solution)/shard_map/ppermute | solution.py:328
  53.2 3.3 %collective-permute-done.10.refs_0_ = bf16[3,160,768]{2,1,0:T(8,128)(2,1)S(1)} collective-permute-done((bf16[3,160,768]{2,1,0:T(8,128)(2,1)S(1)}, bf16[3,160,768]{2,1,0:T(8,128)(2,1)S(1)}, u32[]{:S(2)}, u32[]{:S(2)}) %collective-permute-start.10) | collective-permute-done | bytes 737312 | tf_op jit(solution)/shard_map/ppermute | solution.py:328
  56.6 0.1 collective-permute-start.11
  56.6 0.5 collective-permute-start.12
  57.1 1.2 %collective-permute-done.11 = bf16[3,80,768]{2,1,0:T(8,128)(2,1)S(1)} collective-permute-done((bf16[3,80,768]{2,1,0:T(8,128)(2,1)S(1)}, bf16[3,80,768]{2,1,0:T(8,128)(2,1)S(1)}, u32[]{:S(2)}, u32[]{:S(2)}) %collective-permute-start.11) | collective-permute-done | bytes 368672 | tf_op jit(solution)/shard_map/ppermute | solution.py:328
  58.3 0.5 collective-permute-done.12
  58.9 8.9 %control.3 = (bf16[3,160,768]{2,1,0:T(8,128)(2,1)S(1)}, f32[3,160,768]{2,1,0:T(8,128)S(1)}, f32[3,1,768]{2,1,0:T(1,128)S(1)}, f32[3,640,768]{2,1,0:T(8,128)S(1)}) custom-call(bf16[3,160,768]{2,1,0:T(8,128)(2,1)S(1)} %collective-permute-done.10.refs_0_, bf16[3,160,768]{2,1,0:T(8,128)(2,1)S(1)} %get-tuple-element.39.refs_10_.refs_1_, ...), custom_call_target="tpu_custom_call" | custom-call | tf_op jit(solution)/shard_map/control/pallas_call | solution.py:375
  67.8 1.4 %collective-permute-done.9.refs_2_ = bf16[3,160,768]{2,1,0:T(8,128)(2,1)S(1)} collective-permute-done((bf16[3,160,768]{2,1,0:T(8,128)(2,1)S(1)}, bf16[3,160,768]{2,1,0:T(8,128)(2,1)S(1)}, u32[]{:S(2)}, u32[]{:S(2)}) %collective-permute-start.9) | collective-permute-done | bytes 737312 | tf_op jit(solution)/shard_map/ppermute | solution.py:328
  69.2 1.7 %collective-permute-done.8.refs_0_ = bf16[3,160,768]{2,1,0:T(8,128)(2,1)S(1)} collective-permute-done((bf16[3,160,768]{2,1,0:T(8,128)(2,1)S(1)}, bf16[3,160,768]{2,1,0:T(8,128)(2,1)S(1)}, u32[]{:S(2)}, u32[]{:S(2)}) %collective-permute-start.8) | collective-permute-done | bytes 737312 | tf_op jit(solution)/shard_map/ppermute | solution.py:328
  70.9 5.6 %tangent.3 = bf16[3,160,768]{2,1,0:T(8,128)(2,1)} custom-call(bf16[3,160,768]{2,1,0:T(8,128)(2,1)S(1)} %collective-permute-done.8.refs_0_, bf16[3,160,768]{2,1,0:T(8,128)(2,1)S(1)} %tangent.2.refs_1_, bf16[3,160,768]{2,1,0:T(8,128)(2,1)S(1)} %collective-permute-done.9.refs_2_, bf16[3,7,160,144]{3,2,1,0:T(8,128)(2,1)S(1)} %get-tuple-element.27.taps.refs_6_.refs_3_, ...), custom_call_target="tpu_custom_call" | custom-call | tf_op jit(solution)/shard_map/tangent/pallas_call | solution.py:396
  (2 shorter events, 0.1 us)
Async XLA Ops:
  0.0 20.5 %copy-start.2 = (bf16[768,768]{1,0:T(8,128)(2,1)S(1)}, bf16[768,768]{1,0:T(8,128)(2,1)}, u32[]{:S(2)}) copy-start(bf16[768,768]{1,0:T(8,128)(2,1)} %constant.11.clone.refs_1_) | copy-start | bytes 3538948
  0.0 14.1 %collective-permute-start = (bf16[3,160,768]{2,1,0:T(8,128)(2,1)}, bf16[3,160,768]{2,1,0:T(8,128)(2,1)S(1)}, u32[]{:S(2)}, u32[]{:S(2)}) collective-permute-start(bf16[3,160,768]{2,1,0:T(8,128)(2,1)} %bitcast.7), channel_id=1, source_target_pairs={{0,8},{1,9},{2,10},{3,11},{16,24},{17,25},{18,26},{19,27}} | collective-permute-start | bytes 2211848 | tf_op jit(solution)/shard_map/ppermute | solution.py:328
  1.4 24.0 %collective-permute-start.4 = (bf16[3,160,768]{2,1,0:T(8,128)(2,1)}, bf16[3,160,768]{2,1,0:T(8,128)(2,1)S(1)}, u32[]{:S(2)}, u32[]{:S(2)}) collective-permute-start(bf16[3,160,768]{2,1,0:T(8,128)(2,1)} %bitcast.8), channel_id=1, source_target_pairs={{9,10},{10,9},{4,5},{6,7},{12,13},{14,15},{5,4},{7,6},{13,12},{15,... | collective-permute-start | bytes 2211848 | tf_op jit(solution)/shard_map/ppermute | solution.py:328
  4.9 20.6 %collective-permute-start.3 = (bf16[3,160,768]{2,1,0:T(8,128)(2,1)}, bf16[3,160,768]{2,1,0:T(8,128)(2,1)S(1)}, u32[]{:S(2)}, u32[]{:S(2)}) collective-permute-start(bf16[3,160,768]{2,1,0:T(8,128)(2,1)} %bitcast.9), channel_id=1, source_target_pairs={{8,9},{10,11},{9,8},{11,10},{5,6},{13,14},{6,5},{14,13},{24,25},{2... | collective-permute-start | bytes 2211848 | tf_op jit(solution)/shard_map/ppermute | solution.py:328
  6.9 0.9 %copy-start.3 = (bf16[160,640]{1,0:T(8,128)(2,1)S(1)}, bf16[160,640]{1,0:T(8,128)(2,1)}, u32[]{:S(2)}) copy-start(bf16[160,640]{1,0:T(8,128)(2,1)} %refs_3_.1) | copy-start | bytes 614404
  7.8 0.8 %copy-start.4 = (f32[7,7,160]{2,1,0:T(8,128)S(1)}, f32[7,7,160]{2,1,0:T(8,128)}, u32[]{:S(2)}) copy-start(f32[7,7,160]{2,1,0:T(8,128)} %refs_0_.2) | copy-start | bytes 94084
  8.6 0.7 copy-start.5
  9.3 0.7 copy-start.6
  10.0 0.7 copy-start.7
  10.7 0.7 copy-start.8
  11.4 9.1 %copy-start.9 = (s32[12]{0:T(128)S(1)}, s32[12]{0:T(128)}, u32[]{:S(2)}) copy-start(s32[12]{0:T(128)} %refs_0_.3) | copy-start | bytes 148
  15.3 10.2 %copy-start = (bf16[1,3,160,768]{3,2,1,0:T(8,128)(2,1)S(1)}, bf16[1,3,160,768]{3,2,1,0:T(8,128)(2,1)}, u32[]{:S(2)}) copy-start(bf16[1,3,160,768]{3,2,1,0:T(8,128)(2,1)} %param.10) | copy-start | bytes 2211844
  15.3 15.5 %collective-permute-start.2 = (bf16[3,160,768]{2,1,0:T(8,128)(2,1)S(1)}, bf16[3,160,768]{2,1,0:T(8,128)(2,1)S(1)}, u32[]{:S(2)}, u32[]{:S(2)}) collective-permute-start(bf16[3,160,768]{2,1,0:T(8,128)(2,1)S(1)} %broadcast_select_fusion.refs_1_), channel_id=1, source_target_pairs={{1,2},{9,10},{2,1},{10,9},{17,18},{25,26},{18,17},{26,25}} | collective-permute-start | bytes 2211848 | tf_op jit(solution)/shard_map/ppermute | solution.py:328
  18.5 13.4 %collective-permute-start.1 = (bf16[3,160,768]{2,1,0:T(8,128)(2,1)S(1)}, bf16[3,160,768]{2,1,0:T(8,128)(2,1)S(1)}, u32[]{:S(2)}, u32[]{:S(2)}) collective-permute-start(bf16[3,160,768]{2,1,0:T(8,128)(2,1)S(1)} %broadcast_select_fusion.refs_1_), channel_id=1, source_target_pairs={{0,1},{2,3},{8,9},{10,11},{1,0},{3,2},{9,8},{11,10},{16,17},{18,19... | collective-permute-start | bytes 2211848 | tf_op jit(solution)/shard_map/ppermute | solution.py:328
  24.0 12.4 %copy-start.1 = (bf16[640,160]{0,1:T(8,128)(2,1)S(1)}, bf16[640,160]{0,1:T(8,128)(2,1)}, u32[]{:S(2)}) copy-start(bf16[640,160]{0,1:T(8,128)(2,1)} %param.18) | copy-start | bytes 614404
  24.0 10.8 %collective-permute-start.6 = (bf16[3,160,768]{2,1,0:T(8,128)(2,1)S(1)}, bf16[3,160,768]{2,1,0:T(8,128)(2,1)S(1)}, u32[]{:S(2)}, u32[]{:S(2)}) collective-permute-start(bf16[3,160,768]{2,1,0:T(8,128)(2,1)S(1)} %broadcast_select_fusion.refs_1_), channel_id=1, source_target_pairs={{0,4},{1,5},{2,6},{3,7},{8,12},{9,13},{10,14},{11,15},{16,20},{17,... | collective-permute-start | bytes 2211848 | tf_op jit(solution)/shard_map/ppermute | solution.py:328
  31.9 3.1 %collective-permute-start.7 = (bf16[3,160,768]{2,1,0:T(8,128)(2,1)S(1)}, bf16[3,160,768]{2,1,0:T(8,128)(2,1)S(1)}, u32[]{:S(2)}, u32[]{:S(2)}) collective-permute-start(bf16[3,160,768]{2,1,0:T(8,128)(2,1)S(1)} %collective-permute-done.1.refs_0_), channel_id=1, source_target_pairs={{0,4},{1,5},{2,6},{3,7},{8,12},{9,13},{10,14},{11,15},{16,20},{17,... | collective-permute-start | bytes 2211848 | tf_op jit(solution)/shard_map/ppermute | solution.py:328
  33.2 3.1 %collective-permute-start.5 = (bf16[3,160,768]{2,1,0:T(8,128)(2,1)S(1)}, bf16[3,160,768]{2,1,0:T(8,128)(2,1)S(1)}, u32[]{:S(2)}, u32[]{:S(2)}) collective-permute-start(bf16[3,160,768]{2,1,0:T(8,128)(2,1)S(1)} %collective-permute-done.2.refs_2_), channel_id=1, source_target_pairs={{0,4},{1,5},{2,6},{3,7},{8,12},{9,13},{10,14},{11,15},{16,20},{17,... | collective-permute-start | bytes 2211848 | tf_op jit(solution)/shard_map/ppermute | solution.py:328
  41.8 14.7 %collective-permute-start.10 = (bf16[3,160,768]{2,1,0:T(8,128)(2,1)S(1)}, bf16[3,160,768]{2,1,0:T(8,128)(2,1)S(1)}, u32[]{:S(2)}, u32[]{:S(2)}) collective-permute-start(bf16[3,160,768]{2,1,0:T(8,128)(2,1)S(1)} %get-tuple-element.39.refs_10_.refs_1_), channel_id=1, source_target_pairs={{0,1},{2,3},{8,9},{10,11},{1,0},{3,2},{9,8},{11,10},{5,6},{13,14},... | collective-permute-start | bytes 2211848 | tf_op jit(solution)/shard_map/ppermute | solution.py:328
  48.3 20.9 %collective-permute-start.9 = (bf16[3,160,768]{2,1,0:T(8,128)(2,1)S(1)}, bf16[3,160,768]{2,1,0:T(8,128)(2,1)S(1)}, u32[]{:S(2)}, u32[]{:S(2)}) collective-permute-start(bf16[3,160,768]{2,1,0:T(8,128)(2,1)S(1)} %tangent.2.refs_1_), channel_id=1, source_target_pairs={{9,10},{10,9},{4,5},{6,7},{12,13},{14,15},{5,4},{7,6},{13,12},{15,... | collective-permute-start | bytes 2211848 | tf_op jit(solution)/shard_map/ppermute | solution.py:328
  51.1 19.9 %collective-permute-start.8 = (bf16[3,160,768]{2,1,0:T(8,128)(2,1)S(1)}, bf16[3,160,768]{2,1,0:T(8,128)(2,1)S(1)}, u32[]{:S(2)}, u32[]{:S(2)}) collective-permute-start(bf16[3,160,768]{2,1,0:T(8,128)(2,1)S(1)} %tangent.2.refs_1_), channel_id=1, source_target_pairs={{8,9},{10,11},{9,8},{11,10},{5,6},{13,14},{6,5},{14,13},{24,25},{2... | collective-permute-start | bytes 2211848 | tf_op jit(solution)/shard_map/ppermute | solution.py:328
  56.6 1.8 %collective-permute-start.11 = (bf16[3,80,768]{2,1,0:T(8,128)(2,1)S(1)}, bf16[3,80,768]{2,1,0:T(8,128)(2,1)S(1)}, u32[]{:S(2)}, u32[]{:S(2)}) collective-permute-start(bf16[3,80,768]{2,1,0:T(8,128)(2,1)S(1)} %get-tuple-element.45), channel_id=1, source_target_pairs={{0,4},{1,5},{2,6},{3,7},{8,12},{9,13},{10,14},{11,15},{4,0},{5,1},... | collective-permute-start | bytes 1105928 | tf_op jit(solution)/shard_map/ppermute | solution.py:328
  56.6 2.2 %collective-permute-start.12 = (bf16[3,80,768]{2,1,0:T(8,128)(2,1)S(1)}, bf16[3,80,768]{2,1,0:T(8,128)(2,1)S(1)}, u32[]{:S(2)}, u32[]{:S(2)}) collective-permute-start(bf16[3,80,768]{2,1,0:T(8,128)(2,1)S(1)} %get-tuple-element.46), channel_id=1, source_target_pairs={{0,4},{1,5},{2,6},{3,7},{8,12},{9,13},{10,14},{11,15},{4,0},{5,1},... | collective-permute-start | bytes 1105928 | tf_op jit(solution)/shard_map/ppermute | solution.py:328

commit v8 on v7

--- a/solution.py
+++ b/solution.py
@@ -248,7 +248,11 @@
     refs = refs[10:]
     if not ready:
         conv, refs = refs[0], refs[1:]
-    normed, normed_b, hidden, hidden_b, act, act_b, raw = refs
+    normed, normed_b, hidden, hidden_b, act, act_b, raw = refs[:7]
+    if not ready:
+        done, sent = refs[7:]
+    else:
+        done = out
     normed, hidden, act = (normed, normed_b), (hidden, hidden_b), (act, act_b)
     rows, channels, width = advanced.shape
     hid = w_in.shape[0]
@@ -278,17 +282,26 @@
             land[pl.ds(r, 1), at] * (own[r, :channels, at].astype(f32) + update)
         ).astype(bf16)
         if at.stop == width:
-            polar_filter(raw, filters, out, r)
+            polar_filter(raw, filters, done, r)
+            if not ready:
+                pltpu.make_async_copy(done.at[r], out.at[r], sent.at[r]).start()
 
     @pl.when(is_control)
     def _():
-        out[:, :channels, :] = advanced[...]
+        done[...] = advanced[...]
+        if not ready:
+            for r in range(rows):
+                pltpu.make_async_copy(done.at[r], out.at[r], sent.at[r]).start()
 
     @pl.when(jnp.logical_not(is_control))
     def _():
         if not ready:
             convolve(read(near), read(own), read(far), taps, conv)
         pipeline(rows, across, False, first, mix, third)
+
+    if not ready:
+        for r in range(rows):
+            pltpu.make_async_copy(done.at[r], out.at[r], sent.at[r]).wait()
 
 
 def scratch(rows, channels, width, hid, bias_rows, conv=True):
@@ -397,8 +410,9 @@
             lambda *refs: tangent_kernel(ready, *refs),
             out_shape=field,
             in_specs=[VMEM] * (9 + len(inputs)),
-            out_specs=VMEM,
-            scratch_shapes=scratch(rows, channels, width, hid, 0, not ready),
+            out_specs=VMEM if ready else pl.BlockSpec(memory_space=pl.ANY),
+            scratch_shapes=scratch(rows, channels, width, hid, 0, not ready)
+            + ([] if ready else [pltpu.VMEM(field.shape, bf16), pltpu.SemaphoreType.DMA((rows,))]),
             compiler_params=params,
             name="tangent",
         )(*inputs, gain, w_in, w_out, land, filters, unit, scale, slope, advanced)

time: 77.1 us -> 77.2 us (level)
  no operation moved by 1% of the time
where the time goes in v8:
time: 77.2 us; the launch traced here: 76.6 us
  Pallas kernels  33.4 us (43%)
  starting transfers between devices  23.6 us (31%)
  waiting for transfers between devices  13.3 us (17%)
  local copies, waits for them, and re-layouts  4.56 us (6%)
  other arithmetic  1.25 us (2%)
    ppermute x13, starting transfers between devices, send(): lax.ppermute(block, ('mem', 'lat'), [(a * bands + i, b * bands + j) for (...  23.6 us
    pallas_call x2, Pallas kernels, control_step(): pl.pallas_call(control_kernel, out_shape=(field, shape(rows, channels, wi...  14.3 us
    ppermute x13, waiting for transfers between devices, send(): lax.ppermute(block, ('mem', 'lat'), [(a * bands + i, b * bands + j) for (...  13.3 us
    pallas_call x2, Pallas kernels, tangent_step(): pl.pallas_call(lambda *refs: tangent_kernel(ready, *refs), out_shape=fiel...  10.1 us
    unnamed x20, local copies, waits for them, and re-layouts  4.51 us
    pallas_call x1, Pallas kernels, per_device(): pl.pallas_call(lambda *refs: filter_kernel(bands, *refs), out_shape=shape...  3.49 us
    pallas_call x1, Pallas kernels, conv_step(): pl.pallas_call(conv_kernel, out_shape=shape(rows, channels, width), in_sp...  2.85 us
    pallas_call x1, Pallas kernels, per_device(): pl.pallas_call(prepare_kernel, out_shape=(shape(rows, TAPS, channels, (ro...  2.68 us
  transfers between devices with their start and end apart: 13, of which 9 were waited for; matrix products, arithmetic and copies ran while one was open for 2% of the time, Pallas kernels for 29%

profile of v8, /device:TPU:10, one launch (start us, length us, event | category | flops | bytes accessed | tf_op | source)
XLA Modules:
  0.0 76.6 jit_solution(18308328602732318400)
XLA Ops:
  0.0 0.0 copy-start.2
  0.0 1.4 %collective-permute-start = (bf16[3,160,768]{2,1,0:T(8,128)(2,1)}, bf16[3,160,768]{2,1,0:T(8,128)(2,1)S(1)}, u32[]{:S(2)}, u32[]{:S(2)}) collective-permute-start(bf16[3,160,768]{2,1,0:T(8,128)(2,1)} %bitcast.7), channel_id=1, source_target_pairs={{0,8},{1,9},{2,10},{3,11},{16,24},{17,25},{18,26},{19,27}} | collective-permute-start | bytes 2211848 | tf_op jit(solution)/shard_map/ppermute | solution.py:341
  1.4 3.5 %collective-permute-start.4 = (bf16[3,160,768]{2,1,0:T(8,128)(2,1)}, bf16[3,160,768]{2,1,0:T(8,128)(2,1)S(1)}, u32[]{:S(2)}, u32[]{:S(2)}) collective-permute-start(bf16[3,160,768]{2,1,0:T(8,128)(2,1)} %bitcast.8), channel_id=1, source_target_pairs={{9,10},{10,9},{4,5},{6,7},{12,13},{14,15},{5,4},{7,6},{13,12},{15,... | collective-permute-start | bytes 2211848 | tf_op jit(solution)/shard_map/ppermute | solution.py:341
  4.9 1.9 %collective-permute-start.3 = (bf16[3,160,768]{2,1,0:T(8,128)(2,1)}, bf16[3,160,768]{2,1,0:T(8,128)(2,1)S(1)}, u32[]{:S(2)}, u32[]{:S(2)}) collective-permute-start(bf16[3,160,768]{2,1,0:T(8,128)(2,1)} %bitcast.9), channel_id=1, source_target_pairs={{8,9},{10,11},{9,8},{11,10},{5,6},{13,14},{6,5},{14,13},{24,25},{2... | collective-permute-start | bytes 2211848 | tf_op jit(solution)/shard_map/ppermute | solution.py:341
  6.9 0.0 copy-start.3
  6.9 0.9 %copy-done.3 = bf16[160,640]{1,0:T(8,128)(2,1)S(1)} copy-done((bf16[160,640]{1,0:T(8,128)(2,1)S(1)}, bf16[160,640]{1,0:T(8,128)(2,1)}, u32[]{:S(2)}) %copy-start.3) | copy-done | bytes 204824
  7.8 0.0 copy-start.4
  7.8 0.8 %copy-done.4 = f32[7,7,160]{2,1,0:T(8,128)S(1)} copy-done((f32[7,7,160]{2,1,0:T(8,128)S(1)}, f32[7,7,160]{2,1,0:T(8,128)}, u32[]{:S(2)}) %copy-start.4) | copy-done | bytes 31384
  8.6 0.0 copy-start.5
  8.6 0.7 copy-done.5
  9.3 0.0 copy-start.6
  9.3 0.7 copy-done.6
  10.0 0.0 copy-start.7
  10.0 0.7 copy-done.7
  10.7 0.0 copy-start.8
  10.7 0.7 copy-done.8
  11.4 0.0 copy-start.9
  11.4 2.7 %prepare.1 = (bf16[3,7,160,144]{3,2,1,0:T(8,128)(2,1)S(1)}, f32[160,128]{1,0:T(8,128)S(1)}, f32[160,128]{1,0:T(8,128)S(1)}, bf16[640,176]{1,0:T(8,128)(2,1)S(1)}, f32[3,768]{1,0:T(4,128)S(1)}) custom-call(f32[7,7,160]{2,1,0:T(8,128)S(1)} %copy-done.4, f32[1,160]{1,0:T(1,128)S(1)} %bitcast.17, f32[1,160]{1,0:T(1,128)S(1)} %bitcast.18, ...), custom_call_target="tpu_custom_call" | custom-call | tf_op jit(solution)/shard_map/prepare/pallas_call | solution.py:363
  14.1 0.0 collective-permute-done
  14.1 1.2 %broadcast_select_fusion.refs_1_ = bf16[3,160,768]{2,1,0:T(8,128)(2,1)S(1)} fusion(bf16[3,160,768]{2,1,0:T(8,128)(2,1)S(1)} %collective-permute-done, pred[]{:T(512)S(6)} %and.4, bf16[1,3,160,768]{3,2,1,0:T(8,128)(2,1)} %param.10), kind=kLoop, calls=%fused_computation.1 | loop fusion | flops 368640 | bytes 2211841 | tf_op jit(solution)/shard_map/jit(_where)/select_n | solution.py:425
  15.3 0.0 copy-start
  15.3 3.2 %collective-permute-start.2 = (bf16[3,160,768]{2,1,0:T(8,128)(2,1)S(1)}, bf16[3,160,768]{2,1,0:T(8,128)(2,1)S(1)}, u32[]{:S(2)}, u32[]{:S(2)}) collective-permute-start(bf16[3,160,768]{2,1,0:T(8,128)(2,1)S(1)} %broadcast_select_fusion.refs_1_), channel_id=1, source_target_pairs={{1,2},{9,10},{2,1},{10,9},{17,18},{25,26},{18,17},{26,25}} | collective-permute-start | bytes 2211848 | tf_op jit(solution)/shard_map/ppermute | solution.py:341
  18.5 1.9 %collective-permute-start.1 = (bf16[3,160,768]{2,1,0:T(8,128)(2,1)S(1)}, bf16[3,160,768]{2,1,0:T(8,128)(2,1)S(1)}, u32[]{:S(2)}, u32[]{:S(2)}) collective-permute-start(bf16[3,160,768]{2,1,0:T(8,128)(2,1)S(1)} %broadcast_select_fusion.refs_1_), channel_id=1, source_target_pairs={{0,1},{2,3},{8,9},{10,11},{1,0},{3,2},{9,8},{11,10},{16,17},{18,19... | collective-permute-start | bytes 2211848 | tf_op jit(solution)/shard_map/ppermute | solution.py:341
  20.5 0.0 copy-done.2
  20.5 0.0 copy-done.9
  20.5 3.5 %filters.1.refs_12_.refs_6_.refs_9_.refs_8_ = bf16[3,768,768]{2,1,0:T(8,128)(2,1)S(1)} custom-call(s32[12]{0:T(128)S(1)} %copy-done.9, bf16[768,768]{1,0:T(8,128)(2,1)S(1)} %copy-done.2), custom_call_target="tpu_custom_call" | custom-call | tf_op jit(solution)/shard_map/filters/pallas_call | solution.py:378
  24.0 0.0 copy-start.1
  24.0 1.5 %collective-permute-start.6 = (bf16[3,160,768]{2,1,0:T(8,128)(2,1)S(1)}, bf16[3,160,768]{2,1,0:T(8,128)(2,1)S(1)}, u32[]{:S(2)}, u32[]{:S(2)}) collective-permute-start(bf16[3,160,768]{2,1,0:T(8,128)(2,1)S(1)} %broadcast_select_fusion.refs_1_), channel_id=1, source_target_pairs={{0,4},{1,5},{2,6},{3,7},{8,12},{9,13},{10,14},{11,15},{16,20},{17,... | collective-permute-start | bytes 2211848 | tf_op jit(solution)/shard_map/ppermute | solution.py:341
  25.5 0.0 collective-permute-done.4.second
  25.5 0.0 collective-permute-done.3.first
  25.5 0.0 copy-done
  25.5 2.8 %conv.1.refs_1_ = f32[3,160,768]{2,1,0:T(8,128)S(1)} custom-call(bf16[3,160,768]{2,1,0:T(8,128)(2,1)S(1)} %collective-permute-done.3.first, bf16[3,160,768]{2,1,0:T(8,128)(2,1)S(1)} %bitcast.10, bf16[3,160,768]{2,1,0:T(8,128)(2,1)S(1)} %collective-permute-done.4.second, bf16[3,7,160,144]{3,2,1,0:T(8,128)(2,1)S(1)} %get-tuple-element.27.taps.refs_6_.refs_3_), custom_call_target="tpu_custom_call" | custom-call | tf_op jit(solution)/shard_map/conv/pallas_call | solution.py:399
  28.3 2.4 %collective-permute-done.2.refs_2_ = bf16[3,160,768]{2,1,0:T(8,128)(2,1)S(1)} collective-permute-done((bf16[3,160,768]{2,1,0:T(8,128)(2,1)S(1)}, bf16[3,160,768]{2,1,0:T(8,128)(2,1)S(1)}, u32[]{:S(2)}, u32[]{:S(2)}) %collective-permute-start.2) | collective-permute-done | bytes 737312 | tf_op jit(solution)/shard_map/ppermute | solution.py:341
  30.8 1.1 %collective-permute-done.1.refs_0_ = bf16[3,160,768]{2,1,0:T(8,128)(2,1)S(1)} collective-permute-done((bf16[3,160,768]{2,1,0:T(8,128)(2,1)S(1)}, bf16[3,160,768]{2,1,0:T(8,128)(2,1)S(1)}, u32[]{:S(2)}, u32[]{:S(2)}) %collective-permute-start.1) | collective-permute-done | bytes 737312 | tf_op jit(solution)/shard_map/ppermute | solution.py:341
  31.9 1.3 %collective-permute-start.7 = (bf16[3,160,768]{2,1,0:T(8,128)(2,1)S(1)}, bf16[3,160,768]{2,1,0:T(8,128)(2,1)S(1)}, u32[]{:S(2)}, u32[]{:S(2)}) collective-permute-start(bf16[3,160,768]{2,1,0:T(8,128)(2,1)S(1)} %collective-permute-done.1.refs_0_), channel_id=1, source_target_pairs={{0,4},{1,5},{2,6},{3,7},{8,12},{9,13},{10,14},{11,15},{16,20},{17,... | collective-permute-start | bytes 2211848 | tf_op jit(solution)/shard_map/ppermute | solution.py:341
  33.2 1.5 %collective-permute-start.5 = (bf16[3,160,768]{2,1,0:T(8,128)(2,1)S(1)}, bf16[3,160,768]{2,1,0:T(8,128)(2,1)S(1)}, u32[]{:S(2)}, u32[]{:S(2)}) collective-permute-start(bf16[3,160,768]{2,1,0:T(8,128)(2,1)S(1)} %collective-permute-done.2.refs_2_), channel_id=1, source_target_pairs={{0,4},{1,5},{2,6},{3,7},{8,12},{9,13},{10,14},{11,15},{16,20},{17,... | collective-permute-start | bytes 2211848 | tf_op jit(solution)/shard_map/ppermute | solution.py:341
  34.7 0.0 collective-permute-done.6.refs_4_
  34.8 0.2 collective-permute-done.7.refs_5_
  35.0 1.3 %collective-permute-done.5.refs_3_ = bf16[3,160,768]{2,1,0:T(8,128)(2,1)S(1)} collective-permute-done((bf16[3,160,768]{2,1,0:T(8,128)(2,1)S(1)}, bf16[3,160,768]{2,1,0:T(8,128)(2,1)S(1)}, u32[]{:S(2)}, u32[]{:S(2)}) %collective-permute-start.5) | collective-permute-done | bytes 737312 | tf_op jit(solution)/shard_map/ppermute | solution.py:341
  36.3 0.0 copy-done.1
  36.3 5.4 %control.2 = (bf16[3,160,768]{2,1,0:T(8,128)(2,1)S(1)}, f32[3,160,768]{2,1,0:T(8,128)S(1)}, f32[3,1,768]{2,1,0:T(1,128)S(1)}, f32[3,640,768]{2,1,0:T(8,128)S(1)}) custom-call(bf16[3,160,768]{2,1,0:T(8,128)(2,1)S(1)} %collective-permute-done.1.refs_0_, bf16[3,160,768]{2,1,0:T(8,128)(2,1)S(1)} %broadcast_select_fusion.refs_1_, ...), custom_call_target="tpu_custom_call" | custom-call | tf_op jit(solution)/shard_map/control/pallas_call | solution.py:388
  41.8 1.9 %collective-permute-start.10 = (bf16[3,160,768]{2,1,0:T(8,128)(2,1)S(1)}, bf16[3,160,768]{2,1,0:T(8,128)(2,1)S(1)}, u32[]{:S(2)}, u32[]{:S(2)}) collective-permute-start(bf16[3,160,768]{2,1,0:T(8,128)(2,1)S(1)} %get-tuple-element.39.refs_10_.refs_1_), channel_id=1, source_target_pairs={{0,1},{2,3},{8,9},{10,11},{1,0},{3,2},{9,8},{11,10},{5,6},{13,14},... | collective-permute-start | bytes 2211848 | tf_op jit(solution)/shard_map/ppermute | solution.py:341
  43.7 4.6 %tangent.2.refs_1_ = bf16[3,160,768]{2,1,0:T(8,128)(2,1)S(1)} custom-call(bf16[3,160,768]{2,1,0:T(8,128)(2,1)S(1)} %bitcast.11, f32[3,160,768]{2,1,0:T(8,128)S(1)} %conv.1.refs_1_, f32[160,128]{1,0:T(8,128)S(1)} %get-tuple-element.29.refs_7_.refs_2_.refs_4_, bf16[640,176]{1,0:T(8,128)(2,1)S(1)} %get-tuple-element.30.refs_9_.refs_3_.refs_6_.refs_5_, ...), custom_call_target="tpu_custom_call" | custom-call | tf_op jit(solution)/shard_map/tangent/pallas_call | solution.py:409
  48.3 2.7 %collective-permute-start.9 = (bf16[3,160,768]{2,1,0:T(8,128)(2,1)S(1)}, bf16[3,160,768]{2,1,0:T(8,128)(2,1)S(1)}, u32[]{:S(2)}, u32[]{:S(2)}) collective-permute-start(bf16[3,160,768]{2,1,0:T(8,128)(2,1)S(1)} %tangent.2.refs_1_), channel_id=1, source_target_pairs={{9,10},{10,9},{4,5},{6,7},{12,13},{14,15},{5,4},{7,6},{13,12},{15,... | collective-permute-start | bytes 2211848 | tf_op jit(solution)/shard_map/ppermute | solution.py:341
  51.1 2.1 %collective-permute-start.8 = (bf16[3,160,768]{2,1,0:T(8,128)(2,1)S(1)}, bf16[3,160,768]{2,1,0:T(8,128)(2,1)S(1)}, u32[]{:S(2)}, u32[]{:S(2)}) collective-permute-start(bf16[3,160,768]{2,1,0:T(8,128)(2,1)S(1)} %tangent.2.refs_1_), channel_id=1, source_target_pairs={{8,9},{10,11},{9,8},{11,10},{5,6},{13,14},{6,5},{14,13},{24,25},{2... | collective-permute-start | bytes 2211848 | tf_op jit(solution)/shard_map/ppermute | solution.py:341
  53.2 3.3 %collective-permute-done.10.refs_0_ = bf16[3,160,768]{2,1,0:T(8,128)(2,1)S(1)} collective-permute-done((bf16[3,160,768]{2,1,0:T(8,128)(2,1)S(1)}, bf16[3,160,768]{2,1,0:T(8,128)(2,1)S(1)}, u32[]{:S(2)}, u32[]{:S(2)}) %collective-permute-start.10) | collective-permute-done | bytes 737312 | tf_op jit(solution)/shard_map/ppermute | solution.py:341
  56.6 0.1 collective-permute-start.11
  56.6 0.5 collective-permute-start.12
  57.1 1.2 %collective-permute-done.11 = bf16[3,80,768]{2,1,0:T(8,128)(2,1)S(1)} collective-permute-done((bf16[3,80,768]{2,1,0:T(8,128)(2,1)S(1)}, bf16[3,80,768]{2,1,0:T(8,128)(2,1)S(1)}, u32[]{:S(2)}, u32[]{:S(2)}) %collective-permute-start.11) | collective-permute-done | bytes 368672 | tf_op jit(solution)/shard_map/ppermute | solution.py:341
  58.3 0.5 collective-permute-done.12
  58.9 8.9 %control.3 = (bf16[3,160,768]{2,1,0:T(8,128)(2,1)S(1)}, f32[3,160,768]{2,1,0:T(8,128)S(1)}, f32[3,1,768]{2,1,0:T(1,128)S(1)}, f32[3,640,768]{2,1,0:T(8,128)S(1)}) custom-call(bf16[3,160,768]{2,1,0:T(8,128)(2,1)S(1)} %collective-permute-done.10.refs_0_, bf16[3,160,768]{2,1,0:T(8,128)(2,1)S(1)} %get-tuple-element.39.refs_10_.refs_1_, ...), custom_call_target="tpu_custom_call" | custom-call | tf_op jit(solution)/shard_map/control/pallas_call | solution.py:388
  67.8 1.4 %collective-permute-done.9.refs_2_ = bf16[3,160,768]{2,1,0:T(8,128)(2,1)S(1)} collective-permute-done((bf16[3,160,768]{2,1,0:T(8,128)(2,1)S(1)}, bf16[3,160,768]{2,1,0:T(8,128)(2,1)S(1)}, u32[]{:S(2)}, u32[]{:S(2)}) %collective-permute-start.9) | collective-permute-done | bytes 737312 | tf_op jit(solution)/shard_map/ppermute | solution.py:341
  69.2 1.7 %collective-permute-done.8.refs_0_ = bf16[3,160,768]{2,1,0:T(8,128)(2,1)S(1)} collective-permute-done((bf16[3,160,768]{2,1,0:T(8,128)(2,1)S(1)}, bf16[3,160,768]{2,1,0:T(8,128)(2,1)S(1)}, u32[]{:S(2)}, u32[]{:S(2)}) %collective-permute-start.8) | collective-permute-done | bytes 737312 | tf_op jit(solution)/shard_map/ppermute | solution.py:341
  70.9 5.5 %tangent.3 = bf16[3,160,768]{2,1,0:T(8,128)(2,1)} custom-call(bf16[3,160,768]{2,1,0:T(8,128)(2,1)S(1)} %collective-permute-done.8.refs_0_, bf16[3,160,768]{2,1,0:T(8,128)(2,1)S(1)} %tangent.2.refs_1_, bf16[3,160,768]{2,1,0:T(8,128)(2,1)S(1)} %collective-permute-done.9.refs_2_, bf16[3,7,160,144]{3,2,1,0:T(8,128)(2,1)S(1)} %get-tuple-element.27.taps.refs_6_.refs_3_, ...), custom_call_target="tpu_custom_call" | custom-call | tf_op jit(solution)/shard_map/tangent/pallas_call | solution.py:409
  (2 shorter events, 0.1 us)
Async XLA Ops:
  0.0 20.5 %copy-start.2 = (bf16[768,768]{1,0:T(8,128)(2,1)S(1)}, bf16[768,768]{1,0:T(8,128)(2,1)}, u32[]{:S(2)}) copy-start(bf16[768,768]{1,0:T(8,128)(2,1)} %constant.11.clone.refs_1_) | copy-start | bytes 3538948
  0.0 14.1 %collective-permute-start = (bf16[3,160,768]{2,1,0:T(8,128)(2,1)}, bf16[3,160,768]{2,1,0:T(8,128)(2,1)S(1)}, u32[]{:S(2)}, u32[]{:S(2)}) collective-permute-start(bf16[3,160,768]{2,1,0:T(8,128)(2,1)} %bitcast.7), channel_id=1, source_target_pairs={{0,8},{1,9},{2,10},{3,11},{16,24},{17,25},{18,26},{19,27}} | collective-permute-start | bytes 2211848 | tf_op jit(solution)/shard_map/ppermute | solution.py:341
  1.4 24.0 %collective-permute-start.4 = (bf16[3,160,768]{2,1,0:T(8,128)(2,1)}, bf16[3,160,768]{2,1,0:T(8,128)(2,1)S(1)}, u32[]{:S(2)}, u32[]{:S(2)}) collective-permute-start(bf16[3,160,768]{2,1,0:T(8,128)(2,1)} %bitcast.8), channel_id=1, source_target_pairs={{9,10},{10,9},{4,5},{6,7},{12,13},{14,15},{5,4},{7,6},{13,12},{15,... | collective-permute-start | bytes 2211848 | tf_op jit(solution)/shard_map/ppermute | solution.py:341
  4.9 20.6 %collective-permute-start.3 = (bf16[3,160,768]{2,1,0:T(8,128)(2,1)}, bf16[3,160,768]{2,1,0:T(8,128)(2,1)S(1)}, u32[]{:S(2)}, u32[]{:S(2)}) collective-permute-start(bf16[3,160,768]{2,1,0:T(8,128)(2,1)} %bitcast.9), channel_id=1, source_target_pairs={{8,9},{10,11},{9,8},{11,10},{5,6},{13,14},{6,5},{14,13},{24,25},{2... | collective-permute-start | bytes 2211848 | tf_op jit(solution)/shard_map/ppermute | solution.py:341
  6.9 0.9 %copy-start.3 = (bf16[160,640]{1,0:T(8,128)(2,1)S(1)}, bf16[160,640]{1,0:T(8,128)(2,1)}, u32[]{:S(2)}) copy-start(bf16[160,640]{1,0:T(8,128)(2,1)} %refs_3_.1) | copy-start | bytes 614404
  7.8 0.8 %copy-start.4 = (f32[7,7,160]{2,1,0:T(8,128)S(1)}, f32[7,7,160]{2,1,0:T(8,128)}, u32[]{:S(2)}) copy-start(f32[7,7,160]{2,1,0:T(8,128)} %refs_0_.2) | copy-start | bytes 94084
  8.6 0.7 copy-start.5
  9.3 0.7 copy-start.6
  10.0 0.7 copy-start.7
  10.7 0.7 copy-start.8
  11.4 9.1 %copy-start.9 = (s32[12]{0:T(128)S(1)}, s32[12]{0:T(128)}, u32[]{:S(2)}) copy-start(s32[12]{0:T(128)} %refs_0_.3) | copy-start | bytes 148
  15.3 10.2 %copy-start = (bf16[1,3,160,768]{3,2,1,0:T(8,128)(2,1)S(1)}, bf16[1,3,160,768]{3,2,1,0:T(8,128)(2,1)}, u32[]{:S(2)}) copy-start(bf16[1,3,160,768]{3,2,1,0:T(8,128)(2,1)} %param.10) | copy-start | bytes 2211844
  15.3 15.5 %collective-permute-start.2 = (bf16[3,160,768]{2,1,0:T(8,128)(2,1)S(1)}, bf16[3,160,768]{2,1,0:T(8,128)(2,1)S(1)}, u32[]{:S(2)}, u32[]{:S(2)}) collective-permute-start(bf16[3,160,768]{2,1,0:T(8,128)(2,1)S(1)} %broadcast_select_fusion.refs_1_), channel_id=1, source_target_pairs={{1,2},{9,10},{2,1},{10,9},{17,18},{25,26},{18,17},{26,25}} | collective-permute-start | bytes 2211848 | tf_op jit(solution)/shard_map/ppermute | solution.py:341
  18.5 13.4 %collective-permute-start.1 = (bf16[3,160,768]{2,1,0:T(8,128)(2,1)S(1)}, bf16[3,160,768]{2,1,0:T(8,128)(2,1)S(1)}, u32[]{:S(2)}, u32[]{:S(2)}) collective-permute-start(bf16[3,160,768]{2,1,0:T(8,128)(2,1)S(1)} %broadcast_select_fusion.refs_1_), channel_id=1, source_target_pairs={{0,1},{2,3},{8,9},{10,11},{1,0},{3,2},{9,8},{11,10},{16,17},{18,19... | collective-permute-start | bytes 2211848 | tf_op jit(solution)/shard_map/ppermute | solution.py:341
  24.0 12.4 %copy-start.1 = (bf16[640,160]{0,1:T(8,128)(2,1)S(1)}, bf16[640,160]{0,1:T(8,128)(2,1)}, u32[]{:S(2)}) copy-start(bf16[640,160]{0,1:T(8,128)(2,1)} %param.18) | copy-start | bytes 614404
  24.0 10.8 %collective-permute-start.6 = (bf16[3,160,768]{2,1,0:T(8,128)(2,1)S(1)}, bf16[3,160,768]{2,1,0:T(8,128)(2,1)S(1)}, u32[]{:S(2)}, u32[]{:S(2)}) collective-permute-start(bf16[3,160,768]{2,1,0:T(8,128)(2,1)S(1)} %broadcast_select_fusion.refs_1_), channel_id=1, source_target_pairs={{0,4},{1,5},{2,6},{3,7},{8,12},{9,13},{10,14},{11,15},{16,20},{17,... | collective-permute-start | bytes 2211848 | tf_op jit(solution)/shard_map/ppermute | solution.py:341
  31.9 3.1 %collective-permute-start.7 = (bf16[3,160,768]{2,1,0:T(8,128)(2,1)S(1)}, bf16[3,160,768]{2,1,0:T(8,128)(2,1)S(1)}, u32[]{:S(2)}, u32[]{:S(2)}) collective-permute-start(bf16[3,160,768]{2,1,0:T(8,128)(2,1)S(1)} %collective-permute-done.1.refs_0_), channel_id=1, source_target_pairs={{0,4},{1,5},{2,6},{3,7},{8,12},{9,13},{10,14},{11,15},{16,20},{17,... | collective-permute-start | bytes 2211848 | tf_op jit(solution)/shard_map/ppermute | solution.py:341
  33.2 3.1 %collective-permute-start.5 = (bf16[3,160,768]{2,1,0:T(8,128)(2,1)S(1)}, bf16[3,160,768]{2,1,0:T(8,128)(2,1)S(1)}, u32[]{:S(2)}, u32[]{:S(2)}) collective-permute-start(bf16[3,160,768]{2,1,0:T(8,128)(2,1)S(1)} %collective-permute-done.2.refs_2_), channel_id=1, source_target_pairs={{0,4},{1,5},{2,6},{3,7},{8,12},{9,13},{10,14},{11,15},{16,20},{17,... | collective-permute-start | bytes 2211848 | tf_op jit(solution)/shard_map/ppermute | solution.py:341
  41.8 14.7 %collective-permute-start.10 = (bf16[3,160,768]{2,1,0:T(8,128)(2,1)S(1)}, bf16[3,160,768]{2,1,0:T(8,128)(2,1)S(1)}, u32[]{:S(2)}, u32[]{:S(2)}) collective-permute-start(bf16[3,160,768]{2,1,0:T(8,128)(2,1)S(1)} %get-tuple-element.39.refs_10_.refs_1_), channel_id=1, source_target_pairs={{0,1},{2,3},{8,9},{10,11},{1,0},{3,2},{9,8},{11,10},{5,6},{13,14},... | collective-permute-start | bytes 2211848 | tf_op jit(solution)/shard_map/ppermute | solution.py:341
  48.3 20.9 %collective-permute-start.9 = (bf16[3,160,768]{2,1,0:T(8,128)(2,1)S(1)}, bf16[3,160,768]{2,1,0:T(8,128)(2,1)S(1)}, u32[]{:S(2)}, u32[]{:S(2)}) collective-permute-start(bf16[3,160,768]{2,1,0:T(8,128)(2,1)S(1)} %tangent.2.refs_1_), channel_id=1, source_target_pairs={{9,10},{10,9},{4,5},{6,7},{12,13},{14,15},{5,4},{7,6},{13,12},{15,... | collective-permute-start | bytes 2211848 | tf_op jit(solution)/shard_map/ppermute | solution.py:341
  51.1 19.9 %collective-permute-start.8 = (bf16[3,160,768]{2,1,0:T(8,128)(2,1)S(1)}, bf16[3,160,768]{2,1,0:T(8,128)(2,1)S(1)}, u32[]{:S(2)}, u32[]{:S(2)}) collective-permute-start(bf16[3,160,768]{2,1,0:T(8,128)(2,1)S(1)} %tangent.2.refs_1_), channel_id=1, source_target_pairs={{8,9},{10,11},{9,8},{11,10},{5,6},{13,14},{6,5},{14,13},{24,25},{2... | collective-permute-start | bytes 2211848 | tf_op jit(solution)/shard_map/ppermute | solution.py:341
  56.6 1.8 %collective-permute-start.11 = (bf16[3,80,768]{2,1,0:T(8,128)(2,1)S(1)}, bf16[3,80,768]{2,1,0:T(8,128)(2,1)S(1)}, u32[]{:S(2)}, u32[]{:S(2)}) collective-permute-start(bf16[3,80,768]{2,1,0:T(8,128)(2,1)S(1)} %get-tuple-element.45), channel_id=1, source_target_pairs={{0,4},{1,5},{2,6},{3,7},{8,12},{9,13},{10,14},{11,15},{4,0},{5,1},... | collective-permute-start | bytes 1105928 | tf_op jit(solution)/shard_map/ppermute | solution.py:341
  56.6 2.2 %collective-permute-start.12 = (bf16[3,80,768]{2,1,0:T(8,128)(2,1)S(1)}, bf16[3,80,768]{2,1,0:T(8,128)(2,1)S(1)}, u32[]{:S(2)}, u32[]{:S(2)}) collective-permute-start(bf16[3,80,768]{2,1,0:T(8,128)(2,1)S(1)} %get-tuple-element.46), channel_id=1, source_target_pairs={{0,4},{1,5},{2,6},{3,7},{8,12},{9,13},{10,14},{11,15},{4,0},{5,1},... | collective-permute-start | bytes 1105928 | tf_op jit(solution)/shard_map/ppermute | solution.py:341

commit v9 on v7

--- a/solution.py
+++ b/solution.py
@@ -339,6 +339,9 @@
     def across(block, pairs):
         return send(block, [((a, z), (b, z)) for a, b in pairs for z in range(bands)])
 
+    def in_halves(block, pairs):
+        return jnp.concatenate([across(part, pairs) for part in jnp.split(block, 2, axis=1)], axis=1)
+
     evens = list(range(0, members, 2))
     odds = list(range(1, members, 2))
     partners = [(m - 1, m) for m in odds]
@@ -415,15 +418,14 @@
     control_near, control_far = exchange(control, evens)
     conv = conv_step(near, member, far)
     control_near, control_far, conv, filters = lax.optimization_barrier((control_near, control_far, conv, filters))
-    other = (across(control_far, partners), control_other, across(control_near, partners))
+    other = (in_halves(control_far, partners), control_other, in_halves(control_near, partners))
     control, unit, scale, slope = control_step(control_near, control, control_far, *other)
     for step in range(1, STEPS):
         halo = exchange(control, range(members))[0]
         inputs = (member, conv) if step == 1 else (near, member, far, taps)
         member = tangent_step(step == 1, inputs, unit, scale, slope, control)
         halo, _ = lax.optimization_barrier((halo, member))
-        halves = [across(part, swapped) for part in jnp.split(halo, 2, axis=1)]
-        other = jnp.concatenate(halves, axis=1)
+        other = in_halves(halo, swapped)
         near, far = exchange(member, range(1, members))
         control, unit, scale, slope = control_step(halo, control, other)
     return tangent_step(False, (near, member, far, taps), unit, scale, slope, control)[None]

time: 77.1 us -> 79.6 us (1.032)
  starting transfers between devices: 23.6 us -> 26.3 us
    ppermute x13 -> x15, starting transfers between devices: 23.6 us -> 26.3 us  [send(): lax.ppermute(block, ('mem', 'lat'), [(a * bands + i, b * bands + j) for (...]
    ppermute x13 -> x15, waiting for transfers between devices: 13.3 us -> 12.9 us  [send(): lax.ppermute(block, ('mem', 'lat'), [(a * bands + i, b * bands + j) for (...]
  transfers between devices with their start and end apart: 13 -> 15, of which waited for: 9 -> 8; matrix products, arithmetic and copies ran while one was open for 2% -> 2% of each run, Pallas kernels for 29% -> 28%
where the time goes in v9:
time: 79.6 us; the launch traced here: 78.9 us
  Pallas kernels  33.5 us (42%)
  starting transfers between devices  26.3 us (33%)
  waiting for transfers between devices  12.9 us (16%)
  local copies, waits for them, and re-layouts  4.66 us (6%)
  other arithmetic  1.35 us (2%)
    ppermute x15, starting transfers between devices, send(): lax.ppermute(block, ('mem', 'lat'), [(a * bands + i, b * bands + j) for (...  26.3 us
    pallas_call x2, Pallas kernels, control_step(): pl.pallas_call(control_kernel, out_shape=(field, shape(rows, channels, wi...  14.3 us
    ppermute x15, waiting for transfers between devices, send(): lax.ppermute(block, ('mem', 'lat'), [(a * bands + i, b * bands + j) for (...  12.9 us
    pallas_call x2, Pallas kernels, tangent_step(): pl.pallas_call(lambda *refs: tangent_kernel(ready, *refs), out_shape=fiel...  10.2 us
    unnamed x20, local copies, waits for them, and re-layouts  4.51 us
    pallas_call x1, Pallas kernels, per_device(): pl.pallas_call(lambda *refs: filter_kernel(bands, *refs), out_shape=shape...  3.49 us
    pallas_call x1, Pallas kernels, conv_step(): pl.pallas_call(conv_kernel, out_shape=shape(rows, channels, width), in_sp...  2.86 us
    pallas_call x1, Pallas kernels, per_device(): pl.pallas_call(prepare_kernel, out_shape=(shape(rows, TAPS, channels, (ro...  2.68 us
  transfers between devices with their start and end apart: 15, of which 8 were waited for; matrix products, arithmetic and copies ran while one was open for 2% of the time, Pallas kernels for 28%

profile of v9, /device:TPU:10, one launch (start us, length us, event | category | flops | bytes accessed | tf_op | source)
XLA Modules:
  0.0 78.9 jit_solution(16766327029884086472)
XLA Ops:
  0.0 0.0 copy-start.2
  0.0 1.4 %collective-permute-start = (bf16[3,160,768]{2,1,0:T(8,128)(2,1)}, bf16[3,160,768]{2,1,0:T(8,128)(2,1)S(1)}, u32[]{:S(2)}, u32[]{:S(2)}) collective-permute-start(bf16[3,160,768]{2,1,0:T(8,128)(2,1)} %bitcast.7), channel_id=1, source_target_pairs={{0,8},{1,9},{2,10},{3,11},{16,24},{17,25},{18,26},{19,27}} | collective-permute-start | bytes 2211848 | tf_op jit(solution)/shard_map/ppermute | solution.py:328
  1.4 3.5 %collective-permute-start.4 = (bf16[3,160,768]{2,1,0:T(8,128)(2,1)}, bf16[3,160,768]{2,1,0:T(8,128)(2,1)S(1)}, u32[]{:S(2)}, u32[]{:S(2)}) collective-permute-start(bf16[3,160,768]{2,1,0:T(8,128)(2,1)} %bitcast.8), channel_id=1, source_target_pairs={{9,10},{10,9},{4,5},{6,7},{12,13},{14,15},{5,4},{7,6},{13,12},{15,... | collective-permute-start | bytes 2211848 | tf_op jit(solution)/shard_map/ppermute | solution.py:328
  4.9 1.9 %collective-permute-start.3 = (bf16[3,160,768]{2,1,0:T(8,128)(2,1)}, bf16[3,160,768]{2,1,0:T(8,128)(2,1)S(1)}, u32[]{:S(2)}, u32[]{:S(2)}) collective-permute-start(bf16[3,160,768]{2,1,0:T(8,128)(2,1)} %bitcast.9), channel_id=1, source_target_pairs={{8,9},{10,11},{9,8},{11,10},{5,6},{13,14},{6,5},{14,13},{24,25},{2... | collective-permute-start | bytes 2211848 | tf_op jit(solution)/shard_map/ppermute | solution.py:328
  6.9 0.0 copy-start.3
  6.9 0.9 %copy-done.3 = bf16[160,640]{1,0:T(8,128)(2,1)S(1)} copy-done((bf16[160,640]{1,0:T(8,128)(2,1)S(1)}, bf16[160,640]{1,0:T(8,128)(2,1)}, u32[]{:S(2)}) %copy-start.3) | copy-done | bytes 204824
  7.8 0.0 copy-start.4
  7.8 0.8 %copy-done.4 = f32[7,7,160]{2,1,0:T(8,128)S(1)} copy-done((f32[7,7,160]{2,1,0:T(8,128)S(1)}, f32[7,7,160]{2,1,0:T(8,128)}, u32[]{:S(2)}) %copy-start.4) | copy-done | bytes 31384
  8.6 0.0 copy-start.5
  8.6 0.7 copy-done.5
  9.3 0.0 copy-start.6
  9.3 0.7 copy-done.6
  10.0 0.0 copy-start.7
  10.0 0.7 copy-done.7
  10.7 0.0 copy-start.8
  10.7 0.7 copy-done.8
  11.4 0.0 copy-start.9
  11.4 2.7 %prepare.1 = (bf16[3,7,160,144]{3,2,1,0:T(8,128)(2,1)S(1)}, f32[160,128]{1,0:T(8,128)S(1)}, f32[160,128]{1,0:T(8,128)S(1)}, bf16[640,176]{1,0:T(8,128)(2,1)S(1)}, f32[3,768]{1,0:T(4,128)S(1)}) custom-call(f32[7,7,160]{2,1,0:T(8,128)S(1)} %copy-done.4, f32[1,160]{1,0:T(1,128)S(1)} %bitcast.17, f32[1,160]{1,0:T(1,128)S(1)} %bitcast.18, ...), custom_call_target="tpu_custom_call" | custom-call | tf_op jit(solution)/shard_map/prepare/pallas_call | solution.py:353
  14.1 0.0 collective-permute-done
  14.1 1.2 %broadcast_select_fusion.refs_1_ = bf16[3,160,768]{2,1,0:T(8,128)(2,1)S(1)} fusion(bf16[3,160,768]{2,1,0:T(8,128)(2,1)S(1)} %collective-permute-done, pred[]{:T(512)S(6)} %and.4, bf16[1,3,160,768]{3,2,1,0:T(8,128)(2,1)} %param.10), kind=kLoop, calls=%fused_computation.3 | loop fusion | flops 368640 | bytes 2211841 | tf_op jit(solution)/shard_map/jit(_where)/select_n | solution.py:414
  15.3 0.0 copy-start
  15.3 3.2 %collective-permute-start.2 = (bf16[3,160,768]{2,1,0:T(8,128)(2,1)S(1)}, bf16[3,160,768]{2,1,0:T(8,128)(2,1)S(1)}, u32[]{:S(2)}, u32[]{:S(2)}) collective-permute-start(bf16[3,160,768]{2,1,0:T(8,128)(2,1)S(1)} %broadcast_select_fusion.refs_1_), channel_id=1, source_target_pairs={{1,2},{9,10},{2,1},{10,9},{17,18},{25,26},{18,17},{26,25}} | collective-permute-start | bytes 2211848 | tf_op jit(solution)/shard_map/ppermute | solution.py:328
  18.5 1.9 %collective-permute-start.1 = (bf16[3,160,768]{2,1,0:T(8,128)(2,1)S(1)}, bf16[3,160,768]{2,1,0:T(8,128)(2,1)S(1)}, u32[]{:S(2)}, u32[]{:S(2)}) collective-permute-start(bf16[3,160,768]{2,1,0:T(8,128)(2,1)S(1)} %broadcast_select_fusion.refs_1_), channel_id=1, source_target_pairs={{0,1},{2,3},{8,9},{10,11},{1,0},{3,2},{9,8},{11,10},{16,17},{18,19... | collective-permute-start | bytes 2211848 | tf_op jit(solution)/shard_map/ppermute | solution.py:328
  20.5 0.0 copy-done.2
  20.5 0.0 copy-done.9
  20.5 3.5 %filters.1.refs_12_.refs_6_.refs_9_.refs_8_ = bf16[3,768,768]{2,1,0:T(8,128)(2,1)S(1)} custom-call(s32[12]{0:T(128)S(1)} %copy-done.9, bf16[768,768]{1,0:T(8,128)(2,1)S(1)} %copy-done.2), custom_call_target="tpu_custom_call" | custom-call | tf_op jit(solution)/shard_map/filters/pallas_call | solution.py:368
  24.0 1.3 %collective-permute-start.7 = (bf16[3,160,768]{2,1,0:T(8,128)(2,1)S(1)}, bf16[3,160,768]{2,1,0:T(8,128)(2,1)S(1)}, u32[]{:S(2)}, u32[]{:S(2)}) collective-permute-start(bf16[3,160,768]{2,1,0:T(8,128)(2,1)S(1)} %broadcast_select_fusion.refs_1_), channel_id=1, source_target_pairs={{0,4},{1,5},{2,6},{3,7},{8,12},{9,13},{10,14},{11,15},{16,20},{17,... | collective-permute-start | bytes 2211848 | tf_op jit(solution)/shard_map/ppermute | solution.py:328
  25.3 0.0 collective-permute-done.4.second
  25.3 0.0 collective-permute-done.3.first
  25.3 0.0 copy-done
  25.3 2.9 %conv.1.refs_1_ = f32[3,160,768]{2,1,0:T(8,128)S(1)} custom-call(bf16[3,160,768]{2,1,0:T(8,128)(2,1)S(1)} %collective-permute-done.3.first, bf16[3,160,768]{2,1,0:T(8,128)(2,1)S(1)} %bitcast.10, bf16[3,160,768]{2,1,0:T(8,128)(2,1)S(1)} %collective-permute-done.4.second, bf16[3,7,160,144]{3,2,1,0:T(8,128)(2,1)S(1)} %get-tuple-element.27.taps.refs_6_.refs_3_), custom_call_target="tpu_custom_call" | custom-call | tf_op jit(solution)/shard_map/conv/pallas_call | solution.py:389
  28.2 2.6 %collective-permute-done.2.refs_2_ = bf16[3,160,768]{2,1,0:T(8,128)(2,1)S(1)} collective-permute-done((bf16[3,160,768]{2,1,0:T(8,128)(2,1)S(1)}, bf16[3,160,768]{2,1,0:T(8,128)(2,1)S(1)}, u32[]{:S(2)}, u32[]{:S(2)}) %collective-permute-start.2) | collective-permute-done | bytes 737312 | tf_op jit(solution)/shard_map/ppermute | solution.py:328
  30.8 1.1 %collective-permute-done.1.refs_0_ = bf16[3,160,768]{2,1,0:T(8,128)(2,1)S(1)} collective-permute-done((bf16[3,160,768]{2,1,0:T(8,128)(2,1)S(1)}, bf16[3,160,768]{2,1,0:T(8,128)(2,1)S(1)}, u32[]{:S(2)}, u32[]{:S(2)}) %collective-permute-start.1) | collective-permute-done | bytes 737312 | tf_op jit(solution)/shard_map/ppermute | solution.py:328
  31.9 1.3 %collective-permute-start.8 = (bf16[3,80,768]{2,1,0:T(8,128)(2,1)S(1)}, bf16[3,80,768]{2,1,0:T(8,128)(2,1)S(1)}, u32[]{:S(2)}, u32[]{:S(2)}) collective-permute-start(bf16[3,80,768]{2,1,0:T(8,128)(2,1)S(1)} %get-tuple-element.47), channel_id=1, source_target_pairs={{0,4},{1,5},{2,6},{3,7},{8,12},{9,13},{10,14},{11,15},{16,20},{17,... | collective-permute-start | bytes 1105928 | tf_op jit(solution)/shard_map/ppermute | solution.py:328
  33.3 1.3 %collective-permute-start.9 = (bf16[3,80,768]{2,1,0:T(8,128)(2,1)S(1)}, bf16[3,80,768]{2,1,0:T(8,128)(2,1)S(1)}, u32[]{:S(2)}, u32[]{:S(2)}) collective-permute-start(bf16[3,80,768]{2,1,0:T(8,128)(2,1)S(1)} %get-tuple-element.48), channel_id=1, source_target_pairs={{0,4},{1,5},{2,6},{3,7},{8,12},{9,13},{10,14},{11,15},{16,20},{17,... | collective-permute-start | bytes 1105928 | tf_op jit(solution)/shard_map/ppermute | solution.py:328
  34.6 0.1 fusion.2
  34.6 1.3 %collective-permute-start.5 = (bf16[3,80,768]{2,1,0:T(8,128)(2,1)S(1)}, bf16[3,80,768]{2,1,0:T(8,128)(2,1)S(1)}, u32[]{:S(2)}, u32[]{:S(2)}) collective-permute-start(bf16[3,80,768]{2,1,0:T(8,128)(2,1)S(1)} %get-tuple-element.49), channel_id=1, source_target_pairs={{0,4},{1,5},{2,6},{3,7},{8,12},{9,13},{10,14},{11,15},{16,20},{17,... | collective-permute-start | bytes 1105928 | tf_op jit(solution)/shard_map/ppermute | solution.py:328
  36.0 0.0 copy-start.1
  36.0 1.6 %collective-permute-start.6 = (bf16[3,80,768]{2,1,0:T(8,128)(2,1)S(1)}, bf16[3,80,768]{2,1,0:T(8,128)(2,1)S(1)}, u32[]{:S(2)}, u32[]{:S(2)}) collective-permute-start(bf16[3,80,768]{2,1,0:T(8,128)(2,1)S(1)} %get-tuple-element.50), channel_id=1, source_target_pairs={{0,4},{1,5},{2,6},{3,7},{8,12},{9,13},{10,14},{11,15},{16,20},{17,... | collective-permute-start | bytes 1105928 | tf_op jit(solution)/shard_map/ppermute | solution.py:328
  37.6 0.0 collective-permute-done.8
  37.6 0.0 collective-permute-done.9
  37.6 0.1 pad_maximum_fusion.1.refs_5_
  37.7 0.0 collective-permute-done.5
  37.7 1.0 %collective-permute-done.6 = bf16[3,80,768]{2,1,0:T(8,128)(2,1)S(1)} collective-permute-done((bf16[3,80,768]{2,1,0:T(8,128)(2,1)S(1)}, bf16[3,80,768]{2,1,0:T(8,128)(2,1)S(1)}, u32[]{:S(2)}, u32[]{:S(2)}) %collective-permute-start.6) | collective-permute-done | bytes 368672 | tf_op jit(solution)/shard_map/ppermute | solution.py:328
  38.7 0.0 collective-permute-done.7.refs_4_
  38.8 0.0 copy-done.1
  38.8 5.4 %control.2 = (bf16[3,160,768]{2,1,0:T(8,128)(2,1)S(1)}, f32[3,160,768]{2,1,0:T(8,128)S(1)}, f32[3,1,768]{2,1,0:T(1,128)S(1)}, f32[3,640,768]{2,1,0:T(8,128)S(1)}) custom-call(bf16[3,160,768]{2,1,0:T(8,128)(2,1)S(1)} %collective-permute-done.1.refs_0_, bf16[3,160,768]{2,1,0:T(8,128)(2,1)S(1)} %broadcast_select_fusion.refs_1_, ...), custom_call_target="tpu_custom_call" | custom-call | tf_op jit(solution)/shard_map/control/pallas_call | solution.py:378
  44.2 1.9 %collective-permute-start.12 = (bf16[3,160,768]{2,1,0:T(8,128)(2,1)S(1)}, bf16[3,160,768]{2,1,0:T(8,128)(2,1)S(1)}, u32[]{:S(2)}, u32[]{:S(2)}) collective-permute-start(bf16[3,160,768]{2,1,0:T(8,128)(2,1)S(1)} %get-tuple-element.39.refs_10_.refs_1_), channel_id=1, source_target_pairs={{0,1},{2,3},{8,9},{10,11},{1,0},{3,2},{9,8},{11,10},{5,6},{13,14},... | collective-permute-start | bytes 2211848 | tf_op jit(solution)/shard_map/ppermute | solution.py:328
  46.1 4.6 %tangent.2.refs_1_ = bf16[3,160,768]{2,1,0:T(8,128)(2,1)S(1)} custom-call(bf16[3,160,768]{2,1,0:T(8,128)(2,1)S(1)} %bitcast.11, f32[3,160,768]{2,1,0:T(8,128)S(1)} %conv.1.refs_1_, f32[160,128]{1,0:T(8,128)S(1)} %get-tuple-element.29.refs_7_.refs_2_.refs_4_, bf16[640,176]{1,0:T(8,128)(2,1)S(1)} %get-tuple-element.30.refs_9_.refs_3_.refs_6_.refs_5_, ...), custom_call_target="tpu_custom_call" | custom-call | tf_op jit(solution)/shard_map/tangent/pallas_call | solution.py:399
  50.7 2.7 %collective-permute-start.11 = (bf16[3,160,768]{2,1,0:T(8,128)(2,1)S(1)}, bf16[3,160,768]{2,1,0:T(8,128)(2,1)S(1)}, u32[]{:S(2)}, u32[]{:S(2)}) collective-permute-start(bf16[3,160,768]{2,1,0:T(8,128)(2,1)S(1)} %tangent.2.refs_1_), channel_id=1, source_target_pairs={{9,10},{10,9},{4,5},{6,7},{12,13},{14,15},{5,4},{7,6},{13,12},{15,... | collective-permute-start | bytes 2211848 | tf_op jit(solution)/shard_map/ppermute | solution.py:328
  53.5 2.1 %collective-permute-start.10 = (bf16[3,160,768]{2,1,0:T(8,128)(2,1)S(1)}, bf16[3,160,768]{2,1,0:T(8,128)(2,1)S(1)}, u32[]{:S(2)}, u32[]{:S(2)}) collective-permute-start(bf16[3,160,768]{2,1,0:T(8,128)(2,1)S(1)} %tangent.2.refs_1_), channel_id=1, source_target_pairs={{8,9},{10,11},{9,8},{11,10},{5,6},{13,14},{6,5},{14,13},{24,25},{2... | collective-permute-start | bytes 2211848 | tf_op jit(solution)/shard_map/ppermute | solution.py:328
  55.6 3.3 %collective-permute-done.12.refs_0_ = bf16[3,160,768]{2,1,0:T(8,128)(2,1)S(1)} collective-permute-done((bf16[3,160,768]{2,1,0:T(8,128)(2,1)S(1)}, bf16[3,160,768]{2,1,0:T(8,128)(2,1)S(1)}, u32[]{:S(2)}, u32[]{:S(2)}) %collective-permute-start.12) | collective-permute-done | bytes 737312 | tf_op jit(solution)/shard_map/ppermute | solution.py:328
  59.0 0.1 collective-permute-start.13
  59.0 0.5 collective-permute-start.14
  59.5 1.2 %collective-permute-done.13 = bf16[3,80,768]{2,1,0:T(8,128)(2,1)S(1)} collective-permute-done((bf16[3,80,768]{2,1,0:T(8,128)(2,1)S(1)}, bf16[3,80,768]{2,1,0:T(8,128)(2,1)S(1)}, u32[]{:S(2)}, u32[]{:S(2)}) %collective-permute-start.13) | collective-permute-done | bytes 368672 | tf_op jit(solution)/shard_map/ppermute | solution.py:328
  60.7 0.5 collective-permute-done.14
  61.3 8.9 %control.3 = (bf16[3,160,768]{2,1,0:T(8,128)(2,1)S(1)}, f32[3,160,768]{2,1,0:T(8,128)S(1)}, f32[3,1,768]{2,1,0:T(1,128)S(1)}, f32[3,640,768]{2,1,0:T(8,128)S(1)}) custom-call(bf16[3,160,768]{2,1,0:T(8,128)(2,1)S(1)} %collective-permute-done.12.refs_0_, bf16[3,160,768]{2,1,0:T(8,128)(2,1)S(1)} %get-tuple-element.39.refs_10_.refs_1_, ...), custom_call_target="tpu_custom_call" | custom-call | tf_op jit(solution)/shard_map/control/pallas_call | solution.py:378
  70.2 1.4 %collective-permute-done.11.refs_2_ = bf16[3,160,768]{2,1,0:T(8,128)(2,1)S(1)} collective-permute-done((bf16[3,160,768]{2,1,0:T(8,128)(2,1)S(1)}, bf16[3,160,768]{2,1,0:T(8,128)(2,1)S(1)}, u32[]{:S(2)}, u32[]{:S(2)}) %collective-permute-start.11) | collective-permute-done | bytes 737312 | tf_op jit(solution)/shard_map/ppermute | solution.py:328
  71.6 1.8 %collective-permute-done.10.refs_0_ = bf16[3,160,768]{2,1,0:T(8,128)(2,1)S(1)} collective-permute-done((bf16[3,160,768]{2,1,0:T(8,128)(2,1)S(1)}, bf16[3,160,768]{2,1,0:T(8,128)(2,1)S(1)}, u32[]{:S(2)}, u32[]{:S(2)}) %collective-permute-start.10) | collective-permute-done | bytes 737312 | tf_op jit(solution)/shard_map/ppermute | solution.py:328
  73.4 5.6 %tangent.3 = bf16[3,160,768]{2,1,0:T(8,128)(2,1)} custom-call(bf16[3,160,768]{2,1,0:T(8,128)(2,1)S(1)} %collective-permute-done.10.refs_0_, bf16[3,160,768]{2,1,0:T(8,128)(2,1)S(1)} %tangent.2.refs_1_, bf16[3,160,768]{2,1,0:T(8,128)(2,1)S(1)} %collective-permute-done.11.refs_2_, bf16[3,7,160,144]{3,2,1,0:T(8,128)(2,1)S(1)} %get-tuple-element.27.taps.refs_6_.refs_3_, ...), custom_call_target="tpu_custom_call" | custom-call | tf_op jit(solution)/shard_map/tangent/pallas_call | solution.py:399
  (4 shorter events, 0.2 us)
Async XLA Ops:
  0.0 20.5 %copy-start.2 = (bf16[768,768]{1,0:T(8,128)(2,1)S(1)}, bf16[768,768]{1,0:T(8,128)(2,1)}, u32[]{:S(2)}) copy-start(bf16[768,768]{1,0:T(8,128)(2,1)} %constant.11.clone.refs_1_) | copy-start | bytes 3538948
  0.0 14.1 %collective-permute-start = (bf16[3,160,768]{2,1,0:T(8,128)(2,1)}, bf16[3,160,768]{2,1,0:T(8,128)(2,1)S(1)}, u32[]{:S(2)}, u32[]{:S(2)}) collective-permute-start(bf16[3,160,768]{2,1,0:T(8,128)(2,1)} %bitcast.7), channel_id=1, source_target_pairs={{0,8},{1,9},{2,10},{3,11},{16,24},{17,25},{18,26},{19,27}} | collective-permute-start | bytes 2211848 | tf_op jit(solution)/shard_map/ppermute | solution.py:328
  1.4 23.9 %collective-permute-start.4 = (bf16[3,160,768]{2,1,0:T(8,128)(2,1)}, bf16[3,160,768]{2,1,0:T(8,128)(2,1)S(1)}, u32[]{:S(2)}, u32[]{:S(2)}) collective-permute-start(bf16[3,160,768]{2,1,0:T(8,128)(2,1)} %bitcast.8), channel_id=1, source_target_pairs={{9,10},{10,9},{4,5},{6,7},{12,13},{14,15},{5,4},{7,6},{13,12},{15,... | collective-permute-start | bytes 2211848 | tf_op jit(solution)/shard_map/ppermute | solution.py:328
  4.9 20.4 %collective-permute-start.3 = (bf16[3,160,768]{2,1,0:T(8,128)(2,1)}, bf16[3,160,768]{2,1,0:T(8,128)(2,1)S(1)}, u32[]{:S(2)}, u32[]{:S(2)}) collective-permute-start(bf16[3,160,768]{2,1,0:T(8,128)(2,1)} %bitcast.9), channel_id=1, source_target_pairs={{8,9},{10,11},{9,8},{11,10},{5,6},{13,14},{6,5},{14,13},{24,25},{2... | collective-permute-start | bytes 2211848 | tf_op jit(solution)/shard_map/ppermute | solution.py:328
  6.9 0.9 %copy-start.3 = (bf16[160,640]{1,0:T(8,128)(2,1)S(1)}, bf16[160,640]{1,0:T(8,128)(2,1)}, u32[]{:S(2)}) copy-start(bf16[160,640]{1,0:T(8,128)(2,1)} %refs_3_.1) | copy-start | bytes 614404
  7.8 0.8 %copy-start.4 = (f32[7,7,160]{2,1,0:T(8,128)S(1)}, f32[7,7,160]{2,1,0:T(8,128)}, u32[]{:S(2)}) copy-start(f32[7,7,160]{2,1,0:T(8,128)} %refs_0_.2) | copy-start | bytes 94084
  8.6 0.7 copy-start.5
  9.3 0.7 copy-start.6
  10.0 0.7 copy-start.7
  10.7 0.7 copy-start.8
  11.4 9.1 %copy-start.9 = (s32[12]{0:T(128)S(1)}, s32[12]{0:T(128)}, u32[]{:S(2)}) copy-start(s32[12]{0:T(128)} %refs_0_.3) | copy-start | bytes 148
  15.3 10.1 %copy-start = (bf16[1,3,160,768]{3,2,1,0:T(8,128)(2,1)S(1)}, bf16[1,3,160,768]{3,2,1,0:T(8,128)(2,1)}, u32[]{:S(2)}) copy-start(bf16[1,3,160,768]{3,2,1,0:T(8,128)(2,1)} %param.10) | copy-start | bytes 2211844
  15.3 15.5 %collective-permute-start.2 = (bf16[3,160,768]{2,1,0:T(8,128)(2,1)S(1)}, bf16[3,160,768]{2,1,0:T(8,128)(2,1)S(1)}, u32[]{:S(2)}, u32[]{:S(2)}) collective-permute-start(bf16[3,160,768]{2,1,0:T(8,128)(2,1)S(1)} %broadcast_select_fusion.refs_1_), channel_id=1, source_target_pairs={{1,2},{9,10},{2,1},{10,9},{17,18},{25,26},{18,17},{26,25}} | collective-permute-start | bytes 2211848 | tf_op jit(solution)/shard_map/ppermute | solution.py:328
  18.5 13.4 %collective-permute-start.1 = (bf16[3,160,768]{2,1,0:T(8,128)(2,1)S(1)}, bf16[3,160,768]{2,1,0:T(8,128)(2,1)S(1)}, u32[]{:S(2)}, u32[]{:S(2)}) collective-permute-start(bf16[3,160,768]{2,1,0:T(8,128)(2,1)S(1)} %broadcast_select_fusion.refs_1_), channel_id=1, source_target_pairs={{0,1},{2,3},{8,9},{10,11},{1,0},{3,2},{9,8},{11,10},{16,17},{18,19... | collective-permute-start | bytes 2211848 | tf_op jit(solution)/shard_map/ppermute | solution.py:328
  24.0 14.8 %collective-permute-start.7 = (bf16[3,160,768]{2,1,0:T(8,128)(2,1)S(1)}, bf16[3,160,768]{2,1,0:T(8,128)(2,1)S(1)}, u32[]{:S(2)}, u32[]{:S(2)}) collective-permute-start(bf16[3,160,768]{2,1,0:T(8,128)(2,1)S(1)} %broadcast_select_fusion.refs_1_), channel_id=1, source_target_pairs={{0,4},{1,5},{2,6},{3,7},{8,12},{9,13},{10,14},{11,15},{16,20},{17,... | collective-permute-start | bytes 2211848 | tf_op jit(solution)/shard_map/ppermute | solution.py:328
  31.9 5.7 %collective-permute-start.8 = (bf16[3,80,768]{2,1,0:T(8,128)(2,1)S(1)}, bf16[3,80,768]{2,1,0:T(8,128)(2,1)S(1)}, u32[]{:S(2)}, u32[]{:S(2)}) collective-permute-start(bf16[3,80,768]{2,1,0:T(8,128)(2,1)S(1)} %get-tuple-element.47), channel_id=1, source_target_pairs={{0,4},{1,5},{2,6},{3,7},{8,12},{9,13},{10,14},{11,15},{16,20},{17,... | collective-permute-start | bytes 1105928 | tf_op jit(solution)/shard_map/ppermute | solution.py:328
  33.3 4.4 %collective-permute-start.9 = (bf16[3,80,768]{2,1,0:T(8,128)(2,1)S(1)}, bf16[3,80,768]{2,1,0:T(8,128)(2,1)S(1)}, u32[]{:S(2)}, u32[]{:S(2)}) collective-permute-start(bf16[3,80,768]{2,1,0:T(8,128)(2,1)S(1)} %get-tuple-element.48), channel_id=1, source_target_pairs={{0,4},{1,5},{2,6},{3,7},{8,12},{9,13},{10,14},{11,15},{16,20},{17,... | collective-permute-start | bytes 1105928 | tf_op jit(solution)/shard_map/ppermute | solution.py:328
  34.6 3.0 %collective-permute-start.5 = (bf16[3,80,768]{2,1,0:T(8,128)(2,1)S(1)}, bf16[3,80,768]{2,1,0:T(8,128)(2,1)S(1)}, u32[]{:S(2)}, u32[]{:S(2)}) collective-permute-start(bf16[3,80,768]{2,1,0:T(8,128)(2,1)S(1)} %get-tuple-element.49), channel_id=1, source_target_pairs={{0,4},{1,5},{2,6},{3,7},{8,12},{9,13},{10,14},{11,15},{16,20},{17,... | collective-permute-start | bytes 1105928 | tf_op jit(solution)/shard_map/ppermute | solution.py:328
  36.0 2.8 %copy-start.1 = (bf16[640,160]{0,1:T(8,128)(2,1)S(1)}, bf16[640,160]{0,1:T(8,128)(2,1)}, u32[]{:S(2)}) copy-start(bf16[640,160]{0,1:T(8,128)(2,1)} %param.18) | copy-start | bytes 614404
  36.0 2.7 %collective-permute-start.6 = (bf16[3,80,768]{2,1,0:T(8,128)(2,1)S(1)}, bf16[3,80,768]{2,1,0:T(8,128)(2,1)S(1)}, u32[]{:S(2)}, u32[]{:S(2)}) collective-permute-start(bf16[3,80,768]{2,1,0:T(8,128)(2,1)S(1)} %get-tuple-element.50), channel_id=1, source_target_pairs={{0,4},{1,5},{2,6},{3,7},{8,12},{9,13},{10,14},{11,15},{16,20},{17,... | collective-permute-start | bytes 1105928 | tf_op jit(solution)/shard_map/ppermute | solution.py:328
  44.2 14.7 %collective-permute-start.12 = (bf16[3,160,768]{2,1,0:T(8,128)(2,1)S(1)}, bf16[3,160,768]{2,1,0:T(8,128)(2,1)S(1)}, u32[]{:S(2)}, u32[]{:S(2)}) collective-permute-start(bf16[3,160,768]{2,1,0:T(8,128)(2,1)S(1)} %get-tuple-element.39.refs_10_.refs_1_), channel_id=1, source_target_pairs={{0,1},{2,3},{8,9},{10,11},{1,0},{3,2},{9,8},{11,10},{5,6},{13,14},... | collective-permute-start | bytes 2211848 | tf_op jit(solution)/shard_map/ppermute | solution.py:328
  50.7 20.9 %collective-permute-start.11 = (bf16[3,160,768]{2,1,0:T(8,128)(2,1)S(1)}, bf16[3,160,768]{2,1,0:T(8,128)(2,1)S(1)}, u32[]{:S(2)}, u32[]{:S(2)}) collective-permute-start(bf16[3,160,768]{2,1,0:T(8,128)(2,1)S(1)} %tangent.2.refs_1_), channel_id=1, source_target_pairs={{9,10},{10,9},{4,5},{6,7},{12,13},{14,15},{5,4},{7,6},{13,12},{15,... | collective-permute-start | bytes 2211848 | tf_op jit(solution)/shard_map/ppermute | solution.py:328
  53.5 19.9 %collective-permute-start.10 = (bf16[3,160,768]{2,1,0:T(8,128)(2,1)S(1)}, bf16[3,160,768]{2,1,0:T(8,128)(2,1)S(1)}, u32[]{:S(2)}, u32[]{:S(2)}) collective-permute-start(bf16[3,160,768]{2,1,0:T(8,128)(2,1)S(1)} %tangent.2.refs_1_), channel_id=1, source_target_pairs={{8,9},{10,11},{9,8},{11,10},{5,6},{13,14},{6,5},{14,13},{24,25},{2... | collective-permute-start | bytes 2211848 | tf_op jit(solution)/shard_map/ppermute | solution.py:328
  59.0 1.8 %collective-permute-start.13 = (bf16[3,80,768]{2,1,0:T(8,128)(2,1)S(1)}, bf16[3,80,768]{2,1,0:T(8,128)(2,1)S(1)}, u32[]{:S(2)}, u32[]{:S(2)}) collective-permute-start(bf16[3,80,768]{2,1,0:T(8,128)(2,1)S(1)} %get-tuple-element.45), channel_id=1, source_target_pairs={{0,4},{1,5},{2,6},{3,7},{8,12},{9,13},{10,14},{11,15},{4,0},{5,1},... | collective-permute-start | bytes 1105928 | tf_op jit(solution)/shard_map/ppermute | solution.py:328
  59.0 2.2 %collective-permute-start.14 = (bf16[3,80,768]{2,1,0:T(8,128)(2,1)S(1)}, bf16[3,80,768]{2,1,0:T(8,128)(2,1)S(1)}, u32[]{:S(2)}, u32[]{:S(2)}) collective-permute-start(bf16[3,80,768]{2,1,0:T(8,128)(2,1)S(1)} %get-tuple-element.46), channel_id=1, source_target_pairs={{0,4},{1,5},{2,6},{3,7},{8,12},{9,13},{10,14},{11,15},{4,0},{5,1},... | collective-permute-start | bytes 1105928 | tf_op jit(solution)/shard_map/ppermute | solution.py:328
